TPU v7x, 32 devices: a whole 2x2x4 slice. The times are simulated.
32 devices in a mesh: lat: 4 (over y, x), lon: 8 (over z, core).
Axes of the slice: x: 2, y: 2, z: 4, core: 2. Of those that a mesh axis runs over, the one named last changes fastest.
Arguments:
- field: bfloat16 [128, 256, 512], P('lat', 'lon'), may hold values from -6 to 6
- qkv_fine: bfloat16 [512, 1536], replicated, may hold values from -0.35355339 to 0.35355339
- proj_fine: bfloat16 [512, 512], replicated, may hold values from -0.25 to 0.25
- up_fine: bfloat16 [512, 2048], replicated, may hold values from -0.25 to 0.25
- down_fine: bfloat16 [2048, 512], replicated, may hold values from -0.125 to 0.125
- merge_weight: bfloat16 [2048, 1024], replicated, may hold values from -0.15467961 to 0.15467961
- qkv_coarse: bfloat16 [1024, 3072], P(None, 'lon'), may hold values from -0.25 to 0.25
- proj_coarse: bfloat16 [1024, 1024], P(None, 'lon'), may hold values from -0.1875 to 0.1875
Outputs:
- fine_out: bfloat16 [128, 256, 512], P('lat', 'lon')
- coarse_out: bfloat16 [64, 128, 1024], P('lat', 'lon')
All inputs are finite; a program needn't handle non-finite values.
Results may differ from a plain program's by a relative error of at most 0.018.
Values may be sent and summed in bfloat16 or wider, within the bound.
No kernel may reach another device: no remote copies, remote signals or barrier semaphores. Data moves between devices by JAX's collectives and lax.ppermute only.
A program may use at most 128 MiB of HBM per device.

v0:
```python
import functools

import jax
import jax.numpy as jnp
import numpy as np
from jax import lax
from jax.experimental import pallas as pl
from jax.experimental.pallas import tpu as pltpu
from jax.sharding import PartitionSpec as P

HEAD = 64
WIN = 16
HALF = WIN // 2
QUART = HALF // 2
TOK = WIN * WIN
SLAB = 2 * HEAD
NEG = -1e30
BF = jnp.bfloat16
F32 = jnp.float32


def dot(a, b):
    return jnp.dot(a, b, preferred_element_type=F32)


def norm(values):
    center = values - jnp.mean(values, axis=-1, keepdims=True)
    spread = jnp.mean(center * center, axis=-1, keepdims=True)
    return (center * lax.rsqrt(spread + 1e-05)).astype(BF)


def slab_attention(qkv, mixed, at, width, bias):
    q = qkv[:, pl.ds(at, SLAB)] * BF(HEAD ** (-0.5))
    k = qkv[:, pl.ds(at + width, SLAB)]
    v = qkv[:, pl.ds(at + 2 * width, SLAB)]
    low = lax.broadcasted_iota(jnp.int32, (TOK, SLAB), 1) < HEAD
    zero = jnp.zeros_like(q)
    one = jnp.ones_like(v)
    outs = []
    for qh, vh in (
        (jnp.where(low, q, zero), jnp.where(low, v, one)),
        (jnp.where(low, zero, q), jnp.where(low, one, v)),
    ):
        scores = lax.dot_general(qh, k, (((1,), (1,)), ((), ())), preferred_element_type=F32)
        if bias is not None:
            scores = scores + bias
        top = jnp.max(scores, axis=-1, keepdims=True)
        outs.append(dot(jnp.exp(scores - top).astype(BF), vh))
    sums = pltpu.roll(jnp.where(low, outs[1], outs[0]), HEAD, 1)
    mixed[:, pl.ds(at, SLAB)] = (jnp.where(low, outs[0], outs[1]) / sums).astype(BF)


def attention(qkv, mixed, width, bias):
    for at in range(0, width, SLAB):
        slab_attention(qkv, mixed, at, width, bias)


def mask_bias(last_ref):
    lead = lax.broadcasted_iota(jnp.int32, (TOK, TOK), 0) < TOK // 2
    other = lax.broadcasted_iota(jnp.int32, (TOK, TOK), 1) < TOK // 2
    return jnp.where(lead == other, 0.0, jnp.where(last_ref[0] > 0, NEG, 0.0))


def fine_kernel(masked, last, x_ref, vq, vp, vu, vd, vm, out_ref, merged_ref, qkv, mixed, wide):
    width = x_ref.shape[1]
    x = x_ref[...].astype(F32)
    normed = norm(x)
    for part in range(3):
        cols = slice(part * width, (part + 1) * width)
        qkv[:, cols] = dot(normed, vq[:, cols]).astype(BF)
    attention(qkv, mixed, width, mask_bias(last) if masked else None)
    attended = (x + dot(mixed[...], vp[...])).astype(BF).astype(F32)
    normed = norm(attended)
    total = attended
    step = width
    for at in range(0, vu.shape[1], step):
        hidden = jax.nn.gelu(dot(normed, vu[:, at:at + step])).astype(BF)
        total = total + dot(hidden, vd[at:at + step, :])
    fine = total.astype(BF)
    out_ref[...] = fine
    for c in range(width // 128):
        wide[c] = fine[:, c * 128:(c + 1) * 128].astype(F32)
    groups = []
    for b in range(2):
        picked = jnp.concatenate(
            [wide[c, pl.ds(b, TOK // 2, stride=2), :] for c in range(width // 128)], axis=1
        ).reshape(HALF, 2, HALF, width)
        groups.append((picked[:, 0].reshape(TOK // 4, width), picked[:, 1].reshape(TOK // 4, width)))
    joined = [groups[0][0], groups[0][1], groups[1][0], groups[1][1]]
    count = 4 * width
    mean = sum(jnp.sum(g, axis=-1, keepdims=True) for g in joined) / count
    joined = [g - mean for g in joined]
    spread = sum(jnp.sum(g * g, axis=-1, keepdims=True) for g in joined) / count
    scale = lax.rsqrt(spread + 1e-05)
    merged = 0.0
    for i, g in enumerate(joined):
        merged = merged + dot((g * scale).astype(BF), vm[i * width:(i + 1) * width, :])
    merged_ref[...] = merged.astype(BF)


def fine_window(x, last, weights, masked):
    width = x.shape[-1]
    wide = weights[-1].shape[1]
    flops = 2 * TOK * width * (3 * width + width + 4 * width * 2) + TOK * 2 * width * wide
    size = sum(w.size * 2 for w in weights)
    vmem = pl.BlockSpec(memory_space=pltpu.VMEM)
    return pl.pallas_call(
        functools.partial(fine_kernel, masked),
        out_shape=(
            jax.ShapeDtypeStruct((TOK, width), BF),
            jax.ShapeDtypeStruct((TOK // 4, wide), BF),
        ),
        in_specs=[pl.BlockSpec(memory_space=pltpu.SMEM), vmem] + [vmem] * 5,
        out_specs=(vmem, vmem),
        scratch_shapes=[
            pltpu.VMEM((TOK, 3 * width), BF),
            pltpu.VMEM((TOK, width), BF),
            pltpu.VMEM((width // 128, TOK, 128), F32),
        ],
        compiler_params=pltpu.CompilerParams(vmem_limit_bytes=24 << 20),
        cost_estimate=pl.CostEstimate(
            flops=flops, bytes_accessed=size + 3 * TOK * width * 2, transcendentals=TOK * 4 * width * 2
        ),
        name="fine_masked" if masked else "fine_plain",
    )(last, x, *weights)


def coarse_kernel(plan, last, table, x_ref, *rest):
    count = len(plan)
    pieces = rest[:count]
    out_ref, xn, qkv, mixed = rest[count:]
    width = x_ref.shape[1]
    x = x_ref[...].astype(F32)
    xn[...] = norm(x)

    def project(source, target, which):
        for group, refs, start in plan_groups(plan, pieces, which):
            total = 0.0
            for slot, ref, cols in refs:
                rows = ref.shape[0]
                if rows == width:
                    lhs = source[...]
                else:
                    lhs = source[:, pl.ds(pl.multiple_of(table[2 * slot], rows), rows)]
                total = total + dot(lhs, ref[:, cols])
            size = total.shape[1]
            at = pl.multiple_of(table[2 * group + 1] * size, 128)
            target(pl.ds(at, size), total)

    def keep(cols, total):
        qkv[:, cols] = total.astype(BF)

    def finish(cols, total):
        out_ref[:, cols] = (x_ref[:, cols].astype(F32) + total).astype(BF)

    project(xn, keep, 0)
    attention(qkv, mixed, width, mask_bias(last))
    project(mixed, finish, 1)


def plan_groups(plan, pieces, which):
    shards = {}
    for slot, (shard, cols) in enumerate(plan):
        if cols[which] is not None:
            shards.setdefault(shard, []).append((slot, pieces[slot], slice(*cols[which])))
    return [(refs[0][0], refs, 0) for refs in shards.values()]


def coarse_window(x, last, table, pieces, plan):
    width = x.shape[-1]
    vmem = pl.BlockSpec(memory_space=pltpu.VMEM)
    smem = pl.BlockSpec(memory_space=pltpu.SMEM)
    return pl.pallas_call(
        functools.partial(coarse_kernel, plan),
        out_shape=jax.ShapeDtypeStruct((TOK, width), BF),
        in_specs=[smem, smem, vmem] + [vmem] * len(pieces),
        out_specs=vmem,
        scratch_shapes=[
            pltpu.VMEM((TOK, width), BF),
            pltpu.VMEM((TOK, 3 * width), BF),
            pltpu.VMEM((TOK, width), BF),
        ],
        compiler_params=pltpu.CompilerParams(vmem_limit_bytes=24 << 20),
        cost_estimate=pl.CostEstimate(
            flops=8 * TOK * width * width, bytes_accessed=8 * width * width, transcendentals=TOK * TOK * 16
        ),
        name="coarse",
    )(last, table, x, *pieces)


def line_ring(count):
    return [0] + list(range(1, count, 2)) + list(range(2, count, 2))[::-1]


def moves(order):
    place = {p: i for i, p in enumerate(order)}
    return lambda p, by: order[(place[p] + by) % len(order)]


def send(value, m, n, target):
    pairs = []
    for la in range(m):
        for lo in range(n):
            ta, to = target(la, lo)
            pairs.append((la * n + lo, ta * n + to))
    return lax.ppermute(value, ("lat", "lon"), pairs)


def gather_weights(qkv_shard, proj_shard, m, n):
    deep = qkv_shard.shape[0]
    a, b = qkv_shard.shape[1], proj_shard.shape[1]
    rows = deep // 2
    places = n // 2
    along = moves(line_ring(places))
    ring = line_ring(m)
    across = moves(ring)
    side = jnp.asarray(np.array([ring.index(la) % 2 for la in range(m)], np.int32))[lax.axis_index("lat")]
    part = jnp.concatenate(
        [lax.dynamic_slice_in_dim(w, side * rows, rows, 0) for w in (qkv_shard, proj_shard)], axis=1
    )
    pieces = [qkv_shard, proj_shard]
    plan = [("own", ((0, a), None)), ("own", (None, (0, b)))]

    def swap(value):
        return send(value, m, n, lambda la, lo: (la, lo ^ 1))

    pieces += [swap(qkv_shard), swap(proj_shard)]
    plan += [("peer", ((0, a), None)), ("peer", (None, (0, b)))]
    whole = ((0, a), (a, a + b))
    for s in range(1, places):
        part = send(part, m, n, lambda la, lo: (la, 2 * along(lo // 2, 1) + lo % 2))
        other = send(part, m, n, lambda la, lo: (across(la, 1 - 2 * (lo % 2)), lo))
        pieces += [part, other, swap(part), swap(other)]
        plan += [(s, whole), (s, whole), (-s, whole), (-s, whole)]
    tables = np.zeros((m, n, len(pieces), 2), np.int32)
    for la in range(m):
        for lo in range(n):
            mine = ring.index(la) % 2
            out = [(0, lo), (0, lo), (0, lo ^ 1), (0, lo ^ 1)]
            for s in range(1, places):
                for who in (lo, lo ^ 1):
                    lon = 2 * along(who // 2, -s) + who % 2
                    out += [(mine * rows, lon), ((1 - mine) * rows, lon)]
            tables[la, lo] = out
    table = jnp.asarray(tables.reshape(m * n, -1))[lax.axis_index("lat") * n + lax.axis_index("lon")]
    return pieces, tuple(plan), table


def shifted(value, axis, steps):
    count = lax.axis_size(axis)
    return lax.ppermute(value, axis, [(s, (s + steps) % count) for s in range(count)])


def whole_body(field, qkv_fine, proj_fine, up_fine, down_fine, merge_weight, qkv_coarse, proj_coarse):
    rows, cols, width = field.shape
    wide = merge_weight.shape[1]
    m = lax.axis_size("lat")
    n = lax.axis_size("lon")
    wr, wc = rows // WIN, cols // WIN
    last = (lax.axis_index("lat") == m - 1).astype(jnp.int32).reshape(1)
    fine_weights = (qkv_fine, proj_fine, up_fine, down_fine, merge_weight)

    east = shifted(field[:, :HALF], "lon", -1)
    widened = jnp.concatenate([field[:HALF, HALF:], east[:HALF]], axis=1)
    south = shifted(widened, "lat", -1)
    a, b = qkv_coarse.shape[1], proj_coarse.shape[1]
    if a % 128 == 0 and b % 128 == 0 and n % 2 == 0 and m % 2 == 0:
        pieces, plan, table = gather_weights(qkv_coarse, proj_coarse, m, n)
    else:
        pieces = [lax.all_gather(w, "lon", axis=1, tiled=True) for w in (qkv_coarse, proj_coarse)]
        plan = ((0, ((0, a * n), None)), (0, (None, (0, b * n))))
        table = jnp.zeros((4,), jnp.int32)

    def window(i, j):
        top, left = HALF + i * WIN, HALF + j * WIN
        if i < wr - 1:
            block = field[top:top + WIN, left:left + WIN]
            if j == wc - 1:
                block = jnp.concatenate([block, east[top:top + WIN]], axis=1)
        else:
            block = field[top:, left:left + WIN]
            if j == wc - 1:
                block = jnp.concatenate([block, east[top:]], axis=1)
            block = jnp.concatenate([block, south[:, j * WIN:(j + 1) * WIN]], axis=0)
        return block.reshape(TOK, width)

    fine, merged = {}, {}
    for i in range(wr):
        for j in range(wc):
            out, mer = fine_window(window(i, j), last, fine_weights, i == wr - 1)
            fine[i, j] = out.reshape(WIN, WIN, width)
            merged[i, j] = mer.reshape(HALF, HALF, wide)

    def lay(parts):
        return jnp.concatenate(
            [jnp.concatenate([parts[i, j] for j in range(wc)], axis=1) for i in range(wr)], axis=0
        )

    coarse = lay(merged)
    below = shifted(coarse[:QUART], "lat", -1)
    tall = jnp.concatenate([coarse[QUART:], below], axis=0)
    beside = shifted(tall[:, :QUART], "lon", -1)
    coarse = jnp.concatenate([tall[:, QUART:], beside], axis=1)

    def back(values):
        down = lambda la: (la + 1) % m
        right = lambda lo: (lo + 1) % n
        side = send(values[:-HALF, -HALF:], m, n, lambda la, lo: (la, right(lo)))
        prev = send(values[-HALF:, :-HALF], m, n, lambda la, lo: (down(la), lo))
        corner = send(values[-HALF:, -HALF:], m, n, lambda la, lo: (down(la), right(lo)))
        top = jnp.concatenate([corner, prev], axis=1)
        return jnp.concatenate([top, jnp.concatenate([side, values[:-HALF, :-HALF]], axis=1)], axis=0)

    fine_out = back(lay(fine))
    cr, cc = rows // 2 // WIN, cols // 2 // WIN
    outs = {}
    for i in range(cr):
        for j in range(cc):
            block = coarse[i * WIN:(i + 1) * WIN, j * WIN:(j + 1) * WIN].reshape(TOK, wide)
            seam = last if i == cr - 1 else jnp.zeros_like(last)
            out = coarse_window(block, seam, table, pieces, plan)
            outs[i, j] = out.reshape(WIN, WIN, wide)
    coarse_out = jnp.concatenate(
        [jnp.concatenate([outs[i, j] for j in range(cc)], axis=1) for i in range(cr)], axis=0
    )
    return fine_out, back(coarse_out)


def solution(mesh):
    in_specs = (P("lat", "lon", None), P(), P(), P(), P(), P(), P(None, "lon"), P(None, "lon"))
    out_specs = (P("lat", "lon", None), P("lat", "lon", None))
    return jax.shard_map(whole_body, mesh=mesh, in_specs=in_specs, out_specs=out_specs, check_vma=False)
```

profile of v0, /device:TPU:0, one launch (start us, length us, event | category | flops | bytes accessed | tf_op | source)
XLA Modules:
  0.0 99.9 jit_solution(15730257102209593838)
XLA Ops:
  0.6 1.8 %slice.70 = bf16[32,8,512]{2,1,0:T(8,128)(2,1)} slice(bf16[32,32,512]{2,1,0:T(8,128)(2,1)} %param.10), slice={[0:32], [0:8], [0:512]} | slice | bytes 524288 | tf_op jit(solution)/shard_map/slice | solution.py:263
  2.5 4.5 %collective-permute-start = (bf16[32,8,512]{2,1,0:T(8,128)(2,1)}, bf16[32,8,512]{2,1,0:T(8,128)(2,1)S(1)}, u32[]{:S(2)}, u32[]{:S(2)}) collective-permute-start(bf16[32,8,512]{2,1,0:T(8,128)(2,1)} %slice.70), channel_id=1, source_target_pairs={{0,7},{1,0},{2,1},{3,2},{4,3},{5,4},{6,5},{7,6},{8,15},{9,8},{10,9... | collective-permute-start | bytes 786440 | tf_op jit(solution)/shard_map/ppermute | solution.py:251
  7.0 0.5 collective-permute-start.7
  7.5 1.2 %dynamic_slice.13 = s32[1]{0:T(128)} dynamic-slice(s32[4]{0:T(128)} %constant.27.clone, s32[]{:T(128)S(6)} %select_n.11), dynamic_slice_sizes={1} | dynamic-slice | bytes 12 | tf_op jit(solution)/shard_map/dynamic_slice | solution.py:217
  9.4 0.9 constant_dynamic-slice_fusion
  10.3 1.0 %constant_dynamic-slice_fusion.1 = bf16[512,384]{1,0:T(8,128)(2,1)S(1)} fusion(bf16[1024,384]{1,0:T(8,128)(2,1)} %rest_0_.1, s32[]{:T(128)S(6)} %select_n.12), kind=kLoop, calls=%fused_computation.21 | loop fusion | bytes 786436 | tf_op jit(solution)/shard_map/dynamic_slice | solution.py:219
  11.4 0.8 pad_maximum_fusion.5
  12.2 1.0 slice.79
  13.2 0.0 copy-start
  13.2 2.2 %copy-done = bf16[2048,1024]{1,0:T(8,128)(2,1)S(1)} copy-done((bf16[2048,1024]{1,0:T(8,128)(2,1)S(1)}, bf16[2048,1024]{1,0:T(8,128)(2,1)}, u32[]{:S(2)}) %copy-start) | copy-done | bytes 4194328
  15.4 1.6 %copy-done.3 = bf16[2048,512]{1,0:T(8,128)(2,1)S(1)} copy-done((bf16[2048,512]{1,0:T(8,128)(2,1)S(1)}, bf16[2048,512]{1,0:T(8,128)(2,1)}, u32[]{:S(2)}) %copy-start.3) | copy-done | bytes 2097176
  17.0 1.4 %copy-done.5 = bf16[512,1536]{1,0:T(8,128)(2,1)S(1)} copy-done((bf16[512,1536]{1,0:T(8,128)(2,1)S(1)}, bf16[512,1536]{1,0:T(8,128)(2,1)}, u32[]{:S(2)}) %copy-start.5) | copy-done | bytes 1572888
  18.4 4.9 %fine_plain.2 = (bf16[256,512]{1,0:T(8,128)(2,1)S(1)}, bf16[64,1024]{1,0:T(8,128)(2,1)S(1)}) custom-call(s32[1]{0:T(128)} %bitcast.last, bf16[256,512]{1,0:T(8,128)(2,1)S(1)} %bitcast.38, bf16[512,1536]{1,0:T(8,128)(2,1)S(1)} %copy-done.5, bf16[512,512]{1,0:T(8,128)(2,1)S(1)} %copy-done.7, bf16[512,2048]{1,0:T(8,128)(2,1)S(1)} %copy-done.2, ...), custom_call_target="tpu_custom_call" | custom-call | flops 1879048192 | bytes 11272192 | tf_op jit(solution)/shard_map/fine_plain/pallas_call | solution.py:107
  23.4 2.5 %collective-permute-start.1 = (bf16[8,32,512]{2,1,0:T(8,128)(2,1)S(1)}, bf16[8,32,512]{2,1,0:T(8,128)(2,1)S(1)}, u32[]{:S(2)}, u32[]{:S(2)}) collective-permute-start(bf16[8,32,512]{2,1,0:T(8,128)(2,1)S(1)} %pad_maximum_fusion.6), channel_id=1, source_target_pairs={{0,24},{8,0},{16,8},{24,16},{1,25},{9,1},{17,9},{25,17},{2,26},{10... | collective-permute-start | bytes 786440 | tf_op jit(solution)/shard_map/ppermute | solution.py:251
  26.0 1.3 %collective-permute-done.9.rest_4_ = bf16[512,512]{1,0:T(8,128)(2,1)} collective-permute-done((bf16[512,512]{1,0:T(8,128)(2,1)}, bf16[512,512]{1,0:T(8,128)(2,1)}, u32[]{:S(2)}, u32[]{:S(2)}) %collective-permute-start.9) | collective-permute-done | bytes 524320 | tf_op jit(solution)/shard_map/ppermute | solution.py:206
  27.3 4.9 %fine_plain.3 = (bf16[256,512]{1,0:T(8,128)(2,1)S(1)}, bf16[64,1024]{1,0:T(8,128)(2,1)S(1)}) custom-call(s32[1]{0:T(128)} %bitcast.last, bf16[256,512]{1,0:T(8,128)(2,1)S(1)} %bitcast.37, bf16[512,1536]{1,0:T(8,128)(2,1)S(1)} %copy-done.5, bf16[512,512]{1,0:T(8,128)(2,1)S(1)} %copy-done.7, bf16[512,2048]{1,0:T(8,128)(2,1)S(1)} %copy-done.2, ...), custom_call_target="tpu_custom_call" | custom-call | flops 1879048192 | bytes 11272192 | tf_op jit(solution)/shard_map/fine_plain/pallas_call | solution.py:107
  32.2 2.5 %collective-permute-start.5 = (bf16[4,16,1024]{2,1,0:T(8,128)(2,1)S(1)}, bf16[4,16,1024]{2,1,0:T(8,128)(2,1)S(1)}, u32[]{:S(2)}, u32[]{:S(2)}) collective-permute-start(bf16[4,16,1024]{2,1,0:T(8,128)(2,1)S(1)} %pad_maximum_fusion.12), channel_id=1, source_target_pairs={{0,24},{8,0},{16,8},{24,16},{1,25},{9,1},{17,9},{25,17},{2,26},{10... | collective-permute-start | bytes 393224 | tf_op jit(solution)/shard_map/ppermute | solution.py:251
  34.7 6.7 %collective-permute-done.13.rest_8_ = bf16[512,512]{1,0:T(8,128)(2,1)} collective-permute-done((bf16[512,512]{1,0:T(8,128)(2,1)}, bf16[512,512]{1,0:T(8,128)(2,1)}, u32[]{:S(2)}, u32[]{:S(2)}) %collective-permute-start.13) | collective-permute-done | bytes 524320 | tf_op jit(solution)/shard_map/ppermute | solution.py:206
  41.5 0.0 copy-start.6
  41.5 4.9 %fine_masked.3 = (bf16[256,512]{1,0:T(8,128)(2,1)S(1)}, bf16[64,1024]{1,0:T(8,128)(2,1)S(1)}) custom-call(s32[1]{0:T(128)} %bitcast.last, bf16[256,512]{1,0:T(8,128)(2,1)S(1)} %bitcast.40, bf16[512,1536]{1,0:T(8,128)(2,1)S(1)} %copy-done.5, bf16[512,512]{1,0:T(8,128)(2,1)S(1)} %copy-done.7, bf16[512,2048]{1,0:T(8,128)(2,1)S(1)} %copy-done.2, ...), custom_call_target="tpu_custom_call" | custom-call | flops 1879048192 | bytes 11272192 | tf_op jit(solution)/shard_map/fine_masked/pallas_call | solution.py:107
  46.4 4.9 %fine_masked.2 = (bf16[256,512]{1,0:T(8,128)(2,1)S(1)}, bf16[64,1024]{1,0:T(8,128)(2,1)S(1)}) custom-call(s32[1]{0:T(128)} %bitcast.last, bf16[256,512]{1,0:T(8,128)(2,1)S(1)} %bitcast.39, bf16[512,1536]{1,0:T(8,128)(2,1)S(1)} %copy-done.6, bf16[512,512]{1,0:T(8,128)(2,1)S(1)} %copy-done.7, bf16[512,2048]{1,0:T(8,128)(2,1)S(1)} %copy-done.2, ...), custom_call_target="tpu_custom_call" | custom-call | flops 1879048192 | bytes 11272192 | tf_op jit(solution)/shard_map/fine_masked/pallas_call | solution.py:107
  51.4 0.5 collective-permute-start.6
  51.8 1.1 %collective-permute-start.10 = (bf16[512,512]{1,0:T(8,128)(2,1)}, bf16[512,512]{1,0:T(8,128)(2,1)S(1)}, u32[]{:S(2)}, u32[]{:S(2)}) collective-permute-start(bf16[512,512]{1,0:T(8,128)(2,1)} %collective-permute-done.9.rest_4_), channel_id=1, source_target_pairs={{0,8},{1,17},{2,10},{3,19},{4,12},{5,21},{6,14},{7,23},{8,24},{9,1... | collective-permute-start | bytes 1572872 | tf_op jit(solution)/shard_map/ppermute | solution.py:206
  53.0 0.2 collective-permute-start.11
  53.2 1.2 %collective-permute-done.6 = bf16[16,4,1024]{2,1,0:T(4,128)(2,1)} collective-permute-done((bf16[16,4,1024]{2,1,0:T(4,128)(2,1)S(1)}, bf16[16,4,1024]{2,1,0:T(4,128)(2,1)}, u32[]{:S(2)}, u32[]{:S(2)}) %collective-permute-start.6) | collective-permute-done | bytes 131104 | tf_op jit(solution)/shard_map/ppermute | solution.py:251
  54.4 1.1 %collective-permute-start.14 = (bf16[512,512]{1,0:T(8,128)(2,1)}, bf16[512,512]{1,0:T(8,128)(2,1)S(1)}, u32[]{:S(2)}, u32[]{:S(2)}) collective-permute-start(bf16[512,512]{1,0:T(8,128)(2,1)} %collective-permute-done.13.rest_8_), channel_id=1, source_target_pairs={{0,8},{1,17},{2,10},{3,19},{4,12},{5,21},{6,14},{7,23},{8,24},{9,1... | collective-permute-start | bytes 1572872 | tf_op jit(solution)/shard_map/ppermute | solution.py:206
  55.4 1.6 %collective-permute-start.18 = (bf16[512,512]{1,0:T(8,128)(2,1)}, bf16[512,512]{1,0:T(8,128)(2,1)S(1)}, u32[]{:S(2)}, u32[]{:S(2)}) collective-permute-start(bf16[512,512]{1,0:T(8,128)(2,1)} %collective-permute-done.17.rest_12_), channel_id=1, source_target_pairs={{0,8},{1,17},{2,10},{3,19},{4,12},{5,21},{6,14},{7,23},{8,24},{9,1... | collective-permute-start | bytes 1572872 | tf_op jit(solution)/shard_map/ppermute | solution.py:206
  57.0 2.1 %collective-permute-start.15 = (bf16[512,512]{1,0:T(8,128)(2,1)}, bf16[512,512]{1,0:T(8,128)(2,1)S(1)}, u32[]{:S(2)}, u32[]{:S(2)}) collective-permute-start(bf16[512,512]{1,0:T(8,128)(2,1)} %collective-permute-done.13.rest_8_), channel_id=1, source_target_pairs={{0,1},{1,0},{2,3},{3,2},{4,5},{5,4},{6,7},{7,6},{8,9},{9,8},{10,11... | collective-permute-start | bytes 1572872 | tf_op jit(solution)/shard_map/ppermute | solution.py:206
  59.1 2.1 %collective-permute-done.10.rest_5_ = bf16[512,512]{1,0:T(8,128)(2,1)S(1)} collective-permute-done((bf16[512,512]{1,0:T(8,128)(2,1)}, bf16[512,512]{1,0:T(8,128)(2,1)S(1)}, u32[]{:S(2)}, u32[]{:S(2)}) %collective-permute-start.10) | collective-permute-done | bytes 524320 | tf_op jit(solution)/shard_map/ppermute | solution.py:206
  61.2 0.5 collective-permute-start.19
  61.7 5.1 %collective-permute-done.14.rest_9_ = bf16[512,512]{1,0:T(8,128)(2,1)S(1)} collective-permute-done((bf16[512,512]{1,0:T(8,128)(2,1)}, bf16[512,512]{1,0:T(8,128)(2,1)S(1)}, u32[]{:S(2)}, u32[]{:S(2)}) %collective-permute-start.14) | collective-permute-done | bytes 524320 | tf_op jit(solution)/shard_map/ppermute | solution.py:206
  66.9 5.6 %collective-permute-done.18.rest_13_ = bf16[512,512]{1,0:T(8,128)(2,1)S(1)} collective-permute-done((bf16[512,512]{1,0:T(8,128)(2,1)}, bf16[512,512]{1,0:T(8,128)(2,1)S(1)}, u32[]{:S(2)}, u32[]{:S(2)}) %collective-permute-start.18) | collective-permute-done | bytes 524320 | tf_op jit(solution)/shard_map/ppermute | solution.py:206
  72.5 0.7 fusion.5.table
  73.2 1.0 %fusion.4 = bf16[16,16,1024]{2,1,0:T(8,128)(2,1)S(1)} fusion(bf16[8,8,1024]{2,1,0:T(8,128)(2,1)} %bitcast.44, bf16[8,8,1024]{2,1,0:T(8,128)(2,1)S(1)} %bitcast.42, bf16[8,8,1024]{2,1,0:T(8,128)(2,1)S(1)} %bitcast.32, bf16[8,8,1024]{2,1,0:T(8,128)(2,1)S(1)} %bitcast.29, bf16[4,16,1024]{2,1,0:T(8,128)(2,1)} %copy-done.16), kind=kLoop, calls=%fused_computation.7 | loop fusion | flops 2621440 | bytes 1179648 | tf_op jit(solution)/shard_map/concatenate | solution.py:301
  74.2 0.1 slice.98
  74.4 1.1 %pad_maximum_fusion.4 = bf16[16,16,1024]{2,1,0:T(8,128)(2,1)S(1)} fusion(bf16[16,4,1024]{2,1,0:T(4,128)(2,1)} %collective-permute-done.6, bf16[16,12,1024]{2,1,0:T(8,128)(2,1)S(1)} %slice.98), kind=kLoop, calls=%fused_computation.9 | loop fusion | flops 1048576 | bytes 1048576 | tf_op jit(solution)/shard_map/concatenate | solution.py:303
  75.6 1.3 %collective-permute-start.2 = (bf16[8,8,512]{2,1,0:T(8,128)(2,1)S(1)}, bf16[8,8,512]{2,1,0:T(8,128)(2,1)S(1)}, u32[]{:S(2)}, u32[]{:S(2)}) collective-permute-start(bf16[8,8,512]{2,1,0:T(8,128)(2,1)S(1)} %slice.95), channel_id=1, source_target_pairs={{0,9},{1,10},{2,11},{3,12},{4,13},{5,14},{6,15},{7,8},{8,17},{9,18... | collective-permute-start | bytes 196616 | tf_op jit(solution)/shard_map/ppermute | solution.py:206
  76.8 1.6 %collective-permute-start.4 = (bf16[24,8,512]{2,1,0:T(8,128)(2,1)S(1)}, bf16[24,8,512]{2,1,0:T(8,128)(2,1)S(1)}, u32[]{:S(2)}, u32[]{:S(2)}) collective-permute-start(bf16[24,8,512]{2,1,0:T(8,128)(2,1)S(1)} %maximum_maximum_fusion.1), channel_id=1, source_target_pairs={{0,1},{1,2},{2,3},{3,4},{4,5},{5,6},{6,7},{7,0},{8,9},{9,10},{10,1... | collective-permute-start | bytes 589832 | tf_op jit(solution)/shard_map/ppermute | solution.py:206
  78.4 1.5 %collective-permute-start.3 = (bf16[8,24,512]{2,1,0:T(8,128)(2,1)S(1)}, bf16[8,24,512]{2,1,0:T(8,128)(2,1)S(1)}, u32[]{:S(2)}, u32[]{:S(2)}) collective-permute-start(bf16[8,24,512]{2,1,0:T(8,128)(2,1)S(1)} %pad_maximum_fusion.10), channel_id=1, source_target_pairs={{0,8},{1,9},{2,10},{3,11},{4,12},{5,13},{6,14},{7,15},{8,16},{9,17... | collective-permute-start | bytes 589832 | tf_op jit(solution)/shard_map/ppermute | solution.py:206
  79.9 8.4 %coarse.1 = bf16[256,1024]{1,0:T(8,128)(2,1)S(1)} custom-call(s32[1]{0:T(128)} %bitcast.last, s32[32]{0:T(128)S(1)} %fusion.5.table, bf16[256,1024]{1,0:T(8,128)(2,1)S(1)} %bitcast.25, bf16[1024,384]{1,0:T(8,128)(2,1)S(1)} %copy-done.8, bf16[1024,128]{1,0:T(8,128)(2,1)S(1)} %copy-done.13, bf16[1024,384]{1,0:T(8,128)(2,1)} %collective-permute-done.7.rest_2_, ...), custom_call_target="tpu_custom_call" | custom-call | flops 2147483648 | bytes 8388608 | tf_op jit(solution)/shard_map/coarse/pallas_call | solution.py:173
  88.3 1.6 %collective-permute-start.21 = (bf16[8,8,1024]{2,1,0:T(8,128)(2,1)S(1)}, bf16[8,8,1024]{2,1,0:T(8,128)(2,1)S(1)}, u32[]{:S(2)}, u32[]{:S(2)}) collective-permute-start(bf16[8,8,1024]{2,1,0:T(8,128)(2,1)S(1)} %get-tuple-element.18), channel_id=1, source_target_pairs={{0,9},{1,10},{2,11},{3,12},{4,13},{5,14},{6,15},{7,8},{8,17},{9,18... | collective-permute-start | bytes 393224 | tf_op jit(solution)/shard_map/ppermute | solution.py:206
  89.9 0.9 collective-permute-start.23
  90.8 0.5 collective-permute-start.22
  91.3 1.1 %fusion.2 = bf16[32,32,512]{2,1,0:T(8,128)(2,1)} fusion(bf16[16,16,512]{2,1,0:T(8,128)(2,1)S(1)} %bitcast.21, bf16[16,16,512]{2,1,0:T(8,128)(2,1)S(1)} %bitcast.24, bf16[16,16,512]{2,1,0:T(8,128)(2,1)S(1)} %bitcast.36, bf16[16,16,512]{2,1,0:T(8,128)(2,1)S(1)} %bitcast.34, bf16[24,8,512]{2,1,0:T(8,128)(2,1)S(1)} %collective-permute-done.4, ...), kind=kLoop, calls=%fused_computation.3 | loop fusion | flops 7340032 | bytes 2555904 | tf_op jit(solution)/shard_map/concatenate | solution.py:312
  92.4 4.1 %collective-permute-done.21 = bf16[8,8,1024]{2,1,0:T(8,128)(2,1)S(1)} collective-permute-done((bf16[8,8,1024]{2,1,0:T(8,128)(2,1)S(1)}, bf16[8,8,1024]{2,1,0:T(8,128)(2,1)S(1)}, u32[]{:S(2)}, u32[]{:S(2)}) %collective-permute-start.21) | collective-permute-done | bytes 131104 | tf_op jit(solution)/shard_map/ppermute | solution.py:206
  96.5 0.5 collective-permute-done.23
  97.0 2.1 %collective-permute-done.22 = bf16[8,8,1024]{2,1,0:T(8,128)(2,1)S(1)} collective-permute-done((bf16[8,8,1024]{2,1,0:T(8,128)(2,1)S(1)}, bf16[8,8,1024]{2,1,0:T(8,128)(2,1)S(1)}, u32[]{:S(2)}, u32[]{:S(2)}) %collective-permute-start.22) | collective-permute-done | bytes 131104 | tf_op jit(solution)/shard_map/ppermute | solution.py:206
  99.1 0.8 maximum_maximum_fusion
  (67 shorter events, 0.4 us)
Async XLA Ops:
  0.6 12.6 %copy-start.2 = (bf16[512,2048]{1,0:T(8,128)(2,1)S(1)}, bf16[512,2048]{1,0:T(8,128)(2,1)}, u32[]{:S(2)}) copy-start(bf16[512,2048]{1,0:T(8,128)(2,1)} %vu.7) | copy-start | bytes 6291460
  0.6 12.6 %copy-start.7 = (bf16[512,512]{1,0:T(8,128)(2,1)S(1)}, bf16[512,512]{1,0:T(8,128)(2,1)}, u32[]{:S(2)}) copy-start(bf16[512,512]{1,0:T(8,128)(2,1)} %vp.7) | copy-start | bytes 1572868
  2.5 20.9 %collective-permute-start = (bf16[32,8,512]{2,1,0:T(8,128)(2,1)}, bf16[32,8,512]{2,1,0:T(8,128)(2,1)S(1)}, u32[]{:S(2)}, u32[]{:S(2)}) collective-permute-start(bf16[32,8,512]{2,1,0:T(8,128)(2,1)} %slice.70), channel_id=1, source_target_pairs={{0,7},{1,0},{2,1},{3,2},{4,3},{5,4},{6,5},{7,6},{8,15},{9,8},{10,9... | collective-permute-start | bytes 786440 | tf_op jit(solution)/shard_map/ppermute | solution.py:251
  7.0 46.0 %collective-permute-start.8 = (bf16[1024,128]{1,0:T(8,128)(2,1)}, bf16[1024,128]{1,0:T(8,128)(2,1)}, u32[]{:S(2)}, u32[]{:S(2)}) collective-permute-start(bf16[1024,128]{1,0:T(8,128)(2,1)} %rest_1_.1), channel_id=1, source_target_pairs={{0,1},{1,0},{2,3},{3,2},{4,5},{5,4},{6,7},{7,6},{8,9},{9,8},{10,11... | collective-permute-start | bytes 786440 | tf_op jit(solution)/shard_map/ppermute | solution.py:206
  7.0 50.1 %collective-permute-start.7 = (bf16[1024,384]{1,0:T(8,128)(2,1)}, bf16[1024,384]{1,0:T(8,128)(2,1)}, u32[]{:S(2)}, u32[]{:S(2)}) collective-permute-start(bf16[1024,384]{1,0:T(8,128)(2,1)} %rest_0_.1), channel_id=1, source_target_pairs={{0,1},{1,0},{2,3},{3,2},{4,5},{5,4},{6,7},{7,6},{8,9},{9,8},{10,11... | collective-permute-start | bytes 2359304 | tf_op jit(solution)/shard_map/ppermute | solution.py:206
  12.2 15.0 %collective-permute-start.9 = (bf16[512,512]{1,0:T(8,128)(2,1)}, bf16[512,512]{1,0:T(8,128)(2,1)}, u32[]{:S(2)}, u32[]{:S(2)}) collective-permute-start(bf16[512,512]{1,0:T(8,128)(2,1)} %pad_maximum_fusion.5), channel_id=1, source_target_pairs={{0,2},{1,3},{2,6},{3,7},{4,0},{5,1},{6,4},{7,5},{8,10},{9,11},{10,... | collective-permute-start | bytes 1572872 | tf_op jit(solution)/shard_map/ppermute | solution.py:206
  13.2 2.2 %copy-start = (bf16[2048,1024]{1,0:T(8,128)(2,1)S(1)}, bf16[2048,1024]{1,0:T(8,128)(2,1)}, u32[]{:S(2)}) copy-start(bf16[2048,1024]{1,0:T(8,128)(2,1)} %vm.7) | copy-start | bytes 12582916
  15.4 1.6 %copy-start.3 = (bf16[2048,512]{1,0:T(8,128)(2,1)S(1)}, bf16[2048,512]{1,0:T(8,128)(2,1)}, u32[]{:S(2)}) copy-start(bf16[2048,512]{1,0:T(8,128)(2,1)} %vd.7) | copy-start | bytes 6291460
  17.0 1.4 %copy-start.5 = (bf16[512,1536]{1,0:T(8,128)(2,1)S(1)}, bf16[512,1536]{1,0:T(8,128)(2,1)}, u32[]{:S(2)}) copy-start(bf16[512,1536]{1,0:T(8,128)(2,1)} %vq.7) | copy-start | bytes 4718596
  18.4 4.9 %copy-start.15 = (bf16[32,32,512]{2,1,0:T(8,128)(2,1)S(1)}, bf16[32,32,512]{2,1,0:T(8,128)(2,1)}, u32[]{:S(2)}) copy-start(bf16[32,32,512]{2,1,0:T(8,128)(2,1)} %param.10) | copy-start | bytes 3145732
  23.3 8.8 %copy-start.9 = (bf16[256,512]{1,0:T(8,128)(2,1)}, bf16[256,512]{1,0:T(8,128)(2,1)S(1)}, u32[]{:S(2)}) copy-start(bf16[256,512]{1,0:T(8,128)(2,1)S(1)} %get-tuple-element.12) | copy-start | bytes 786436
  23.4 11.2 %collective-permute-start.1 = (bf16[8,32,512]{2,1,0:T(8,128)(2,1)S(1)}, bf16[8,32,512]{2,1,0:T(8,128)(2,1)S(1)}, u32[]{:S(2)}, u32[]{:S(2)}) collective-permute-start(bf16[8,32,512]{2,1,0:T(8,128)(2,1)S(1)} %pad_maximum_fusion.6), channel_id=1, source_target_pairs={{0,24},{8,0},{16,8},{24,16},{1,25},{9,1},{17,9},{25,17},{2,26},{10... | collective-permute-start | bytes 786440 | tf_op jit(solution)/shard_map/ppermute | solution.py:251
  27.3 14.2 %collective-permute-start.13 = (bf16[512,512]{1,0:T(8,128)(2,1)}, bf16[512,512]{1,0:T(8,128)(2,1)}, u32[]{:S(2)}, u32[]{:S(2)}) collective-permute-start(bf16[512,512]{1,0:T(8,128)(2,1)} %collective-permute-done.9.rest_4_), channel_id=1, source_target_pairs={{0,2},{1,3},{2,6},{3,7},{4,0},{5,1},{6,4},{7,5},{8,10},{9,11},{10,... | collective-permute-start | bytes 1572872 | tf_op jit(solution)/shard_map/ppermute | solution.py:206
  32.1 14.2 %copy-start.11 = (bf16[256,512]{1,0:T(8,128)(2,1)}, bf16[256,512]{1,0:T(8,128)(2,1)S(1)}, u32[]{:S(2)}) copy-start(bf16[256,512]{1,0:T(8,128)(2,1)S(1)} %get-tuple-element.13) | copy-start | bytes 786436
  32.2 19.1 %collective-permute-start.5 = (bf16[4,16,1024]{2,1,0:T(8,128)(2,1)S(1)}, bf16[4,16,1024]{2,1,0:T(8,128)(2,1)S(1)}, u32[]{:S(2)}, u32[]{:S(2)}) collective-permute-start(bf16[4,16,1024]{2,1,0:T(8,128)(2,1)S(1)} %pad_maximum_fusion.12), channel_id=1, source_target_pairs={{0,24},{8,0},{16,8},{24,16},{1,25},{9,1},{17,9},{25,17},{2,26},{10... | collective-permute-start | bytes 393224 | tf_op jit(solution)/shard_map/ppermute | solution.py:251
  41.4 14.0 %collective-permute-start.17 = (bf16[512,512]{1,0:T(8,128)(2,1)}, bf16[512,512]{1,0:T(8,128)(2,1)}, u32[]{:S(2)}, u32[]{:S(2)}) collective-permute-start(bf16[512,512]{1,0:T(8,128)(2,1)} %collective-permute-done.13.rest_8_), channel_id=1, source_target_pairs={{0,2},{1,3},{2,6},{3,7},{4,0},{5,1},{6,4},{7,5},{8,10},{9,11},{10,... | collective-permute-start | bytes 1572872 | tf_op jit(solution)/shard_map/ppermute | solution.py:206
  41.4 4.9 %copy-start.1 = (bf16[2048,1024]{1,0:T(8,128)(2,1)S(1)}, bf16[2048,1024]{1,0:T(8,128)(2,1)}, u32[]{:S(2)}) copy-start(bf16[2048,1024]{1,0:T(8,128)(2,1)} %vm.7) | copy-start | bytes 12582916
  41.4 4.9 %copy-start.4 = (bf16[2048,512]{1,0:T(8,128)(2,1)S(1)}, bf16[2048,512]{1,0:T(8,128)(2,1)}, u32[]{:S(2)}) copy-start(bf16[2048,512]{1,0:T(8,128)(2,1)} %vd.7) | copy-start | bytes 6291460
  41.5 4.9 %copy-start.6 = (bf16[512,1536]{1,0:T(8,128)(2,1)S(1)}, bf16[512,1536]{1,0:T(8,128)(2,1)}, u32[]{:S(2)}) copy-start(bf16[512,1536]{1,0:T(8,128)(2,1)} %vq.7) | copy-start | bytes 4718596
  51.3 4.2 %copy-start.14 = (bf16[64,1024]{1,0:T(8,128)(2,1)}, bf16[64,1024]{1,0:T(8,128)(2,1)S(1)}, u32[]{:S(2)}) copy-start(bf16[64,1024]{1,0:T(8,128)(2,1)S(1)} %get-tuple-element.17) | copy-start | bytes 393220
  51.3 23.1 %copy-start.10 = (bf16[256,512]{1,0:T(8,128)(2,1)S(1)}, bf16[256,512]{1,0:T(8,128)(2,1)}, u32[]{:S(2)}) copy-start(bf16[256,512]{1,0:T(8,128)(2,1)} %copy-done.9) | copy-start | bytes 786436
  51.3 23.1 %copy-start.12 = (bf16[256,512]{1,0:T(8,128)(2,1)S(1)}, bf16[256,512]{1,0:T(8,128)(2,1)}, u32[]{:S(2)}) copy-start(bf16[256,512]{1,0:T(8,128)(2,1)} %copy-done.11) | copy-start | bytes 786436
  51.3 4.1 %copy-start.16 = (bf16[4,16,1024]{2,1,0:T(8,128)(2,1)}, bf16[4,16,1024]{2,1,0:T(8,128)(2,1)S(1)}, u32[]{:S(2)}) copy-start(bf16[4,16,1024]{2,1,0:T(8,128)(2,1)S(1)} %collective-permute-done.5) | copy-start | bytes 393220
  51.4 3.0 %collective-permute-start.6 = (bf16[16,4,1024]{2,1,0:T(4,128)(2,1)S(1)}, bf16[16,4,1024]{2,1,0:T(4,128)(2,1)}, u32[]{:S(2)}, u32[]{:S(2)}) collective-permute-start(bf16[16,4,1024]{2,1,0:T(4,128)(2,1)S(1)} %pad_maximum_fusion.11), channel_id=1, source_target_pairs={{0,7},{1,0},{2,1},{3,2},{4,3},{5,4},{6,5},{7,6},{8,15},{9,8},{10,9... | collective-permute-start | bytes 393224 | tf_op jit(solution)/shard_map/ppermute | solution.py:251
  51.8 9.4 %collective-permute-start.10 = (bf16[512,512]{1,0:T(8,128)(2,1)}, bf16[512,512]{1,0:T(8,128)(2,1)S(1)}, u32[]{:S(2)}, u32[]{:S(2)}) collective-permute-start(bf16[512,512]{1,0:T(8,128)(2,1)} %collective-permute-done.9.rest_4_), channel_id=1, source_target_pairs={{0,8},{1,17},{2,10},{3,19},{4,12},{5,21},{6,14},{7,23},{8,24},{9,1... | collective-permute-start | bytes 1572872 | tf_op jit(solution)/shard_map/ppermute | solution.py:206
  53.0 8.3 %collective-permute-start.11 = (bf16[512,512]{1,0:T(8,128)(2,1)}, bf16[512,512]{1,0:T(8,128)(2,1)S(1)}, u32[]{:S(2)}, u32[]{:S(2)}) collective-permute-start(bf16[512,512]{1,0:T(8,128)(2,1)} %collective-permute-done.9.rest_4_), channel_id=1, source_target_pairs={{0,1},{1,0},{2,3},{3,2},{4,5},{5,4},{6,7},{7,6},{8,9},{9,8},{10,11... | collective-permute-start | bytes 1572872 | tf_op jit(solution)/shard_map/ppermute | solution.py:206
  54.4 12.5 %collective-permute-start.14 = (bf16[512,512]{1,0:T(8,128)(2,1)}, bf16[512,512]{1,0:T(8,128)(2,1)S(1)}, u32[]{:S(2)}, u32[]{:S(2)}) collective-permute-start(bf16[512,512]{1,0:T(8,128)(2,1)} %collective-permute-done.13.rest_8_), channel_id=1, source_target_pairs={{0,8},{1,17},{2,10},{3,19},{4,12},{5,21},{6,14},{7,23},{8,24},{9,1... | collective-permute-start | bytes 1572872 | tf_op jit(solution)/shard_map/ppermute | solution.py:206
  55.4 17.0 %collective-permute-start.18 = (bf16[512,512]{1,0:T(8,128)(2,1)}, bf16[512,512]{1,0:T(8,128)(2,1)S(1)}, u32[]{:S(2)}, u32[]{:S(2)}) collective-permute-start(bf16[512,512]{1,0:T(8,128)(2,1)} %collective-permute-done.17.rest_12_), channel_id=1, source_target_pairs={{0,8},{1,17},{2,10},{3,19},{4,12},{5,21},{6,14},{7,23},{8,24},{9,1... | collective-permute-start | bytes 1572872 | tf_op jit(solution)/shard_map/ppermute | solution.py:206
  57.0 18.5 %collective-permute-start.15 = (bf16[512,512]{1,0:T(8,128)(2,1)}, bf16[512,512]{1,0:T(8,128)(2,1)S(1)}, u32[]{:S(2)}, u32[]{:S(2)}) collective-permute-start(bf16[512,512]{1,0:T(8,128)(2,1)} %collective-permute-done.13.rest_8_), channel_id=1, source_target_pairs={{0,1},{1,0},{2,3},{3,2},{4,5},{5,4},{6,7},{7,6},{8,9},{9,8},{10,11... | collective-permute-start | bytes 1572872 | tf_op jit(solution)/shard_map/ppermute | solution.py:206
  61.2 15.6 %collective-permute-start.12 = (bf16[512,512]{1,0:T(8,128)(2,1)S(1)}, bf16[512,512]{1,0:T(8,128)(2,1)S(1)}, u32[]{:S(2)}, u32[]{:S(2)}) collective-permute-start(bf16[512,512]{1,0:T(8,128)(2,1)S(1)} %collective-permute-done.10.rest_5_), channel_id=1, source_target_pairs={{0,1},{1,0},{2,3},{3,2},{4,5},{5,4},{6,7},{7,6},{8,9},{9,8},{10,11... | collective-permute-start | bytes 1572872 | tf_op jit(solution)/shard_map/ppermute | solution.py:206
  61.2 17.2 %collective-permute-start.19 = (bf16[512,512]{1,0:T(8,128)(2,1)}, bf16[512,512]{1,0:T(8,128)(2,1)S(1)}, u32[]{:S(2)}, u32[]{:S(2)}) collective-permute-start(bf16[512,512]{1,0:T(8,128)(2,1)} %collective-permute-done.17.rest_12_), channel_id=1, source_target_pairs={{0,1},{1,0},{2,3},{3,2},{4,5},{5,4},{6,7},{7,6},{8,9},{9,8},{10,11... | collective-permute-start | bytes 1572872 | tf_op jit(solution)/shard_map/ppermute | solution.py:206
  66.8 13.1 %collective-permute-start.16 = (bf16[512,512]{1,0:T(8,128)(2,1)S(1)}, bf16[512,512]{1,0:T(8,128)(2,1)S(1)}, u32[]{:S(2)}, u32[]{:S(2)}) collective-permute-start(bf16[512,512]{1,0:T(8,128)(2,1)S(1)} %collective-permute-done.14.rest_9_), channel_id=1, source_target_pairs={{0,1},{1,0},{2,3},{3,2},{4,5},{5,4},{6,7},{7,6},{8,9},{9,8},{10,11... | collective-permute-start | bytes 1572872 | tf_op jit(solution)/shard_map/ppermute | solution.py:206
  72.5 7.4 %collective-permute-start.20 = (bf16[512,512]{1,0:T(8,128)(2,1)S(1)}, bf16[512,512]{1,0:T(8,128)(2,1)S(1)}, u32[]{:S(2)}, u32[]{:S(2)}) collective-permute-start(bf16[512,512]{1,0:T(8,128)(2,1)S(1)} %collective-permute-done.18.rest_13_), channel_id=1, source_target_pairs={{0,1},{1,0},{2,3},{3,2},{4,5},{5,4},{6,7},{7,6},{8,9},{9,8},{10,11... | collective-permute-start | bytes 1572872 | tf_op jit(solution)/shard_map/ppermute | solution.py:206
  74.2 5.7 %copy-start.8 = (bf16[1024,384]{1,0:T(8,128)(2,1)S(1)}, bf16[1024,384]{1,0:T(8,128)(2,1)}, u32[]{:S(2)}) copy-start(bf16[1024,384]{1,0:T(8,128)(2,1)} %rest_0_.1) | copy-start | bytes 2359300
  74.2 5.7 %copy-start.13 = (bf16[1024,128]{1,0:T(8,128)(2,1)S(1)}, bf16[1024,128]{1,0:T(8,128)(2,1)}, u32[]{:S(2)}) copy-start(bf16[1024,128]{1,0:T(8,128)(2,1)} %rest_1_.1) | copy-start | bytes 786436
  75.6 15.3 %collective-permute-start.2 = (bf16[8,8,512]{2,1,0:T(8,128)(2,1)S(1)}, bf16[8,8,512]{2,1,0:T(8,128)(2,1)S(1)}, u32[]{:S(2)}, u32[]{:S(2)}) collective-permute-start(bf16[8,8,512]{2,1,0:T(8,128)(2,1)S(1)} %slice.95), channel_id=1, source_target_pairs={{0,9},{1,10},{2,11},{3,12},{4,13},{5,14},{6,15},{7,8},{8,17},{9,18... | collective-permute-start | bytes 196616 | tf_op jit(solution)/shard_map/ppermute | solution.py:206
  76.8 14.4 %collective-permute-start.4 = (bf16[24,8,512]{2,1,0:T(8,128)(2,1)S(1)}, bf16[24,8,512]{2,1,0:T(8,128)(2,1)S(1)}, u32[]{:S(2)}, u32[]{:S(2)}) collective-permute-start(bf16[24,8,512]{2,1,0:T(8,128)(2,1)S(1)} %maximum_maximum_fusion.1), channel_id=1, source_target_pairs={{0,1},{1,2},{2,3},{3,4},{4,5},{5,6},{6,7},{7,0},{8,9},{9,10},{10,1... | collective-permute-start | bytes 589832 | tf_op jit(solution)/shard_map/ppermute | solution.py:206
  78.4 12.9 %collective-permute-start.3 = (bf16[8,24,512]{2,1,0:T(8,128)(2,1)S(1)}, bf16[8,24,512]{2,1,0:T(8,128)(2,1)S(1)}, u32[]{:S(2)}, u32[]{:S(2)}) collective-permute-start(bf16[8,24,512]{2,1,0:T(8,128)(2,1)S(1)} %pad_maximum_fusion.10), channel_id=1, source_target_pairs={{0,8},{1,9},{2,10},{3,11},{4,12},{5,13},{6,14},{7,15},{8,16},{9,17... | collective-permute-start | bytes 589832 | tf_op jit(solution)/shard_map/ppermute | solution.py:206
  88.3 8.1 %collective-permute-start.21 = (bf16[8,8,1024]{2,1,0:T(8,128)(2,1)S(1)}, bf16[8,8,1024]{2,1,0:T(8,128)(2,1)S(1)}, u32[]{:S(2)}, u32[]{:S(2)}) collective-permute-start(bf16[8,8,1024]{2,1,0:T(8,128)(2,1)S(1)} %get-tuple-element.18), channel_id=1, source_target_pairs={{0,9},{1,10},{2,11},{3,12},{4,13},{5,14},{6,15},{7,8},{8,17},{9,18... | collective-permute-start | bytes 393224 | tf_op jit(solution)/shard_map/ppermute | solution.py:206
  89.9 7.1 %collective-permute-start.23 = (bf16[8,8,1024]{2,1,0:T(8,128)(2,1)S(1)}, bf16[8,8,1024]{2,1,0:T(8,128)(2,1)S(1)}, u32[]{:S(2)}, u32[]{:S(2)}) collective-permute-start(bf16[8,8,1024]{2,1,0:T(8,128)(2,1)S(1)} %get-tuple-element.20), channel_id=1, source_target_pairs={{0,1},{1,2},{2,3},{3,4},{4,5},{5,6},{6,7},{7,0},{8,9},{9,10},{10,1... | collective-permute-start | bytes 393224 | tf_op jit(solution)/shard_map/ppermute | solution.py:206
  90.8 8.3 %collective-permute-start.22 = (bf16[8,8,1024]{2,1,0:T(8,128)(2,1)S(1)}, bf16[8,8,1024]{2,1,0:T(8,128)(2,1)S(1)}, u32[]{:S(2)}, u32[]{:S(2)}) collective-permute-start(bf16[8,8,1024]{2,1,0:T(8,128)(2,1)S(1)} %get-tuple-element.21), channel_id=1, source_target_pairs={{0,8},{1,9},{2,10},{3,11},{4,12},{5,13},{6,14},{7,15},{8,16},{9,17... | collective-permute-start | bytes 393224 | tf_op jit(solution)/shard_map/ppermute | solution.py:206
where the time goes:
time: 100 us; the launch traced here: 99.9 us
  waiting for transfers between devices  28.8 us (29%)
  Pallas kernels  27.9 us (28%)
  starting transfers between devices  24.3 us (24%)
  local copies, waits for them, and re-layouts  12.2 us (12%)
  other arithmetic  5.04 us (5%)
  between operations  1.68 us (2%)
    ppermute x20, waiting for transfers between devices, send(): return lax.ppermute(value, ('lat', 'lon'), pairs)  27.6 us
    pallas_call x4, Pallas kernels, fine_window(): pl.pallas_call(functools.partial(fine_kernel, masked), out_shape=(jax.Sha...  19.5 us
    ppermute x20, starting transfers between devices, send(): return lax.ppermute(value, ('lat', 'lon'), pairs)  14.4 us
    ppermute x4, starting transfers between devices, shifted(): lax.ppermute(value, axis, [(s, (s + steps) % count) for s in range(count)])  9.98 us
    pallas_call x1, Pallas kernels, coarse_window(): pl.pallas_call(functools.partial(coarse_kernel, plan), out_shape=jax.Shap...  8.37 us
    unnamed x34, local copies, waits for them, and re-layouts  5.25 us
  transfers between devices with their start and end apart: 24, of which 9 were waited for; matrix products, arithmetic and copies ran while one was open for 9% of the time, Pallas kernels for 28%

commit v1 on v0

--- a/solution.py
+++ b/solution.py
@@ -61,16 +61,64 @@
     return jnp.where(lead == other, 0.0, jnp.where(last_ref[0] > 0, NEG, 0.0))
 
 
-def fine_kernel(masked, last, x_ref, vq, vp, vu, vd, vm, out_ref, merged_ref, qkv, mixed, wide):
-    width = x_ref.shape[1]
-    x = x_ref[...].astype(F32)
+def window_blocks(i, j, rows, cols):
+    top, left = HALF + i * WIN, HALF + j * WIN
+    tall = [(0, top, 0, min(WIN, rows - top))]
+    wide = [(0, left, 0, min(WIN, cols - left))]
+    if top + WIN > rows:
+        tall.append((1, 0, HALF, HALF))
+    if left + WIN > cols:
+        wide.append((1, 0, HALF, HALF))
+    out = []
+    for below, r, to_r, count_r in tall:
+        for beside, c, to_c, count_c in wide:
+            source = ("field", "east", "south", "corner")[2 * below + beside]
+            at_c = c - HALF if source == "south" else c
+            out.append((source, r, at_c, to_r, to_c, count_r, count_c))
+    return out
+
+
+def fine_kernel(masked, first, names, blocks, last, *refs):
+    count = len(names)
+    sources = dict(zip(names, refs[:count]))
+    weights, refs = refs[count:count + 5], refs[count + 5:]
+    out_ref, merged_ref = refs[:2]
+    qkv, mixed, wide, window, sems = refs[-5:]
+    moves_in = []
+    for at, (name, r, c, to_r, to_c, nr, nc) in enumerate(blocks):
+        moves_in.append(pltpu.make_async_copy(
+            sources[name].at[pl.ds(r, nr), pl.ds(c, nc)],
+            window.at[pl.ds(to_r, nr), pl.ds(to_c, nc)], sems.at[at]))
+    for copy in moves_in:
+        copy.start()
+    loads = []
+    if first:
+        held = refs[2:7]
+        for at, (src, dst) in enumerate(zip(weights, held)):
+            loads.append(pltpu.make_async_copy(src, dst, sems.at[4 + at]))
+            loads[-1].start()
+        weights = held
+    vq, vp, vu, vd, vm = weights
+
+    def ready(at):
+        if first:
+            loads[at].wait()
+
+    for copy in moves_in:
+        copy.wait()
+    width = window.shape[2]
+    x = window[...].reshape(TOK, width).astype(F32)
     normed = norm(x)
+    ready(0)
     for part in range(3):
         cols = slice(part * width, (part + 1) * width)
         qkv[:, cols] = dot(normed, vq[:, cols]).astype(BF)
     attention(qkv, mixed, width, mask_bias(last) if masked else None)
+    ready(1)
     attended = (x + dot(mixed[...], vp[...])).astype(BF).astype(F32)
     normed = norm(attended)
+    ready(2)
+    ready(3)
     total = attended
     step = width
     for at in range(0, vu.shape[1], step):
@@ -92,78 +140,117 @@
     joined = [g - mean for g in joined]
     spread = sum(jnp.sum(g * g, axis=-1, keepdims=True) for g in joined) / count
     scale = lax.rsqrt(spread + 1e-05)
+    ready(4)
     merged = 0.0
     for i, g in enumerate(joined):
         merged = merged + dot((g * scale).astype(BF), vm[i * width:(i + 1) * width, :])
     merged_ref[...] = merged.astype(BF)
 
 
-def fine_window(x, last, weights, masked):
-    width = x.shape[-1]
+def fine_window(i, j, arrays, last, weights, masked, first):
+    rows, cols, width = arrays["field"].shape
     wide = weights[-1].shape[1]
+    blocks = window_blocks(i, j, rows, cols)
+    names = tuple(dict.fromkeys(block[0] for block in blocks))
     flops = 2 * TOK * width * (3 * width + width + 4 * width * 2) + TOK * 2 * width * wide
     size = sum(w.size * 2 for w in weights)
+    hbm = pl.BlockSpec(memory_space=pl.ANY)
     vmem = pl.BlockSpec(memory_space=pltpu.VMEM)
+    held = [jax.ShapeDtypeStruct(w.shape, BF) for w in weights] if first else []
     return pl.pallas_call(
-        functools.partial(fine_kernel, masked),
-        out_shape=(
+        functools.partial(fine_kernel, masked, first, names, blocks),
+        out_shape=[
             jax.ShapeDtypeStruct((TOK, width), BF),
             jax.ShapeDtypeStruct((TOK // 4, wide), BF),
-        ),
-        in_specs=[pl.BlockSpec(memory_space=pltpu.SMEM), vmem] + [vmem] * 5,
-        out_specs=(vmem, vmem),
+        ]
+        + held,
+        in_specs=[pl.BlockSpec(memory_space=pltpu.SMEM)] + [hbm] * len(names) + [hbm if first else vmem] * 5,
+        out_specs=[vmem] * (2 + len(held)),
         scratch_shapes=[
             pltpu.VMEM((TOK, 3 * width), BF),
             pltpu.VMEM((TOK, width), BF),
             pltpu.VMEM((width // 128, TOK, 128), F32),
+            pltpu.VMEM((WIN, WIN, width), BF),
+            pltpu.SemaphoreType.DMA((9,)),
         ],
         compiler_params=pltpu.CompilerParams(vmem_limit_bytes=24 << 20),
         cost_estimate=pl.CostEstimate(
             flops=flops, bytes_accessed=size + 3 * TOK * width * 2, transcendentals=TOK * 4 * width * 2
         ),
-        name="fine_masked" if masked else "fine_plain",
-    )(last, x, *weights)
+        name="fine_first" if first else "fine_masked" if masked else "fine_plain",
+    )(last, *[arrays[name] for name in names], *weights)
+
+
+def cut_kernel(regions, offsets, *refs):
+    count = (len(refs) - 1) // 2
+    sems = refs[-1]
+    copies = []
+    for at, (src, dst, region) in enumerate(zip(refs[:count], refs[count:-1], regions)):
+        where = []
+        for start, size in region:
+            if isinstance(start, str):
+                start = pl.multiple_of(offsets[int(start)], size)
+            where.append(pl.ds(start, size))
+        copies.append(pltpu.make_async_copy(src.at[tuple(where)], dst, sems.at[at]))
+    for copy in copies:
+        copy.start()
+    for copy in copies:
+        copy.wait()
+
+
+def cut(offsets, cuts):
+    hbm = pl.BlockSpec(memory_space=pl.ANY)
+    vmem = pl.BlockSpec(memory_space=pltpu.VMEM)
+    shapes = [tuple(size for _, size in region) for _, region in cuts]
+    return pl.pallas_call(
+        functools.partial(cut_kernel, tuple(region for _, region in cuts)),
+        out_shape=[jax.ShapeDtypeStruct(shape, BF) for shape in shapes],
+        in_specs=[pl.BlockSpec(memory_space=pltpu.SMEM)] + [hbm] * len(cuts),
+        out_specs=[vmem] * len(cuts),
+        scratch_shapes=[pltpu.SemaphoreType.DMA((len(cuts),))],
+        compiler_params=pltpu.CompilerParams(vmem_limit_bytes=8 << 20),
+        cost_estimate=pl.CostEstimate(
+            flops=0, bytes_accessed=sum(2 * int(np.prod(shape)) for shape in shapes), transcendentals=0
+        ),
+        name="cut",
+    )(offsets, *[array for array, _ in cuts])
 
 
 def coarse_kernel(plan, last, table, x_ref, *rest):
-    count = len(plan)
+    count = max(entry[0] for entry in plan) + 1
     pieces = rest[:count]
-    out_ref, xn, qkv, mixed = rest[count:]
+    out_ref, xn, qkv, mixed, proj, sem = rest[count:]
     width = x_ref.shape[1]
-    x = x_ref[...].astype(F32)
-    xn[...] = norm(x)
-
-    def project(source, target, which):
-        for group, refs, start in plan_groups(plan, pieces, which):
-            total = 0.0
-            for slot, ref, cols in refs:
-                rows = ref.shape[0]
-                if rows == width:
-                    lhs = source[...]
-                else:
-                    lhs = source[:, pl.ds(pl.multiple_of(table[2 * slot], rows), rows)]
-                total = total + dot(lhs, ref[:, cols])
-            size = total.shape[1]
-            at = pl.multiple_of(table[2 * group + 1] * size, 128)
-            target(pl.ds(at, size), total)
-
-    def keep(cols, total):
-        qkv[:, cols] = total.astype(BF)
-
-    def finish(cols, total):
-        out_ref[:, cols] = (x_ref[:, cols].astype(F32) + total).astype(BF)
-
-    project(xn, keep, 0)
+
+    def place(slot, rows, columns):
+        row = pl.multiple_of(table[2 * slot], rows)
+        column = pl.multiple_of(table[2 * slot + 1] * columns, 128)
+        return pl.ds(row, rows), pl.ds(column, columns)
+
+    copies, shards = [], {}
+    for slot, (piece, r, rows, c, columns, shard, which) in enumerate(plan):
+        part = pieces[piece].at[pl.ds(r, rows), pl.ds(c, columns)]
+        if which == 1:
+            copies.append(pltpu.make_async_copy(part, proj.at[place(slot, rows, columns)], sem.at[len(copies)]))
+        else:
+            shards.setdefault(shard, []).append((slot, part, rows, columns))
+    for copy in copies:
+        copy.start()
+    xn[...] = norm(x_ref[...].astype(F32))
+    for parts in shards.values():
+        total = 0.0
+        for slot, part, rows, columns in parts:
+            row, column = place(slot, rows, columns)
+            lhs = xn[...] if rows == width else xn[:, row]
+            total = total + dot(lhs, part[...])
+        qkv[:, column] = total.astype(BF)
     attention(qkv, mixed, width, mask_bias(last))
-    project(mixed, finish, 1)
-
-
-def plan_groups(plan, pieces, which):
-    shards = {}
-    for slot, (shard, cols) in enumerate(plan):
-        if cols[which] is not None:
-            shards.setdefault(shard, []).append((slot, pieces[slot], slice(*cols[which])))
-    return [(refs[0][0], refs, 0) for refs in shards.values()]
+    for copy in copies:
+        copy.wait()
+    step = width // 2
+    for at in range(0, width, step):
+        cols = slice(at, at + step)
+        out_ref[:, cols] = (x_ref[:, cols].astype(F32) + dot(mixed[...], proj[:, cols])).astype(BF)
 
 
 def coarse_window(x, last, table, pieces, plan):
@@ -179,6 +266,8 @@
             pltpu.VMEM((TOK, width), BF),
             pltpu.VMEM((TOK, 3 * width), BF),
             pltpu.VMEM((TOK, width), BF),
+            pltpu.VMEM((width, width), BF),
+            pltpu.SemaphoreType.DMA((sum(entry[6] for entry in plan),)),
         ],
         compiler_params=pltpu.CompilerParams(vmem_limit_bytes=24 << 20),
         cost_estimate=pl.CostEstimate(
@@ -206,42 +295,54 @@
     return lax.ppermute(value, ("lat", "lon"), pairs)
 
 
-def gather_weights(qkv_shard, proj_shard, m, n):
+def half_of(ring, la):
+    return ring.index(la) % 2
+
+
+def gather_weights(qkv_shard, proj_shard, qkv_part, proj_part, m, n):
     deep = qkv_shard.shape[0]
     a, b = qkv_shard.shape[1], proj_shard.shape[1]
-    rows = deep // 2
+    half, share = qkv_part.shape[0], proj_part.shape[0]
     places = n // 2
     along = moves(line_ring(places))
     ring = line_ring(m)
     across = moves(ring)
-    side = jnp.asarray(np.array([ring.index(la) % 2 for la in range(m)], np.int32))[lax.axis_index("lat")]
-    part = jnp.concatenate(
-        [lax.dynamic_slice_in_dim(w, side * rows, rows, 0) for w in (qkv_shard, proj_shard)], axis=1
-    )
-    pieces = [qkv_shard, proj_shard]
-    plan = [("own", ((0, a), None)), ("own", (None, (0, b)))]
+    turn = lambda lo: 1 - 2 * (lo % 2)
+    origin = lambda lo, s: 2 * along(lo // 2, s) + lo % 2
 
     def swap(value):
         return send(value, m, n, lambda la, lo: (la, lo ^ 1))
 
-    pieces += [swap(qkv_shard), swap(proj_shard)]
-    plan += [("peer", ((0, a), None)), ("peer", (None, (0, b)))]
-    whole = ((0, a), (a, a + b))
+    pieces, plan, spots = [], [], []
+
+    def add(value, which, spot, columns, cuts):
+        for twin in range(2):
+            for r, rows, key in cuts:
+                plan.append((len(pieces), r, rows, 0, columns, (twin, key), which))
+                spots.append((twin, spot, key))
+            pieces.append(swap(value) if twin else value)
+
+    add(qkv_shard, 0, lambda la, lo, key: (0, lo), a, [(0, deep, 0)])
+    add(proj_shard, 1, lambda la, lo, key: (0, lo), b, [(0, deep, 0)])
+    part = qkv_part
+    shares = []
     for s in range(1, places):
-        part = send(part, m, n, lambda la, lo: (la, 2 * along(lo // 2, 1) + lo % 2))
-        other = send(part, m, n, lambda la, lo: (across(la, 1 - 2 * (lo % 2)), lo))
-        pieces += [part, other, swap(part), swap(other)]
-        plan += [(s, whole), (s, whole), (-s, whole), (-s, whole)]
-    tables = np.zeros((m, n, len(pieces), 2), np.int32)
+        part = send(part, m, n, lambda la, lo: (la, origin(lo, 1)))
+        shares.append(send(proj_part, m, n, lambda la, lo: (la, origin(lo, s))))
+        other = send(part, m, n, lambda la, lo: (across(la, turn(lo)), lo))
+        for value, flip in ((part, 0), (other, 1)):
+            spot = lambda la, lo, key, flip=flip: ((half_of(ring, la) ^ flip) * half, origin(lo, -key))
+            add(value, 0, spot, a, [(0, half, s)])
+    plane = jnp.concatenate(shares, axis=0)
+    for k in range(m):
+        if k > 0:
+            plane = send(plane, m, n, lambda la, lo: (across(la, turn(lo)), lo))
+        spot = lambda la, lo, key, k=k: (across(la, -k * turn(lo)) * share, origin(lo, -key))
+        add(plane, 1, spot, b, [((s - 1) * share, share, s) for s in range(1, places)])
+    tables = np.zeros((m, n, len(spots), 2), np.int32)
     for la in range(m):
         for lo in range(n):
-            mine = ring.index(la) % 2
-            out = [(0, lo), (0, lo), (0, lo ^ 1), (0, lo ^ 1)]
-            for s in range(1, places):
-                for who in (lo, lo ^ 1):
-                    lon = 2 * along(who // 2, -s) + who % 2
-                    out += [(mine * rows, lon), ((1 - mine) * rows, lon)]
-            tables[la, lo] = out
+            tables[la, lo] = [spot(la, lo ^ twin, key) for twin, spot, key in spots]
     table = jnp.asarray(tables.reshape(m * n, -1))[lax.axis_index("lat") * n + lax.axis_index("lon")]
     return pieces, tuple(plan), table
 
@@ -260,34 +361,42 @@
     last = (lax.axis_index("lat") == m - 1).astype(jnp.int32).reshape(1)
     fine_weights = (qkv_fine, proj_fine, up_fine, down_fine, merge_weight)
 
-    east = shifted(field[:, :HALF], "lon", -1)
-    widened = jnp.concatenate([field[:HALF, HALF:], east[:HALF]], axis=1)
-    south = shifted(widened, "lat", -1)
-    a, b = qkv_coarse.shape[1], proj_coarse.shape[1]
-    if a % 128 == 0 and b % 128 == 0 and n % 2 == 0 and m % 2 == 0:
-        pieces, plan, table = gather_weights(qkv_coarse, proj_coarse, m, n)
+    deep, a = qkv_coarse.shape
+    b = proj_coarse.shape[1]
+    direct = a % 128 == 0 and b % 128 == 0 and n % 2 == 0 and m % 2 == 0 and deep % (16 * m) == 0
+    cuts = [
+        (field, ((0, rows), (0, HALF), (0, width))),
+        (field, ((0, HALF), (HALF, cols - HALF), (0, width))),
+        (field, ((0, HALF), (0, HALF), (0, width))),
+    ]
+    lat = lax.axis_index("lat")
+    ring = line_ring(m)
+    offsets = jnp.asarray(
+        np.array([(half_of(ring, la) * (deep // 2), la * (deep // m)) for la in range(m)], np.int32)
+    )[lat]
+    if direct:
+        cuts += [(qkv_coarse, (("0", deep // 2), (0, a))), (proj_coarse, (("1", deep // m), (0, b)))]
+    parts = cut(offsets, cuts)
+    up = lambda la: (la - 1) % m
+    left = lambda lo: (lo - 1) % n
+    arrays = {"field": field}
+    arrays["east"] = send(parts[0], m, n, lambda la, lo: (la, left(lo)))
+    arrays["south"] = send(parts[1], m, n, lambda la, lo: (up(la), lo))
+    arrays["corner"] = send(parts[2], m, n, lambda la, lo: (up(la), left(lo)))
+    if direct:
+        pieces, plan, table = gather_weights(qkv_coarse, proj_coarse, parts[3], parts[4], m, n)
     else:
         pieces = [lax.all_gather(w, "lon", axis=1, tiled=True) for w in (qkv_coarse, proj_coarse)]
-        plan = ((0, ((0, a * n), None)), (0, (None, (0, b * n))))
+        plan = ((0, 0, deep, 0, a * n, 0, 0), (1, 0, deep, 0, b * n, 0, 1))
         table = jnp.zeros((4,), jnp.int32)
 
-    def window(i, j):
-        top, left = HALF + i * WIN, HALF + j * WIN
-        if i < wr - 1:
-            block = field[top:top + WIN, left:left + WIN]
-            if j == wc - 1:
-                block = jnp.concatenate([block, east[top:top + WIN]], axis=1)
-        else:
-            block = field[top:, left:left + WIN]
-            if j == wc - 1:
-                block = jnp.concatenate([block, east[top:]], axis=1)
-            block = jnp.concatenate([block, south[:, j * WIN:(j + 1) * WIN]], axis=0)
-        return block.reshape(TOK, width)
-
     fine, merged = {}, {}
+    held = fine_weights
     for i in range(wr):
         for j in range(wc):
-            out, mer = fine_window(window(i, j), last, fine_weights, i == wr - 1)
+            first = i == 0 and j == 0
+            out, mer, *kept = fine_window(i, j, arrays, last, held, i == wr - 1, first)
+            held = kept if first else held
             fine[i, j] = out.reshape(WIN, WIN, width)
             merged[i, j] = mer.reshape(HALF, HALF, wide)
 
@@ -296,10 +405,12 @@
             [jnp.concatenate([parts[i, j] for j in range(wc)], axis=1) for i in range(wr)], axis=0
         )
 
-    coarse = lay(merged)
-    below = shifted(coarse[:QUART], "lat", -1)
-    tall = jnp.concatenate([coarse[QUART:], below], axis=0)
-    beside = shifted(tall[:, :QUART], "lon", -1)
+    top = jnp.concatenate([merged[0, j][:QUART] for j in range(wc)], axis=1)
+    below = shifted(top, "lat", -1)
+    side = jnp.concatenate([merged[i, 0][:, :QUART] for i in range(wr)], axis=0)
+    side = jnp.concatenate([side[QUART:], below[:, :QUART]], axis=0)
+    beside = shifted(side, "lon", -1)
+    tall = jnp.concatenate([lay(merged)[QUART:], below], axis=0)
     coarse = jnp.concatenate([tall[:, QUART:], beside], axis=1)
 
     def back(values):

time: 100 us -> 131 us (1.31)
  local copies, waits for them, and re-layouts: 12.2 us -> 30.4 us
  starting transfers between devices: 24.3 us -> 40.5 us
  waiting for transfers between devices: 28.8 us -> 23.2 us
  Pallas kernels: 27.9 us -> 32 us
  other arithmetic: 5.04 us -> 2.31 us
    ppermute x20 -> x33, starting transfers between devices: 14.4 us -> 38.5 us  [send(): return lax.ppermute(value, ('lat', 'lon'), pairs)]
    unnamed x34 -> x112, local copies, waits for them, and re-layouts: 5.25 us -> 28.1 us
    ppermute x4 -> x2, starting transfers between devices: 9.98 us -> 2 us  [shifted(): lax.ppermute(value, axis, [(s, (s + steps) % count) for s in range(count)])]
    ppermute x20 -> x33, waiting for transfers between devices: 27.6 us -> 20.3 us  [send(): return lax.ppermute(value, ('lat', 'lon'), pairs)]
    pallas_call x4 -> x5, Pallas kernels: 19.5 us -> 22.7 us  [the longest x4 21.2 us: fine_window(): pl.pallas_call(functools.partial(fine_kernel, masked, first, names, block...]
    dynamic_slice x3 -> x0, local copies, waits for them, and re-layouts: 3.2 us -> none  [the longest x2 1.96 us: gather_weights(): lax.dynamic_slice_in_dim(w, side * rows, rows, 0)]
    slice x10 -> x4, local copies, waits for them, and re-layouts: 3.01 us -> 0.06 us  [the longest x2 0.04 us: whole_body(): side = jnp.concatenate([merged[i, 0][:, :QUART] for i in range(wr)], axis=0)]
    concatenate x5 -> x2, other arithmetic: 1.93 us -> 0.11 us  [the longest x1 0.1 us: whole_body(): side = jnp.concatenate([side[QUART:], below[:, :QUART]], axis=0)]
  transfers between devices with their start and end apart: 24 -> 35, of which waited for: 9 -> 9; matrix products, arithmetic and copies ran while one was open for 9% -> 4% of each run, Pallas kernels for 28% -> 25%
where the time goes in v1:
time: 131 us; the launch traced here: 130 us
  starting transfers between devices  40.5 us (31%)
  Pallas kernels  32 us (24%)
  local copies, waits for them, and re-layouts  30.4 us (23%)
  waiting for transfers between devices  23.2 us (18%)
  other arithmetic  2.31 us (2%)
    ppermute x33, starting transfers between devices, send(): return lax.ppermute(value, ('lat', 'lon'), pairs)  38.5 us
    unnamed x112, local copies, waits for them, and re-layouts  28.1 us
    pallas_call x4, Pallas kernels, fine_window(): pl.pallas_call(functools.partial(fine_kernel, masked, first, names, block...  21.2 us
    ppermute x33, waiting for transfers between devices, send(): return lax.ppermute(value, ('lat', 'lon'), pairs)  20.3 us
    pallas_call x1, Pallas kernels, coarse_window(): pl.pallas_call(functools.partial(coarse_kernel, plan), out_shape=jax.Shap...  9.25 us
    ppermute x2, waiting for transfers between devices, shifted(): lax.ppermute(value, axis, [(s, (s + steps) % count) for s in range(count)])  2.85 us
  transfers between devices with their start and end apart: 35, of which 9 were waited for; matrix products, arithmetic and copies ran while one was open for 4% of the time, Pallas kernels for 25%

profile of v1, /device:TPU:0, one launch (start us, length us, event | category | flops | bytes accessed | tf_op | source)
XLA Modules:
  0.0 129.7 jit_solution(2781088011475730890)
XLA Ops:
  2.0 1.2 copy-done
  3.2 1.1 copy-done.11
  4.3 0.9 copy-done.16
  5.3 1.6 %cut.1 = (bf16[32,8,512]{2,1,0:T(8,128)(2,1)S(1)}, bf16[8,24,512]{2,1,0:T(8,128)(2,1)S(1)}, bf16[8,8,512]{2,1,0:T(8,128)(2,1)S(1)}, bf16[512,384]{1,0:T(8,128)(2,1)S(1)}, bf16[256,128]{1,0:T(8,128)(2,1)}) custom-call(s32[2]{0:T(128)S(1)} %dynamic-slice_bitcast_fusion.1.offsets, bf16[32,32,512]{2,1,0:T(8,128)(2,1)S(1)} %copy-done, ...), custom_call_target="tpu_custom_call" | custom-call | bytes 983040 | tf_op jit(solution)/shard_map/cut/pallas_call | solution.py:205
  8.9 3.0 %collective-permute-start.22 = (bf16[256,128]{1,0:T(8,128)(2,1)}, bf16[256,128]{1,0:T(8,128)(2,1)}, u32[]{:S(2)}, u32[]{:S(2)}) collective-permute-start(bf16[256,128]{1,0:T(8,128)(2,1)} %get-tuple-element.37), channel_id=1, source_target_pairs={{0,2},{1,3},{2,6},{3,7},{4,0},{5,1},{6,4},{7,5},{8,10},{9,11},{10,... | collective-permute-start | bytes 196616 | tf_op jit(solution)/shard_map/ppermute | solution.py:295
  11.9 2.5 %collective-permute-start.23 = (bf16[256,128]{1,0:T(8,128)(2,1)}, bf16[256,128]{1,0:T(8,128)(2,1)}, u32[]{:S(2)}, u32[]{:S(2)}) collective-permute-start(bf16[256,128]{1,0:T(8,128)(2,1)} %get-tuple-element.37), channel_id=1, source_target_pairs={{0,6},{1,7},{2,4},{3,5},{4,2},{5,3},{6,0},{7,1},{8,14},{9,15},{10,... | collective-permute-start | bytes 196616 | tf_op jit(solution)/shard_map/ppermute | solution.py:295
  14.4 1.6 %collective-permute-start.24 = (bf16[256,128]{1,0:T(8,128)(2,1)}, bf16[256,128]{1,0:T(8,128)(2,1)}, u32[]{:S(2)}, u32[]{:S(2)}) collective-permute-start(bf16[256,128]{1,0:T(8,128)(2,1)} %get-tuple-element.37), channel_id=1, source_target_pairs={{0,4},{1,5},{2,0},{3,1},{4,6},{5,7},{6,2},{7,3},{8,12},{9,13},{10,... | collective-permute-start | bytes 196616 | tf_op jit(solution)/shard_map/ppermute | solution.py:295
  15.9 2.2 %copy-done.10 = bf16[2048,1024]{1,0:T(8,128)(2,1)S(1)} copy-done((bf16[2048,1024]{1,0:T(8,128)(2,1)S(1)}, bf16[2048,1024]{1,0:T(8,128)(2,1)}, u32[]{:S(2)}) %copy-start.10) | copy-done | bytes 4194328
  18.1 1.6 %copy-done.13 = bf16[512,2048]{1,0:T(8,128)(2,1)S(1)} copy-done((bf16[512,2048]{1,0:T(8,128)(2,1)S(1)}, bf16[512,2048]{1,0:T(8,128)(2,1)}, u32[]{:S(2)}) %copy-start.13) | copy-done | bytes 2097176
  19.7 1.6 %copy-done.14 = bf16[2048,512]{1,0:T(8,128)(2,1)S(1)} copy-done((bf16[2048,512]{1,0:T(8,128)(2,1)S(1)}, bf16[2048,512]{1,0:T(8,128)(2,1)}, u32[]{:S(2)}) %copy-start.14) | copy-done | bytes 2097176
  21.3 1.4 %copy-done.15 = bf16[512,1536]{1,0:T(8,128)(2,1)S(1)} copy-done((bf16[512,1536]{1,0:T(8,128)(2,1)S(1)}, bf16[512,1536]{1,0:T(8,128)(2,1)}, u32[]{:S(2)}) %copy-start.15) | copy-done | bytes 1572888
  22.7 1.0 copy-done.26
  23.8 6.0 %fine_first.1 = (bf16[256,512]{1,0:T(8,128)(2,1)S(1)}, bf16[64,1024]{1,0:T(8,128)(2,1)S(1)}, bf16[512,1536]{1,0:T(8,128)(2,1)S(1)}, bf16[512,512]{1,0:T(8,128)(2...) custom-call(s32[1]{0:T(128)} %bitcast.last, ...), custom_call_target="tpu_custom_call" | custom-call | flops 1879048192 | bytes 11272192 | tf_op jit(solution)/shard_map/fine_first/pallas_call | solution.py:160
  30.6 0.9 constant_dynamic-update-slice_fusion.2
  32.4 0.9 constant_dynamic-update-slice_fusion.1
  33.3 2.5 %collective-permute-start.1 = (bf16[8,24,512]{2,1,0:T(8,128)(2,1)S(1)}, bf16[8,24,512]{2,1,0:T(8,128)(2,1)S(1)}, u32[]{:S(2)}, u32[]{:S(2)}) collective-permute-start(bf16[8,24,512]{2,1,0:T(8,128)(2,1)S(1)} %copy-done.48), channel_id=1, source_target_pairs={{0,24},{1,25},{2,26},{3,27},{4,28},{5,29},{6,30},{7,31},{8,0},{9,1... | collective-permute-start | bytes 589832 | tf_op jit(solution)/shard_map/ppermute | solution.py:295
  36.7 5.2 %collective-permute-start.2 = (bf16[8,8,512]{2,1,0:T(8,128)(2,1)S(1)}, bf16[8,8,512]{2,1,0:T(8,128)(2,1)S(1)}, u32[]{:S(2)}, u32[]{:S(2)}) collective-permute-start(bf16[8,8,512]{2,1,0:T(8,128)(2,1)S(1)} %copy-done.50), channel_id=1, source_target_pairs={{0,31},{1,24},{2,25},{3,26},{4,27},{5,28},{6,29},{7,30},{8,7},{9,0... | collective-permute-start | bytes 196616 | tf_op jit(solution)/shard_map/ppermute | solution.py:295
  41.9 5.0 %fine_plain.1 = (bf16[256,512]{1,0:T(8,128)(2,1)S(1)}, bf16[64,1024]{1,0:T(8,128)(2,1)S(1)}) custom-call(s32[1]{0:T(128)} %bitcast.last, bf16[32,32,512]{2,1,0:T(8,128)(2,1)S(1)} %copy-done.1, bf16[32,8,512]{2,1,0:T(8,128)(2,1)S(1)} %collective-permute-done.refs_1_, bf16[512,1536]{1,0:T(8,128)(2,1)S(1)} %get-tuple-element.23.refs_4_.refs_2_, ...), custom_call_target="tpu_custom_call" | custom-call | flops 1879048192 | bytes 11272192 | tf_op jit(solution)/shard_map/fine_plain/pallas_call | solution.py:160
  47.0 6.0 %collective-permute-start.14 = (bf16[512,384]{1,0:T(8,128)(2,1)}, bf16[512,384]{1,0:T(8,128)(2,1)}, u32[]{:S(2)}, u32[]{:S(2)}) collective-permute-start(bf16[512,384]{1,0:T(8,128)(2,1)} %collective-permute-done.10.rest_4_), channel_id=1, source_target_pairs={{0,2},{1,3},{2,6},{3,7},{4,0},{5,1},{6,4},{7,5},{8,10},{9,11},{10,... | collective-permute-start | bytes 1179656 | tf_op jit(solution)/shard_map/ppermute | solution.py:295
  53.1 2.0 %collective-permute-start.6 = (bf16[4,16,1024]{2,1,0:T(8,128)(2,1)S(1)}, bf16[4,16,1024]{2,1,0:T(8,128)(2,1)S(1)}, u32[]{:S(2)}, u32[]{:S(2)}) collective-permute-start(bf16[4,16,1024]{2,1,0:T(8,128)(2,1)S(1)} %pad_maximum_fusion.7), channel_id=1, source_target_pairs={{0,24},{8,0},{16,8},{24,16},{1,25},{9,1},{17,9},{25,17},{2,26},{10... | collective-permute-start | bytes 393224 | tf_op jit(solution)/shard_map/ppermute | solution.py:352
  55.1 3.6 %collective-permute-done.26.rest_18_ = bf16[768,128]{1,0:T(8,128)(2,1)S(1)} collective-permute-done((bf16[768,128]{1,0:T(8,128)(2,1)S(1)}, bf16[768,128]{1,0:T(8,128)(2,1)S(1)}, u32[]{:S(2)}, u32[]{:S(2)}) %collective-permute-start.26) | collective-permute-done | bytes 196640 | tf_op jit(solution)/shard_map/ppermute | solution.py:295
  59.5 1.9 %collective-permute-start.18 = (bf16[512,384]{1,0:T(8,128)(2,1)}, bf16[512,384]{1,0:T(8,128)(2,1)}, u32[]{:S(2)}, u32[]{:S(2)}) collective-permute-start(bf16[512,384]{1,0:T(8,128)(2,1)} %collective-permute-done.14.rest_8_), channel_id=1, source_target_pairs={{0,2},{1,3},{2,6},{3,7},{4,0},{5,1},{6,4},{7,5},{8,10},{9,11},{10,... | collective-permute-start | bytes 1179656 | tf_op jit(solution)/shard_map/ppermute | solution.py:295
  61.4 5.1 %fine_masked.3 = (bf16[256,512]{1,0:T(8,128)(2,1)S(1)}, bf16[64,1024]{1,0:T(8,128)(2,1)S(1)}) custom-call(s32[1]{0:T(128)} %bitcast.last, bf16[32,32,512]{2,1,0:T(8,128)(2,1)S(1)} %copy-done.1, bf16[8,24,512]{2,1,0:T(8,128)(2,1)S(1)} %collective-permute-done.1.refs_2_.refs_1_, bf16[512,1536]{1,0:T(8,128)(2,1)S(1)} %get-tuple-element.23.refs_4_.refs_2_, ...), custom_call_target="tpu_custom_call" | custom-call | flops 1879048192 | bytes 11272192 | tf_op jit(solution)/shard_map/fine_masked/pallas_call | solution.py:160
  67.8 1.5 %collective-permute-start.30 = (bf16[768,128]{1,0:T(8,128)(2,1)S(1)}, bf16[768,128]{1,0:T(8,128)(2,1)}, u32[]{:S(2)}, u32[]{:S(2)}) collective-permute-start(bf16[768,128]{1,0:T(8,128)(2,1)S(1)} %collective-permute-done.28.rest_20_), channel_id=1, source_target_pairs={{0,8},{1,17},{2,10},{3,19},{4,12},{5,21},{6,14},{7,23},{8,24},{9,1... | collective-permute-start | bytes 589832 | tf_op jit(solution)/shard_map/ppermute | solution.py:295
  70.1 2.5 %collective-permute-done.7 = bf16[16,4,1024]{2,1,0:T(4,128)(2,1)S(1)} collective-permute-done((bf16[16,4,1024]{2,1,0:T(4,128)(2,1)S(1)}, bf16[16,4,1024]{2,1,0:T(4,128)(2,1)S(1)}, u32[]{:S(2)}, u32[]{:S(2)}) %collective-permute-start.7) | collective-permute-done | bytes 131104 | tf_op jit(solution)/shard_map/ppermute | solution.py:352
  72.6 1.6 %collective-permute-start.11 = (bf16[512,384]{1,0:T(8,128)(2,1)}, bf16[512,384]{1,0:T(8,128)(2,1)}, u32[]{:S(2)}, u32[]{:S(2)}) collective-permute-start(bf16[512,384]{1,0:T(8,128)(2,1)} %collective-permute-done.10.rest_4_), channel_id=1, source_target_pairs={{0,1},{1,0},{2,3},{3,2},{4,5},{5,4},{6,7},{7,6},{8,9},{9,8},{10,11... | collective-permute-start | bytes 1179656 | tf_op jit(solution)/shard_map/ppermute | solution.py:295
  74.9 0.9 collective-permute-start.12
  75.8 1.5 %collective-permute-start.16 = (bf16[512,384]{1,0:T(8,128)(2,1)}, bf16[512,384]{1,0:T(8,128)(2,1)}, u32[]{:S(2)}, u32[]{:S(2)}) collective-permute-start(bf16[512,384]{1,0:T(8,128)(2,1)} %collective-permute-done.14.rest_8_), channel_id=1, source_target_pairs={{0,8},{1,17},{2,10},{3,19},{4,12},{5,21},{6,14},{7,23},{8,24},{9,1... | collective-permute-start | bytes 1179656 | tf_op jit(solution)/shard_map/ppermute | solution.py:295
  77.3 1.1 collective-permute-start.20
  79.7 3.3 %collective-permute-done.12.rest_6_ = bf16[512,384]{1,0:T(8,128)(2,1)} collective-permute-done((bf16[512,384]{1,0:T(8,128)(2,1)}, bf16[512,384]{1,0:T(8,128)(2,1)}, u32[]{:S(2)}, u32[]{:S(2)}) %collective-permute-start.12) | collective-permute-done | bytes 393248 | tf_op jit(solution)/shard_map/ppermute | solution.py:295
  83.5 3.7 %collective-permute-done.16.rest_10_ = bf16[512,384]{1,0:T(8,128)(2,1)} collective-permute-done((bf16[512,384]{1,0:T(8,128)(2,1)}, bf16[512,384]{1,0:T(8,128)(2,1)}, u32[]{:S(2)}, u32[]{:S(2)}) %collective-permute-start.16) | collective-permute-done | bytes 393248 | tf_op jit(solution)/shard_map/ppermute | solution.py:295
  87.2 4.2 %collective-permute-done.20.rest_14_ = bf16[512,384]{1,0:T(8,128)(2,1)} collective-permute-done((bf16[512,384]{1,0:T(8,128)(2,1)}, bf16[512,384]{1,0:T(8,128)(2,1)}, u32[]{:S(2)}, u32[]{:S(2)}) %collective-permute-start.20) | collective-permute-done | bytes 393248 | tf_op jit(solution)/shard_map/ppermute | solution.py:295
  91.5 2.2 %copy-done.3 = bf16[2048,1024]{1,0:T(8,128)(2,1)S(1)} copy-done((bf16[2048,1024]{1,0:T(8,128)(2,1)S(1)}, bf16[2048,1024]{1,0:T(8,128)(2,1)}, u32[]{:S(2)}) %copy-start.3) | copy-done | bytes 4194328
  93.6 1.6 %copy-done.5 = bf16[2048,512]{1,0:T(8,128)(2,1)S(1)} copy-done((bf16[2048,512]{1,0:T(8,128)(2,1)S(1)}, bf16[2048,512]{1,0:T(8,128)(2,1)}, u32[]{:S(2)}) %copy-start.5) | copy-done | bytes 2097176
  95.2 1.4 %copy-done.7 = bf16[512,1536]{1,0:T(8,128)(2,1)S(1)} copy-done((bf16[512,1536]{1,0:T(8,128)(2,1)S(1)}, bf16[512,1536]{1,0:T(8,128)(2,1)}, u32[]{:S(2)}) %copy-start.7) | copy-done | bytes 1572888
  96.6 1.0 copy-done.9
  97.7 0.9 copy-done.23
  98.6 0.9 copy-done.25
  100.4 5.1 %fine_masked.2 = (bf16[256,512]{1,0:T(8,128)(2,1)S(1)}, bf16[64,1024]{1,0:T(8,128)(2,1)S(1)}) custom-call(s32[1]{0:T(128)} %bitcast.last, bf16[32,32,512]{2,1,0:T(8,128)(2,1)S(1)} %copy-done.1, bf16[32,8,512]{2,1,0:T(8,128)(2,1)S(1)} %copy-done.23, bf16[8,24,512]{2,1,0:T(8,128)(2,1)S(1)} %copy-done.25, bf16[8,8,512]{2,1,0:T(8,128)(2,1)S(1)} %copy-done.44, ...), custom_call_target="tpu_custom_call" | custom-call | flops 1879048192 | bytes 11272192 | tf_op jit(solution)/shard_map/fine_masked/pallas_call | solution.py:160
  107.3 0.9 collective-permute-start.4
  108.2 1.4 %collective-permute-start.3 = (bf16[8,8,512]{2,1,0:T(8,128)(2,1)S(1)}, bf16[8,8,512]{2,1,0:T(8,128)(2,1)S(1)}, u32[]{:S(2)}, u32[]{:S(2)}) collective-permute-start(bf16[8,8,512]{2,1,0:T(8,128)(2,1)S(1)} %slice.72), channel_id=1, source_target_pairs={{0,9},{1,10},{2,11},{3,12},{4,13},{5,14},{6,15},{7,8},{8,17},{9,18... | collective-permute-start | bytes 196616 | tf_op jit(solution)/shard_map/ppermute | solution.py:295
  109.8 9.3 %coarse.1 = bf16[256,1024]{1,0:T(8,128)(2,1)S(1)} custom-call(s32[1]{0:T(128)} %bitcast.last, s32[80]{0:T(128)S(1)} %dynamic-slice_bitcast_fusion.table, bf16[256,1024]{1,0:T(8,128)(2,1)S(1)} %bitcast.26, bf16[1024,384]{1,0:T(8,128)(2,1)S(1)} %copy-done.12, bf16[1024,384]{1,0:T(8,128)(2,1)} %collective-permute-done.8.rest_1_, ...), custom_call_target="tpu_custom_call" | custom-call | flops 2147483648 | bytes 8388608 | tf_op jit(solution)/shard_map/coarse/pallas_call | solution.py:260
  119.3 1.4 %collective-permute-start.33 = (bf16[8,8,1024]{2,1,0:T(8,128)(2,1)S(1)}, bf16[8,8,1024]{2,1,0:T(8,128)(2,1)S(1)}, u32[]{:S(2)}, u32[]{:S(2)}) collective-permute-start(bf16[8,8,1024]{2,1,0:T(8,128)(2,1)S(1)} %get-tuple-element.41), channel_id=1, source_target_pairs={{0,8},{1,9},{2,10},{3,11},{4,12},{5,13},{6,14},{7,15},{8,16},{9,17... | collective-permute-start | bytes 393224 | tf_op jit(solution)/shard_map/ppermute | solution.py:295
  120.7 1.6 %collective-permute-start.32 = (bf16[8,8,1024]{2,1,0:T(8,128)(2,1)S(1)}, bf16[8,8,1024]{2,1,0:T(8,128)(2,1)S(1)}, u32[]{:S(2)}, u32[]{:S(2)}) collective-permute-start(bf16[8,8,1024]{2,1,0:T(8,128)(2,1)S(1)} %get-tuple-element.38), channel_id=1, source_target_pairs={{0,9},{1,10},{2,11},{3,12},{4,13},{5,14},{6,15},{7,8},{8,17},{9,18... | collective-permute-start | bytes 393224 | tf_op jit(solution)/shard_map/ppermute | solution.py:295
  122.3 1.1 fusion.2
  123.4 1.9 %collective-permute-done.34 = bf16[8,8,1024]{2,1,0:T(8,128)(2,1)S(1)} collective-permute-done((bf16[8,8,1024]{2,1,0:T(8,128)(2,1)S(1)}, bf16[8,8,1024]{2,1,0:T(8,128)(2,1)S(1)}, u32[]{:S(2)}, u32[]{:S(2)}) %collective-permute-start.34) | collective-permute-done | bytes 131104 | tf_op jit(solution)/shard_map/ppermute | solution.py:295
  125.4 1.1 collective-permute-done.33
  126.4 2.4 %collective-permute-done.32 = bf16[8,8,1024]{2,1,0:T(8,128)(2,1)S(1)} collective-permute-done((bf16[8,8,1024]{2,1,0:T(8,128)(2,1)S(1)}, bf16[8,8,1024]{2,1,0:T(8,128)(2,1)S(1)}, u32[]{:S(2)}, u32[]{:S(2)}) %collective-permute-start.32) | collective-permute-done | bytes 131104 | tf_op jit(solution)/shard_map/ppermute | solution.py:295
  (156 shorter events, 14.8 us)
Async XLA Ops:
  0.6 77.9 %collective-permute-start.8 = (bf16[1024,384]{1,0:T(8,128)(2,1)}, bf16[1024,384]{1,0:T(8,128)(2,1)}, u32[]{:S(2)}, u32[]{:S(2)}) collective-permute-start(bf16[1024,384]{1,0:T(8,128)(2,1)} %rest_0_.1), channel_id=1, source_target_pairs={{0,1},{1,0},{2,3},{3,2},{4,5},{5,4},{6,7},{7,6},{8,9},{9,8},{10,11... | collective-permute-start | bytes 2359304 | tf_op jit(solution)/shard_map/ppermute | solution.py:295
  1.2 57.6 %collective-permute-start.9 = (bf16[1024,128]{1,0:T(8,128)(2,1)}, bf16[1024,128]{1,0:T(8,128)(2,1)}, u32[]{:S(2)}, u32[]{:S(2)}) collective-permute-start(bf16[1024,128]{1,0:T(8,128)(2,1)} %rest_2_.1), channel_id=1, source_target_pairs={{0,1},{1,0},{2,3},{3,2},{4,5},{5,4},{6,7},{7,6},{8,9},{9,8},{10,11... | collective-permute-start | bytes 786440 | tf_op jit(solution)/shard_map/ppermute | solution.py:295
  5.3 10.7 %copy-start.1 = (bf16[32,32,512]{2,1,0:T(8,128)(2,1)S(1)}, bf16[32,32,512]{2,1,0:T(8,128)(2,1)}, u32[]{:S(2)}) copy-start(bf16[32,32,512]{2,1,0:T(8,128)(2,1)} %refs_0_.9) | copy-start | bytes 3145732
  8.9 21.6 %collective-permute-start.22 = (bf16[256,128]{1,0:T(8,128)(2,1)}, bf16[256,128]{1,0:T(8,128)(2,1)}, u32[]{:S(2)}, u32[]{:S(2)}) collective-permute-start(bf16[256,128]{1,0:T(8,128)(2,1)} %get-tuple-element.37), channel_id=1, source_target_pairs={{0,2},{1,3},{2,6},{3,7},{4,0},{5,1},{6,4},{7,5},{8,10},{9,11},{10,... | collective-permute-start | bytes 196616 | tf_op jit(solution)/shard_map/ppermute | solution.py:295
  11.9 19.6 %collective-permute-start.23 = (bf16[256,128]{1,0:T(8,128)(2,1)}, bf16[256,128]{1,0:T(8,128)(2,1)}, u32[]{:S(2)}, u32[]{:S(2)}) collective-permute-start(bf16[256,128]{1,0:T(8,128)(2,1)} %get-tuple-element.37), channel_id=1, source_target_pairs={{0,6},{1,7},{2,4},{3,5},{4,2},{5,3},{6,0},{7,1},{8,14},{9,15},{10,... | collective-permute-start | bytes 196616 | tf_op jit(solution)/shard_map/ppermute | solution.py:295
  14.4 19.0 %collective-permute-start.24 = (bf16[256,128]{1,0:T(8,128)(2,1)}, bf16[256,128]{1,0:T(8,128)(2,1)}, u32[]{:S(2)}, u32[]{:S(2)}) collective-permute-start(bf16[256,128]{1,0:T(8,128)(2,1)} %get-tuple-element.37), channel_id=1, source_target_pairs={{0,4},{1,5},{2,0},{3,1},{4,6},{5,7},{6,2},{7,3},{8,12},{9,13},{10,... | collective-permute-start | bytes 196616 | tf_op jit(solution)/shard_map/ppermute | solution.py:295
  23.8 7.7 %copy-start.46 = (bf16[512,384]{1,0:T(8,128)(2,1)S(1)}, bf16[512,384]{1,0:T(8,128)(2,1)}, u32[]{:S(2)}) copy-start(bf16[512,384]{1,0:T(8,128)(2,1)} %copy-done.45) | copy-start | bytes 1179652
  23.8 9.6 %copy-start.48 = (bf16[8,24,512]{2,1,0:T(8,128)(2,1)S(1)}, bf16[8,24,512]{2,1,0:T(8,128)(2,1)}, u32[]{:S(2)}) copy-start(bf16[8,24,512]{2,1,0:T(8,128)(2,1)} %copy-done.47) | copy-start | bytes 589828
  23.8 13.0 %copy-start.50 = (bf16[8,8,512]{2,1,0:T(8,128)(2,1)S(1)}, bf16[8,8,512]{2,1,0:T(8,128)(2,1)}, u32[]{:S(2)}) copy-start(bf16[8,8,512]{2,1,0:T(8,128)(2,1)} %copy-done.49) | copy-start | bytes 196612
  30.5 30.9 %copy-start.2 = (bf16[2048,1024]{1,0:T(8,128)(2,1)}, bf16[2048,1024]{1,0:T(8,128)(2,1)S(1)}, u32[]{:S(2)}) copy-start(bf16[2048,1024]{1,0:T(8,128)(2,1)S(1)} %get-tuple-element.27.refs_8_.refs_6_) | copy-start | bytes 12582916
  30.5 30.9 %copy-start.4 = (bf16[2048,512]{1,0:T(8,128)(2,1)}, bf16[2048,512]{1,0:T(8,128)(2,1)S(1)}, u32[]{:S(2)}) copy-start(bf16[2048,512]{1,0:T(8,128)(2,1)S(1)} %get-tuple-element.26.refs_7_.refs_5_) | copy-start | bytes 6291460
  30.5 30.9 %copy-start.6 = (bf16[512,1536]{1,0:T(8,128)(2,1)}, bf16[512,1536]{1,0:T(8,128)(2,1)S(1)}, u32[]{:S(2)}) copy-start(bf16[512,1536]{1,0:T(8,128)(2,1)S(1)} %get-tuple-element.23.refs_4_.refs_2_) | copy-start | bytes 4718596
  30.5 30.9 %copy-start.8 = (bf16[512,512]{1,0:T(8,128)(2,1)}, bf16[512,512]{1,0:T(8,128)(2,1)S(1)}, u32[]{:S(2)}) copy-start(bf16[512,512]{1,0:T(8,128)(2,1)S(1)} %get-tuple-element.24.refs_5_.refs_3_) | copy-start | bytes 1572868
  30.5 6.2 %collective-permute-start = (bf16[32,8,512]{2,1,0:T(8,128)(2,1)S(1)}, bf16[32,8,512]{2,1,0:T(8,128)(2,1)S(1)}, u32[]{:S(2)}, u32[]{:S(2)}) collective-permute-start(bf16[32,8,512]{2,1,0:T(8,128)(2,1)S(1)} %get-tuple-element.20), channel_id=1, source_target_pairs={{0,7},{1,0},{2,1},{3,2},{4,3},{5,4},{6,5},{7,6},{8,15},{9,8},{10,9... | collective-permute-start | bytes 786440 | tf_op jit(solution)/shard_map/ppermute | solution.py:295
  31.5 15.5 %collective-permute-start.10 = (bf16[512,384]{1,0:T(8,128)(2,1)S(1)}, bf16[512,384]{1,0:T(8,128)(2,1)}, u32[]{:S(2)}, u32[]{:S(2)}) collective-permute-start(bf16[512,384]{1,0:T(8,128)(2,1)S(1)} %copy-done.46), channel_id=1, source_target_pairs={{0,2},{1,3},{2,6},{3,7},{4,0},{5,1},{6,4},{7,5},{8,10},{9,11},{10,... | collective-permute-start | bytes 1179656 | tf_op jit(solution)/shard_map/ppermute | solution.py:295
  33.3 19.8 %collective-permute-start.1 = (bf16[8,24,512]{2,1,0:T(8,128)(2,1)S(1)}, bf16[8,24,512]{2,1,0:T(8,128)(2,1)S(1)}, u32[]{:S(2)}, u32[]{:S(2)}) collective-permute-start(bf16[8,24,512]{2,1,0:T(8,128)(2,1)S(1)} %copy-done.48), channel_id=1, source_target_pairs={{0,24},{1,25},{2,26},{3,27},{4,28},{5,29},{6,30},{7,31},{8,0},{9,1... | collective-permute-start | bytes 589832 | tf_op jit(solution)/shard_map/ppermute | solution.py:295
  36.7 22.1 %copy-start.27 = (bf16[768,128]{1,0:T(8,128)(2,1)}, bf16[768,128]{1,0:T(8,128)(2,1)S(1)}, u32[]{:S(2)}) copy-start(bf16[768,128]{1,0:T(8,128)(2,1)S(1)} %constant_dynamic-update-slice_fusion.rest_16_) | copy-start | bytes 589828
  36.7 10.3 %copy-start.22 = (bf16[32,8,512]{2,1,0:T(8,128)(2,1)}, bf16[32,8,512]{2,1,0:T(8,128)(2,1)S(1)}, u32[]{:S(2)}) copy-start(bf16[32,8,512]{2,1,0:T(8,128)(2,1)S(1)} %collective-permute-done.refs_1_) | copy-start | bytes 786436
  36.7 16.3 %collective-permute-start.2 = (bf16[8,8,512]{2,1,0:T(8,128)(2,1)S(1)}, bf16[8,8,512]{2,1,0:T(8,128)(2,1)S(1)}, u32[]{:S(2)}, u32[]{:S(2)}) collective-permute-start(bf16[8,8,512]{2,1,0:T(8,128)(2,1)S(1)} %copy-done.50), channel_id=1, source_target_pairs={{0,31},{1,24},{2,25},{3,26},{4,27},{5,28},{6,29},{7,30},{8,7},{9,0... | collective-permute-start | bytes 196616 | tf_op jit(solution)/shard_map/ppermute | solution.py:295
  47.0 12.5 %copy-start.20 = (bf16[256,512]{1,0:T(8,128)(2,1)}, bf16[256,512]{1,0:T(8,128)(2,1)S(1)}, u32[]{:S(2)}) copy-start(bf16[256,512]{1,0:T(8,128)(2,1)S(1)} %get-tuple-element.31) | copy-start | bytes 786436
  47.0 12.5 %copy-start.31 = (bf16[64,1024]{1,0:T(8,128)(2,1)}, bf16[64,1024]{1,0:T(8,128)(2,1)S(1)}, u32[]{:S(2)}) copy-start(bf16[64,1024]{1,0:T(8,128)(2,1)S(1)} %get-tuple-element.33) | copy-start | bytes 393220
  47.0 12.4 %collective-permute-start.14 = (bf16[512,384]{1,0:T(8,128)(2,1)}, bf16[512,384]{1,0:T(8,128)(2,1)}, u32[]{:S(2)}, u32[]{:S(2)}) collective-permute-start(bf16[512,384]{1,0:T(8,128)(2,1)} %collective-permute-done.10.rest_4_), channel_id=1, source_target_pairs={{0,2},{1,3},{2,6},{3,7},{4,0},{5,1},{6,4},{7,5},{8,10},{9,11},{10,... | collective-permute-start | bytes 1179656 | tf_op jit(solution)/shard_map/ppermute | solution.py:295
  53.0 5.7 %collective-permute-start.26 = (bf16[768,128]{1,0:T(8,128)(2,1)S(1)}, bf16[768,128]{1,0:T(8,128)(2,1)S(1)}, u32[]{:S(2)}, u32[]{:S(2)}) collective-permute-start(bf16[768,128]{1,0:T(8,128)(2,1)S(1)} %constant_dynamic-update-slice_fusion.rest_16_), channel_id=1, source_target_pairs={{0,8},{1,17},{2,10},{3,19},{4,12},{5,21},{6,14},{7,23},{8,24},{9,1... | collective-permute-start | bytes 589832 | tf_op jit(solution)/shard_map/ppermute | solution.py:295
  53.1 13.3 %copy-start.24 = (bf16[8,24,512]{2,1,0:T(8,128)(2,1)}, bf16[8,24,512]{2,1,0:T(8,128)(2,1)S(1)}, u32[]{:S(2)}) copy-start(bf16[8,24,512]{2,1,0:T(8,128)(2,1)S(1)} %collective-permute-done.1.refs_2_.refs_1_) | copy-start | bytes 589828
  53.1 6.1 %collective-permute-start.6 = (bf16[4,16,1024]{2,1,0:T(8,128)(2,1)S(1)}, bf16[4,16,1024]{2,1,0:T(8,128)(2,1)S(1)}, u32[]{:S(2)}, u32[]{:S(2)}) collective-permute-start(bf16[4,16,1024]{2,1,0:T(8,128)(2,1)S(1)} %pad_maximum_fusion.7), channel_id=1, source_target_pairs={{0,24},{8,0},{16,8},{24,16},{1,25},{9,1},{17,9},{25,17},{2,26},{10... | collective-permute-start | bytes 393224 | tf_op jit(solution)/shard_map/ppermute | solution.py:352
  58.8 7.8 %collective-permute-start.28 = (bf16[768,128]{1,0:T(8,128)(2,1)S(1)}, bf16[768,128]{1,0:T(8,128)(2,1)S(1)}, u32[]{:S(2)}, u32[]{:S(2)}) collective-permute-start(bf16[768,128]{1,0:T(8,128)(2,1)S(1)} %collective-permute-done.26.rest_18_), channel_id=1, source_target_pairs={{0,8},{1,17},{2,10},{3,19},{4,12},{5,21},{6,14},{7,23},{8,24},{9,1... | collective-permute-start | bytes 589832 | tf_op jit(solution)/shard_map/ppermute | solution.py:295
  58.8 7.9 %collective-permute-start.25 = (bf16[768,128]{1,0:T(8,128)(2,1)S(1)}, bf16[768,128]{1,0:T(8,128)(2,1)S(1)}, u32[]{:S(2)}, u32[]{:S(2)}) collective-permute-start(bf16[768,128]{1,0:T(8,128)(2,1)S(1)} %constant_dynamic-update-slice_fusion.rest_16_), channel_id=1, source_target_pairs={{0,1},{1,0},{2,3},{3,2},{4,5},{5,4},{6,7},{7,6},{8,9},{9,8},{10,11... | collective-permute-start | bytes 589832 | tf_op jit(solution)/shard_map/ppermute | solution.py:295
  59.2 10.2 %collective-permute-start.27 = (bf16[768,128]{1,0:T(8,128)(2,1)S(1)}, bf16[768,128]{1,0:T(8,128)(2,1)S(1)}, u32[]{:S(2)}, u32[]{:S(2)}) collective-permute-start(bf16[768,128]{1,0:T(8,128)(2,1)S(1)} %collective-permute-done.26.rest_18_), channel_id=1, source_target_pairs={{0,1},{1,0},{2,3},{3,2},{4,5},{5,4},{6,7},{7,6},{8,9},{9,8},{10,11... | collective-permute-start | bytes 589832 | tf_op jit(solution)/shard_map/ppermute | solution.py:295
  59.5 17.9 %collective-permute-start.18 = (bf16[512,384]{1,0:T(8,128)(2,1)}, bf16[512,384]{1,0:T(8,128)(2,1)}, u32[]{:S(2)}, u32[]{:S(2)}) collective-permute-start(bf16[512,384]{1,0:T(8,128)(2,1)} %collective-permute-done.14.rest_8_), channel_id=1, source_target_pairs={{0,2},{1,3},{2,6},{3,7},{4,0},{5,1},{6,4},{7,5},{8,10},{9,11},{10,... | collective-permute-start | bytes 1179656 | tf_op jit(solution)/shard_map/ppermute | solution.py:295
  66.6 7.7 %collective-permute-start.29 = (bf16[768,128]{1,0:T(8,128)(2,1)S(1)}, bf16[768,128]{1,0:T(8,128)(2,1)S(1)}, u32[]{:S(2)}, u32[]{:S(2)}) collective-permute-start(bf16[768,128]{1,0:T(8,128)(2,1)S(1)} %collective-permute-done.28.rest_20_), channel_id=1, source_target_pairs={{0,1},{1,0},{2,3},{3,2},{4,5},{5,4},{6,7},{7,6},{8,9},{9,8},{10,11... | collective-permute-start | bytes 589832 | tf_op jit(solution)/shard_map/ppermute | solution.py:295
  67.8 8.1 %collective-permute-start.30 = (bf16[768,128]{1,0:T(8,128)(2,1)S(1)}, bf16[768,128]{1,0:T(8,128)(2,1)}, u32[]{:S(2)}, u32[]{:S(2)}) collective-permute-start(bf16[768,128]{1,0:T(8,128)(2,1)S(1)} %collective-permute-done.28.rest_20_), channel_id=1, source_target_pairs={{0,8},{1,17},{2,10},{3,19},{4,12},{5,21},{6,14},{7,23},{8,24},{9,1... | collective-permute-start | bytes 589832 | tf_op jit(solution)/shard_map/ppermute | solution.py:295
  70.1 2.5 %collective-permute-start.7 = (bf16[16,4,1024]{2,1,0:T(4,128)(2,1)S(1)}, bf16[16,4,1024]{2,1,0:T(4,128)(2,1)S(1)}, u32[]{:S(2)}, u32[]{:S(2)}) collective-permute-start(bf16[16,4,1024]{2,1,0:T(4,128)(2,1)S(1)} %fusion.5), channel_id=1, source_target_pairs={{0,7},{1,0},{2,1},{3,2},{4,3},{5,4},{6,5},{7,6},{8,15},{9,8},{10,9... | collective-permute-start | bytes 393224 | tf_op jit(solution)/shard_map/ppermute | solution.py:352
  72.6 6.6 %collective-permute-start.11 = (bf16[512,384]{1,0:T(8,128)(2,1)}, bf16[512,384]{1,0:T(8,128)(2,1)}, u32[]{:S(2)}, u32[]{:S(2)}) collective-permute-start(bf16[512,384]{1,0:T(8,128)(2,1)} %collective-permute-done.10.rest_4_), channel_id=1, source_target_pairs={{0,1},{1,0},{2,3},{3,2},{4,5},{5,4},{6,7},{7,6},{8,9},{9,8},{10,11... | collective-permute-start | bytes 1179656 | tf_op jit(solution)/shard_map/ppermute | solution.py:295
  74.9 8.1 %collective-permute-start.12 = (bf16[512,384]{1,0:T(8,128)(2,1)}, bf16[512,384]{1,0:T(8,128)(2,1)}, u32[]{:S(2)}, u32[]{:S(2)}) collective-permute-start(bf16[512,384]{1,0:T(8,128)(2,1)} %collective-permute-done.10.rest_4_), channel_id=1, source_target_pairs={{0,8},{1,17},{2,10},{3,19},{4,12},{5,21},{6,14},{7,23},{8,24},{9,1... | collective-permute-start | bytes 1179656 | tf_op jit(solution)/shard_map/ppermute | solution.py:295
  75.8 11.4 %collective-permute-start.16 = (bf16[512,384]{1,0:T(8,128)(2,1)}, bf16[512,384]{1,0:T(8,128)(2,1)}, u32[]{:S(2)}, u32[]{:S(2)}) collective-permute-start(bf16[512,384]{1,0:T(8,128)(2,1)} %collective-permute-done.14.rest_8_), channel_id=1, source_target_pairs={{0,8},{1,17},{2,10},{3,19},{4,12},{5,21},{6,14},{7,23},{8,24},{9,1... | collective-permute-start | bytes 1179656 | tf_op jit(solution)/shard_map/ppermute | solution.py:295
  77.3 14.1 %collective-permute-start.20 = (bf16[512,384]{1,0:T(8,128)(2,1)}, bf16[512,384]{1,0:T(8,128)(2,1)}, u32[]{:S(2)}, u32[]{:S(2)}) collective-permute-start(bf16[512,384]{1,0:T(8,128)(2,1)} %collective-permute-done.18.rest_12_), channel_id=1, source_target_pairs={{0,8},{1,17},{2,10},{3,19},{4,12},{5,21},{6,14},{7,23},{8,24},{9,1... | collective-permute-start | bytes 1179656 | tf_op jit(solution)/shard_map/ppermute | solution.py:295
  78.5 4.6 %collective-permute-start.31 = (bf16[768,128]{1,0:T(8,128)(2,1)}, bf16[768,128]{1,0:T(8,128)(2,1)}, u32[]{:S(2)}, u32[]{:S(2)}) collective-permute-start(bf16[768,128]{1,0:T(8,128)(2,1)} %collective-permute-done.30.rest_22_), channel_id=1, source_target_pairs={{0,1},{1,0},{2,3},{3,2},{4,5},{5,4},{6,7},{7,6},{8,9},{9,8},{10,11... | collective-permute-start | bytes 589832 | tf_op jit(solution)/shard_map/ppermute | solution.py:295
  79.2 28.1 %collective-permute-start.15 = (bf16[512,384]{1,0:T(8,128)(2,1)}, bf16[512,384]{1,0:T(8,128)(2,1)S(1)}, u32[]{:S(2)}, u32[]{:S(2)}) collective-permute-start(bf16[512,384]{1,0:T(8,128)(2,1)} %collective-permute-done.14.rest_8_), channel_id=1, source_target_pairs={{0,1},{1,0},{2,3},{3,2},{4,5},{5,4},{6,7},{7,6},{8,9},{9,8},{10,11... | collective-permute-start | bytes 1179656 | tf_op jit(solution)/shard_map/ppermute | solution.py:295
  83.0 23.7 %collective-permute-start.13 = (bf16[512,384]{1,0:T(8,128)(2,1)}, bf16[512,384]{1,0:T(8,128)(2,1)S(1)}, u32[]{:S(2)}, u32[]{:S(2)}) collective-permute-start(bf16[512,384]{1,0:T(8,128)(2,1)} %collective-permute-done.12.rest_6_), channel_id=1, source_target_pairs={{0,1},{1,0},{2,3},{3,2},{4,5},{5,4},{6,7},{7,6},{8,9},{9,8},{10,11... | collective-permute-start | bytes 1179656 | tf_op jit(solution)/shard_map/ppermute | solution.py:295
  83.0 26.6 %collective-permute-start.19 = (bf16[512,384]{1,0:T(8,128)(2,1)}, bf16[512,384]{1,0:T(8,128)(2,1)S(1)}, u32[]{:S(2)}, u32[]{:S(2)}) collective-permute-start(bf16[512,384]{1,0:T(8,128)(2,1)} %collective-permute-done.18.rest_12_), channel_id=1, source_target_pairs={{0,1},{1,0},{2,3},{3,2},{4,5},{5,4},{6,7},{7,6},{8,9},{9,8},{10,11... | collective-permute-start | bytes 1179656 | tf_op jit(solution)/shard_map/ppermute | solution.py:295
  87.2 21.0 %collective-permute-start.17 = (bf16[512,384]{1,0:T(8,128)(2,1)}, bf16[512,384]{1,0:T(8,128)(2,1)S(1)}, u32[]{:S(2)}, u32[]{:S(2)}) collective-permute-start(bf16[512,384]{1,0:T(8,128)(2,1)} %collective-permute-done.16.rest_10_), channel_id=1, source_target_pairs={{0,1},{1,0},{2,3},{3,2},{4,5},{5,4},{6,7},{7,6},{8,9},{9,8},{10,11... | collective-permute-start | bytes 1179656 | tf_op jit(solution)/shard_map/ppermute | solution.py:295
  91.5 18.2 %collective-permute-start.21 = (bf16[512,384]{1,0:T(8,128)(2,1)}, bf16[512,384]{1,0:T(8,128)(2,1)S(1)}, u32[]{:S(2)}, u32[]{:S(2)}) collective-permute-start(bf16[512,384]{1,0:T(8,128)(2,1)} %collective-permute-done.20.rest_14_), channel_id=1, source_target_pairs={{0,1},{1,0},{2,3},{3,2},{4,5},{5,4},{6,7},{7,6},{8,9},{9,8},{10,11... | collective-permute-start | bytes 1179656 | tf_op jit(solution)/shard_map/ppermute | solution.py:295
  106.7 15.6 %collective-permute-start.5 = (bf16[24,8,512]{2,1,0:T(8,128)(2,1)S(1)}, bf16[24,8,512]{2,1,0:T(8,128)(2,1)S(1)}, u32[]{:S(2)}, u32[]{:S(2)}) collective-permute-start(bf16[24,8,512]{2,1,0:T(8,128)(2,1)S(1)} %maximum_maximum_fusion.1), channel_id=1, source_target_pairs={{0,1},{1,2},{2,3},{3,4},{4,5},{5,6},{6,7},{7,0},{8,9},{9,10},{10,1... | collective-permute-start | bytes 589832 | tf_op jit(solution)/shard_map/ppermute | solution.py:295
  107.3 15.0 %collective-permute-start.4 = (bf16[8,24,512]{2,1,0:T(8,128)(2,1)S(1)}, bf16[8,24,512]{2,1,0:T(8,128)(2,1)S(1)}, u32[]{:S(2)}, u32[]{:S(2)}) collective-permute-start(bf16[8,24,512]{2,1,0:T(8,128)(2,1)S(1)} %pad_maximum_fusion.5), channel_id=1, source_target_pairs={{0,8},{1,9},{2,10},{3,11},{4,12},{5,13},{6,14},{7,15},{8,16},{9,17... | collective-permute-start | bytes 589832 | tf_op jit(solution)/shard_map/ppermute | solution.py:295
  108.2 12.5 %collective-permute-start.3 = (bf16[8,8,512]{2,1,0:T(8,128)(2,1)S(1)}, bf16[8,8,512]{2,1,0:T(8,128)(2,1)S(1)}, u32[]{:S(2)}, u32[]{:S(2)}) collective-permute-start(bf16[8,8,512]{2,1,0:T(8,128)(2,1)S(1)} %slice.72), channel_id=1, source_target_pairs={{0,9},{1,10},{2,11},{3,12},{4,13},{5,14},{6,15},{7,8},{8,17},{9,18... | collective-permute-start | bytes 196616 | tf_op jit(solution)/shard_map/ppermute | solution.py:295
  119.1 6.3 %collective-permute-start.34 = (bf16[8,8,1024]{2,1,0:T(8,128)(2,1)S(1)}, bf16[8,8,1024]{2,1,0:T(8,128)(2,1)S(1)}, u32[]{:S(2)}, u32[]{:S(2)}) collective-permute-start(bf16[8,8,1024]{2,1,0:T(8,128)(2,1)S(1)} %get-tuple-element.40), channel_id=1, source_target_pairs={{0,1},{1,2},{2,3},{3,4},{4,5},{5,6},{6,7},{7,0},{8,9},{9,10},{10,1... | collective-permute-start | bytes 393224 | tf_op jit(solution)/shard_map/ppermute | solution.py:295
  119.3 7.1 %collective-permute-start.33 = (bf16[8,8,1024]{2,1,0:T(8,128)(2,1)S(1)}, bf16[8,8,1024]{2,1,0:T(8,128)(2,1)S(1)}, u32[]{:S(2)}, u32[]{:S(2)}) collective-permute-start(bf16[8,8,1024]{2,1,0:T(8,128)(2,1)S(1)} %get-tuple-element.41), channel_id=1, source_target_pairs={{0,8},{1,9},{2,10},{3,11},{4,12},{5,13},{6,14},{7,15},{8,16},{9,17... | collective-permute-start | bytes 393224 | tf_op jit(solution)/shard_map/ppermute | solution.py:295
  120.7 8.1 %collective-permute-start.32 = (bf16[8,8,1024]{2,1,0:T(8,128)(2,1)S(1)}, bf16[8,8,1024]{2,1,0:T(8,128)(2,1)S(1)}, u32[]{:S(2)}, u32[]{:S(2)}) collective-permute-start(bf16[8,8,1024]{2,1,0:T(8,128)(2,1)S(1)} %get-tuple-element.38), channel_id=1, source_target_pairs={{0,9},{1,10},{2,11},{3,12},{4,13},{5,14},{6,15},{7,8},{8,17},{9,18... | collective-permute-start | bytes 393224 | tf_op jit(solution)/shard_map/ppermute | solution.py:295
  (42 other events, 109.2 us)

commit v2 on v1

--- a/solution.py
+++ b/solution.py
@@ -84,18 +84,11 @@
     weights, refs = refs[count:count + 5], refs[count + 5:]
     out_ref, merged_ref = refs[:2]
     qkv, mixed, wide, window, sems = refs[-5:]
-    moves_in = []
-    for at, (name, r, c, to_r, to_c, nr, nc) in enumerate(blocks):
-        moves_in.append(pltpu.make_async_copy(
-            sources[name].at[pl.ds(r, nr), pl.ds(c, nc)],
-            window.at[pl.ds(to_r, nr), pl.ds(to_c, nc)], sems.at[at]))
-    for copy in moves_in:
-        copy.start()
     loads = []
     if first:
         held = refs[2:7]
         for at, (src, dst) in enumerate(zip(weights, held)):
-            loads.append(pltpu.make_async_copy(src, dst, sems.at[4 + at]))
+            loads.append(pltpu.make_async_copy(src, dst, sems.at[at]))
             loads[-1].start()
         weights = held
     vq, vp, vu, vd, vm = weights
@@ -104,8 +97,8 @@
         if first:
             loads[at].wait()
 
-    for copy in moves_in:
-        copy.wait()
+    for name, r, c, to_r, to_c, nr, nc in blocks:
+        window[to_r:to_r + nr, to_c:to_c + nc] = sources[name][r:r + nr, c:c + nc]
     width = window.shape[2]
     x = window[...].reshape(TOK, width).astype(F32)
     normed = norm(x)
@@ -148,13 +141,16 @@
 
 
 def fine_window(i, j, arrays, last, weights, masked, first):
-    rows, cols, width = arrays["field"].shape
+    rows, cols, width = arrays["shape"]
     wide = weights[-1].shape[1]
     blocks = window_blocks(i, j, rows, cols)
+    top, left = HALF + i * WIN, HALF + j * WIN
+    blocks = [(n, r - top, c - left, *to) if n == "field" else (n, r, c, *to) for n, r, c, *to in blocks]
+    arrays = dict(arrays, field=arrays[i, j])
     names = tuple(dict.fromkeys(block[0] for block in blocks))
     flops = 2 * TOK * width * (3 * width + width + 4 * width * 2) + TOK * 2 * width * wide
     size = sum(w.size * 2 for w in weights)
-    hbm = pl.BlockSpec(memory_space=pl.ANY)
+    hbm = pl.BlockSpec(memory_space=pltpu.HBM)
     vmem = pl.BlockSpec(memory_space=pltpu.VMEM)
     held = [jax.ShapeDtypeStruct(w.shape, BF) for w in weights] if first else []
     return pl.pallas_call(
@@ -164,14 +160,14 @@
             jax.ShapeDtypeStruct((TOK // 4, wide), BF),
         ]
         + held,
-        in_specs=[pl.BlockSpec(memory_space=pltpu.SMEM)] + [hbm] * len(names) + [hbm if first else vmem] * 5,
+        in_specs=[pl.BlockSpec(memory_space=pltpu.SMEM)] + [vmem] * len(names) + [hbm if first else vmem] * 5,
         out_specs=[vmem] * (2 + len(held)),
         scratch_shapes=[
             pltpu.VMEM((TOK, 3 * width), BF),
             pltpu.VMEM((TOK, width), BF),
             pltpu.VMEM((width // 128, TOK, 128), F32),
             pltpu.VMEM((WIN, WIN, width), BF),
-            pltpu.SemaphoreType.DMA((9,)),
+            pltpu.SemaphoreType.DMA((5,)),
         ],
         compiler_params=pltpu.CompilerParams(vmem_limit_bytes=24 << 20),
         cost_estimate=pl.CostEstimate(
@@ -181,39 +177,41 @@
     )(last, *[arrays[name] for name in names], *weights)
 
 
-def cut_kernel(regions, offsets, *refs):
-    count = (len(refs) - 1) // 2
+def cut_kernel(parts, offsets, *refs):
+    arrays = max(part[0] for part in parts) + 1
     sems = refs[-1]
     copies = []
-    for at, (src, dst, region) in enumerate(zip(refs[:count], refs[count:-1], regions)):
+    for at, (source, out, region, column) in enumerate(parts):
         where = []
         for start, size in region:
-            if isinstance(start, str):
-                start = pl.multiple_of(offsets[int(start)], size)
+            if start is None:
+                start = pl.multiple_of(offsets[0], size)
             where.append(pl.ds(start, size))
-        copies.append(pltpu.make_async_copy(src.at[tuple(where)], dst, sems.at[at]))
+        src, dst = refs[source].at[tuple(where)], refs[arrays + out]
+        if column is not None:
+            dst = dst.at[:, pl.ds(column, region[-1][1])]
+        copies.append(pltpu.make_async_copy(src, dst, sems.at[at]))
     for copy in copies:
         copy.start()
     for copy in copies:
         copy.wait()
 
 
-def cut(offsets, cuts):
-    hbm = pl.BlockSpec(memory_space=pl.ANY)
+def cut(offsets, arrays, parts, shapes):
+    hbm = pl.BlockSpec(memory_space=pltpu.HBM)
     vmem = pl.BlockSpec(memory_space=pltpu.VMEM)
-    shapes = [tuple(size for _, size in region) for _, region in cuts]
     return pl.pallas_call(
-        functools.partial(cut_kernel, tuple(region for _, region in cuts)),
+        functools.partial(cut_kernel, tuple(parts)),
         out_shape=[jax.ShapeDtypeStruct(shape, BF) for shape in shapes],
-        in_specs=[pl.BlockSpec(memory_space=pltpu.SMEM)] + [hbm] * len(cuts),
-        out_specs=[vmem] * len(cuts),
-        scratch_shapes=[pltpu.SemaphoreType.DMA((len(cuts),))],
+        in_specs=[pl.BlockSpec(memory_space=pltpu.SMEM)] + [hbm] * len(arrays),
+        out_specs=[vmem] * len(shapes),
+        scratch_shapes=[pltpu.SemaphoreType.DMA((len(parts),))],
         compiler_params=pltpu.CompilerParams(vmem_limit_bytes=8 << 20),
         cost_estimate=pl.CostEstimate(
             flops=0, bytes_accessed=sum(2 * int(np.prod(shape)) for shape in shapes), transcendentals=0
         ),
         name="cut",
-    )(offsets, *[array for array, _ in cuts])
+    )(offsets, *arrays)
 
 
 def coarse_kernel(plan, last, table, x_ref, *rest):
@@ -299,10 +297,10 @@
     return ring.index(la) % 2
 
 
-def gather_weights(qkv_shard, proj_shard, qkv_part, proj_part, m, n):
+def gather_weights(qkv_shard, proj_shard, part, m, n):
     deep = qkv_shard.shape[0]
     a, b = qkv_shard.shape[1], proj_shard.shape[1]
-    half, share = qkv_part.shape[0], proj_part.shape[0]
+    half = part.shape[0]
     places = n // 2
     along = moves(line_ring(places))
     ring = line_ring(m)
@@ -315,30 +313,21 @@
 
     pieces, plan, spots = [], [], []
 
-    def add(value, which, spot, columns, cuts):
+    def add(value, spot, rows, key, columns):
         for twin in range(2):
-            for r, rows, key in cuts:
-                plan.append((len(pieces), r, rows, 0, columns, (twin, key), which))
+            for c, count, which in columns:
+                plan.append((len(pieces), 0, rows, c, count, (twin, key), which))
                 spots.append((twin, spot, key))
             pieces.append(swap(value) if twin else value)
 
-    add(qkv_shard, 0, lambda la, lo, key: (0, lo), a, [(0, deep, 0)])
-    add(proj_shard, 1, lambda la, lo, key: (0, lo), b, [(0, deep, 0)])
-    part = qkv_part
-    shares = []
+    add(qkv_shard, lambda la, lo, key: (0, lo), deep, 0, [(0, a, 0)])
+    add(proj_shard, lambda la, lo, key: (0, lo), deep, 0, [(0, b, 1)])
     for s in range(1, places):
         part = send(part, m, n, lambda la, lo: (la, origin(lo, 1)))
-        shares.append(send(proj_part, m, n, lambda la, lo: (la, origin(lo, s))))
         other = send(part, m, n, lambda la, lo: (across(la, turn(lo)), lo))
         for value, flip in ((part, 0), (other, 1)):
             spot = lambda la, lo, key, flip=flip: ((half_of(ring, la) ^ flip) * half, origin(lo, -key))
-            add(value, 0, spot, a, [(0, half, s)])
-    plane = jnp.concatenate(shares, axis=0)
-    for k in range(m):
-        if k > 0:
-            plane = send(plane, m, n, lambda la, lo: (across(la, turn(lo)), lo))
-        spot = lambda la, lo, key, k=k: (across(la, -k * turn(lo)) * share, origin(lo, -key))
-        add(plane, 1, spot, b, [((s - 1) * share, share, s) for s in range(1, places)])
+            add(value, spot, half, s, [(0, a, 0), (a, b, 1)])
     tables = np.zeros((m, n, len(spots), 2), np.int32)
     for la in range(m):
         for lo in range(n):
@@ -364,27 +353,37 @@
     deep, a = qkv_coarse.shape
     b = proj_coarse.shape[1]
     direct = a % 128 == 0 and b % 128 == 0 and n % 2 == 0 and m % 2 == 0 and deep % (16 * m) == 0
-    cuts = [
-        (field, ((0, rows), (0, HALF), (0, width))),
-        (field, ((0, HALF), (HALF, cols - HALF), (0, width))),
-        (field, ((0, HALF), (0, HALF), (0, width))),
+    parts = [
+        (0, 0, ((0, rows), (0, HALF), (0, width)), None),
+        (0, 1, ((0, HALF), (HALF, cols - HALF), (0, width)), None),
+        (0, 2, ((0, HALF), (0, HALF), (0, width)), None),
     ]
+    inner = [(i, j) for i in range(wr) for j in range(wc)]
+    for at, (i, j) in enumerate(inner):
+        top, left = HALF + i * WIN, HALF + j * WIN
+        region = ((top, min(WIN, rows - top)), (left, min(WIN, cols - left)), (0, width))
+        parts.append((0, 3 + at, region, None))
+    shapes = [tuple(size for _, size in part[2]) for part in parts]
+    sources = [field]
     lat = lax.axis_index("lat")
     ring = line_ring(m)
-    offsets = jnp.asarray(
-        np.array([(half_of(ring, la) * (deep // 2), la * (deep // m)) for la in range(m)], np.int32)
-    )[lat]
+    offsets = jnp.asarray(np.array([[half_of(ring, la) * (deep // 2)] for la in range(m)], np.int32))[lat]
     if direct:
-        cuts += [(qkv_coarse, (("0", deep // 2), (0, a))), (proj_coarse, (("1", deep // m), (0, b)))]
-    parts = cut(offsets, cuts)
+        parts.append((1, len(shapes), ((None, deep // 2), (0, a)), 0))
+        parts.append((2, len(shapes), ((None, deep // 2), (0, b)), a))
+        shapes.append((deep // 2, a + b))
+        sources += [qkv_coarse, proj_coarse]
+    got = cut(offsets, sources, parts, shapes)
     up = lambda la: (la - 1) % m
     left = lambda lo: (lo - 1) % n
-    arrays = {"field": field}
-    arrays["east"] = send(parts[0], m, n, lambda la, lo: (la, left(lo)))
-    arrays["south"] = send(parts[1], m, n, lambda la, lo: (up(la), lo))
-    arrays["corner"] = send(parts[2], m, n, lambda la, lo: (up(la), left(lo)))
+    arrays = {"shape": field.shape}
+    for at, place in enumerate(inner):
+        arrays[place] = got[3 + at]
+    arrays["east"] = send(got[0], m, n, lambda la, lo: (la, left(lo)))
+    arrays["south"] = send(got[1], m, n, lambda la, lo: (up(la), lo))
+    arrays["corner"] = send(got[2], m, n, lambda la, lo: (up(la), left(lo)))
     if direct:
-        pieces, plan, table = gather_weights(qkv_coarse, proj_coarse, parts[3], parts[4], m, n)
+        pieces, plan, table = gather_weights(qkv_coarse, proj_coarse, got[-1], m, n)
     else:
         pieces = [lax.all_gather(w, "lon", axis=1, tiled=True) for w in (qkv_coarse, proj_coarse)]
         plan = ((0, 0, deep, 0, a * n, 0, 0), (1, 0, deep, 0, b * n, 0, 1))

time: 131 us -> 124 us (0.947)
  starting transfers between devices: 40.5 us -> 26.8 us
  waiting for transfers between devices: 23.2 us -> 33.7 us
  local copies, waits for them, and re-layouts: 30.4 us -> 23.6 us
  Pallas kernels: 32 us -> 34.8 us
    ppermute x33 -> x23, starting transfers between devices: 38.5 us -> 24.1 us  [send(): return lax.ppermute(value, ('lat', 'lon'), pairs)]
    ppermute x33 -> x23, waiting for transfers between devices: 20.3 us -> 33.7 us  [send(): return lax.ppermute(value, ('lat', 'lon'), pairs)]
    unnamed x112 -> x60, local copies, waits for them, and re-layouts: 28.1 us -> 21.6 us
    ppermute x2, waiting for transfers between devices: 2.85 us -> 0.01 us  [shifted(): lax.ppermute(value, axis, [(s, (s + steps) % count) for s in range(count)])]
    pallas_call x4, Pallas kernels: 21.2 us -> 22.7 us  [fine_window(): pl.pallas_call(functools.partial(fine_kernel, masked, first, names, block...]
  transfers between devices with their start and end apart: 35 -> 25, of which waited for: 9 -> 8; matrix products, arithmetic and copies ran while one was open for 4% -> 3% of each run, Pallas kernels for 25% -> 26%
where the time goes in v2:
time: 124 us; the launch traced here: 123 us
  Pallas kernels  34.8 us (28%)
  waiting for transfers between devices  33.7 us (27%)
  starting transfers between devices  26.8 us (22%)
  local copies, waits for them, and re-layouts  23.6 us (19%)
  other arithmetic  3.22 us (3%)
    ppermute x23, waiting for transfers between devices, send(): return lax.ppermute(value, ('lat', 'lon'), pairs)  33.7 us
    ppermute x23, starting transfers between devices, send(): return lax.ppermute(value, ('lat', 'lon'), pairs)  24.1 us
    pallas_call x4, Pallas kernels, fine_window(): pl.pallas_call(functools.partial(fine_kernel, masked, first, names, block...  22.7 us
    unnamed x60, local copies, waits for them, and re-layouts  21.6 us
    pallas_call x1, Pallas kernels, coarse_window(): pl.pallas_call(functools.partial(coarse_kernel, plan), out_shape=jax.Shap...  9.53 us
    ppermute x2, starting transfers between devices, shifted(): lax.ppermute(value, axis, [(s, (s + steps) % count) for s in range(count)])  2.74 us
    pallas_call x1, Pallas kernels, cut(): pl.pallas_call(functools.partial(cut_kernel, tuple(parts)), out_shape=[ja...  2.56 us
  transfers between devices with their start and end apart: 25, of which 8 were waited for; matrix products, arithmetic and copies ran while one was open for 3% of the time, Pallas kernels for 26%

profile of v2, /device:TPU:0, one launch (start us, length us, event | category | flops | bytes accessed | tf_op | source)
XLA Modules:
  0.0 123.1 jit_solution(7386392887866047413)
XLA Ops:
  0.6 1.2 constant_dynamic-slice_fusion
  1.8 1.2 copy-done.12
  3.1 2.6 %cut.1 = (bf16[32,8,512]{2,1,0:T(8,128)(2,1)}, bf16[8,24,512]{2,1,0:T(8,128)(2,1)}, bf16[8,8,512]{2,1,0:T(8,128)(2,1)S(1)}, bf16[16,16,512]{2,1,0:T(8,128)(2,1)S...) custom-call(s32[1]{0:T(128)} %bitcast.1.offsets, ...), custom_call_target="tpu_custom_call" | custom-call | bytes 1638400 | tf_op jit(solution)/shard_map/cut/pallas_call | solution.py:203
  5.6 0.6 copy-done.18
  6.3 0.6 copy-done.20
  6.9 0.6 copy-done.22
  7.5 0.6 copy-done.26
  8.1 3.1 %collective-permute-start.10 = (bf16[512,512]{1,0:T(8,128)(2,1)S(1)}, bf16[512,512]{1,0:T(8,128)(2,1)}, u32[]{:S(2)}, u32[]{:S(2)}) collective-permute-start(bf16[512,512]{1,0:T(8,128)(2,1)S(1)} %get-tuple-element.43), channel_id=1, source_target_pairs={{0,2},{1,3},{2,6},{3,7},{4,0},{5,1},{6,4},{7,5},{8,10},{9,11},{10,... | collective-permute-start | bytes 1572872 | tf_op jit(solution)/shard_map/ppermute | solution.py:293
  11.2 1.6 %collective-permute-start = (bf16[32,8,512]{2,1,0:T(8,128)(2,1)}, bf16[32,8,512]{2,1,0:T(8,128)(2,1)S(1)}, u32[]{:S(2)}, u32[]{:S(2)}) collective-permute-start(bf16[32,8,512]{2,1,0:T(8,128)(2,1)} %get-tuple-element.24), channel_id=1, source_target_pairs={{0,7},{1,0},{2,1},{3,2},{4,3},{5,4},{6,5},{7,6},{8,15},{9,8},{10,9... | collective-permute-start | bytes 786440 | tf_op jit(solution)/shard_map/ppermute | solution.py:293
  13.3 2.4 %collective-permute-start.1 = (bf16[8,24,512]{2,1,0:T(8,128)(2,1)}, bf16[8,24,512]{2,1,0:T(8,128)(2,1)}, u32[]{:S(2)}, u32[]{:S(2)}) collective-permute-start(bf16[8,24,512]{2,1,0:T(8,128)(2,1)} %get-tuple-element.25), channel_id=1, source_target_pairs={{0,24},{1,25},{2,26},{3,27},{4,28},{5,29},{6,30},{7,31},{8,0},{9,1... | collective-permute-start | bytes 589832 | tf_op jit(solution)/shard_map/ppermute | solution.py:293
  15.8 8.5 %collective-permute-done.10.rest_4_ = bf16[512,512]{1,0:T(8,128)(2,1)} collective-permute-done((bf16[512,512]{1,0:T(8,128)(2,1)S(1)}, bf16[512,512]{1,0:T(8,128)(2,1)}, u32[]{:S(2)}, u32[]{:S(2)}) %collective-permute-start.10) | collective-permute-done | bytes 524320 | tf_op jit(solution)/shard_map/ppermute | solution.py:293
  24.3 3.4 %collective-permute-start.14 = (bf16[512,512]{1,0:T(8,128)(2,1)}, bf16[512,512]{1,0:T(8,128)(2,1)}, u32[]{:S(2)}, u32[]{:S(2)}) collective-permute-start(bf16[512,512]{1,0:T(8,128)(2,1)} %collective-permute-done.10.rest_4_), channel_id=1, source_target_pairs={{0,2},{1,3},{2,6},{3,7},{4,0},{5,1},{6,4},{7,5},{8,10},{9,11},{10,... | collective-permute-start | bytes 1572872 | tf_op jit(solution)/shard_map/ppermute | solution.py:293
  27.7 2.2 %copy-done.6 = bf16[2048,1024]{1,0:T(8,128)(2,1)S(1)} copy-done((bf16[2048,1024]{1,0:T(8,128)(2,1)S(1)}, bf16[2048,1024]{1,0:T(8,128)(2,1)}, u32[]{:S(2)}) %copy-start.6) | copy-done | bytes 4194328
  29.9 1.6 %copy-done.7 = bf16[512,2048]{1,0:T(8,128)(2,1)S(1)} copy-done((bf16[512,2048]{1,0:T(8,128)(2,1)S(1)}, bf16[512,2048]{1,0:T(8,128)(2,1)}, u32[]{:S(2)}) %copy-start.7) | copy-done | bytes 2097176
  31.5 1.6 %copy-done.8 = bf16[2048,512]{1,0:T(8,128)(2,1)S(1)} copy-done((bf16[2048,512]{1,0:T(8,128)(2,1)S(1)}, bf16[2048,512]{1,0:T(8,128)(2,1)}, u32[]{:S(2)}) %copy-start.8) | copy-done | bytes 2097176
  33.1 1.4 %copy-done.9 = bf16[512,1536]{1,0:T(8,128)(2,1)S(1)} copy-done((bf16[512,1536]{1,0:T(8,128)(2,1)S(1)}, bf16[512,1536]{1,0:T(8,128)(2,1)}, u32[]{:S(2)}) %copy-start.9) | copy-done | bytes 1572888
  34.5 1.0 copy-done.13
  35.6 5.9 %fine_first.1 = (bf16[256,512]{1,0:T(8,128)(2,1)S(1)}, bf16[64,1024]{1,0:T(8,128)(2,1)S(1)}, bf16[512,1536]{1,0:T(8,128)(2,1)S(1)}, bf16[512,512]{1,0:T(8,128)(2...) custom-call(s32[1]{0:T(128)} %bitcast.last, ...), custom_call_target="tpu_custom_call" | custom-call | flops 1879048192 | bytes 11272192 | tf_op jit(solution)/shard_map/fine_first/pallas_call | solution.py:156
  41.6 5.0 %fine_plain.1 = (bf16[256,512]{1,0:T(8,128)(2,1)S(1)}, bf16[64,1024]{1,0:T(8,128)(2,1)S(1)}) custom-call(s32[1]{0:T(128)} %bitcast.last, bf16[16,8,512]{2,1,0:T(8,128)(2,1)S(1)} %copy-done.21, bf16[32,8,512]{2,1,0:T(8,128)(2,1)S(1)} %collective-permute-done.refs_1_, bf16[512,1536]{1,0:T(8,128)(2,1)S(1)} %get-tuple-element.28.refs_4_.refs_2_, ...), custom_call_target="tpu_custom_call" | custom-call | flops 1879048192 | bytes 11272192 | tf_op jit(solution)/shard_map/fine_plain/pallas_call | solution.py:156
  46.6 3.6 %collective-permute-start.18 = (bf16[512,512]{1,0:T(8,128)(2,1)}, bf16[512,512]{1,0:T(8,128)(2,1)}, u32[]{:S(2)}, u32[]{:S(2)}) collective-permute-start(bf16[512,512]{1,0:T(8,128)(2,1)} %collective-permute-done.14.rest_8_), channel_id=1, source_target_pairs={{0,2},{1,3},{2,6},{3,7},{4,0},{5,1},{6,4},{7,5},{8,10},{9,11},{10,... | collective-permute-start | bytes 1572872 | tf_op jit(solution)/shard_map/ppermute | solution.py:293
  50.2 2.7 %collective-permute-start.6 = (bf16[4,16,1024]{2,1,0:T(8,128)(2,1)S(1)}, bf16[4,16,1024]{2,1,0:T(8,128)(2,1)S(1)}, u32[]{:S(2)}, u32[]{:S(2)}) collective-permute-start(bf16[4,16,1024]{2,1,0:T(8,128)(2,1)S(1)} %pad_maximum_fusion.7), channel_id=1, source_target_pairs={{0,24},{8,0},{16,8},{24,16},{1,25},{9,1},{17,9},{25,17},{2,26},{10... | collective-permute-start | bytes 393224 | tf_op jit(solution)/shard_map/ppermute | solution.py:341
  52.9 5.9 %fine_masked.3 = (bf16[256,512]{1,0:T(8,128)(2,1)S(1)}, bf16[64,1024]{1,0:T(8,128)(2,1)S(1)}) custom-call(s32[1]{0:T(128)} %bitcast.last, bf16[8,16,512]{2,1,0:T(8,128)(2,1)S(1)} %copy-done.19, bf16[8,24,512]{2,1,0:T(8,128)(2,1)} %collective-permute-done.1.refs_2_.refs_1_, bf16[512,1536]{1,0:T(8,128)(2,1)S(1)} %get-tuple-element.28.refs_4_.refs_2_, ...), custom_call_target="tpu_custom_call" | custom-call | flops 1879048192 | bytes 11272192 | tf_op jit(solution)/shard_map/fine_masked/pallas_call | solution.py:156
  58.9 0.6 copy-done.14
  59.8 3.7 %collective-permute-done.2.refs_3_ = bf16[8,8,512]{2,1,0:T(8,128)(2,1)S(1)} collective-permute-done((bf16[8,8,512]{2,1,0:T(8,128)(2,1)S(1)}, bf16[8,8,512]{2,1,0:T(8,128)(2,1)S(1)}, u32[]{:S(2)}, u32[]{:S(2)}) %collective-permute-start.2) | collective-permute-done | bytes 65568 | tf_op jit(solution)/shard_map/ppermute | solution.py:293
  63.5 0.6 copy-done.24
  64.6 1.1 collective-permute-start.11
  65.7 1.5 %collective-permute-start.16 = (bf16[512,512]{1,0:T(8,128)(2,1)}, bf16[512,512]{1,0:T(8,128)(2,1)}, u32[]{:S(2)}, u32[]{:S(2)}) collective-permute-start(bf16[512,512]{1,0:T(8,128)(2,1)} %collective-permute-done.14.rest_8_), channel_id=1, source_target_pairs={{0,8},{1,17},{2,10},{3,19},{4,12},{5,21},{6,14},{7,23},{8,24},{9,1... | collective-permute-start | bytes 1572872 | tf_op jit(solution)/shard_map/ppermute | solution.py:293
  67.7 0.7 dynamic-slice_bitcast_fusion.table
  68.4 5.2 %collective-permute-done.12.rest_6_ = bf16[512,512]{1,0:T(8,128)(2,1)} collective-permute-done((bf16[512,512]{1,0:T(8,128)(2,1)}, bf16[512,512]{1,0:T(8,128)(2,1)}, u32[]{:S(2)}, u32[]{:S(2)}) %collective-permute-start.12) | collective-permute-done | bytes 524320 | tf_op jit(solution)/shard_map/ppermute | solution.py:293
  74.1 5.1 %collective-permute-done.16.rest_10_ = bf16[512,512]{1,0:T(8,128)(2,1)} collective-permute-done((bf16[512,512]{1,0:T(8,128)(2,1)}, bf16[512,512]{1,0:T(8,128)(2,1)}, u32[]{:S(2)}, u32[]{:S(2)}) %collective-permute-start.16) | collective-permute-done | bytes 524320 | tf_op jit(solution)/shard_map/ppermute | solution.py:293
  79.7 5.1 %collective-permute-done.20.rest_14_ = bf16[512,512]{1,0:T(8,128)(2,1)} collective-permute-done((bf16[512,512]{1,0:T(8,128)(2,1)}, bf16[512,512]{1,0:T(8,128)(2,1)}, u32[]{:S(2)}, u32[]{:S(2)}) %collective-permute-start.20) | collective-permute-done | bytes 524320 | tf_op jit(solution)/shard_map/ppermute | solution.py:293
  85.1 2.2 %copy-done.1 = bf16[2048,1024]{1,0:T(8,128)(2,1)S(1)} copy-done((bf16[2048,1024]{1,0:T(8,128)(2,1)S(1)}, bf16[2048,1024]{1,0:T(8,128)(2,1)}, u32[]{:S(2)}) %copy-start.1) | copy-done | bytes 4194328
  87.2 1.6 %copy-done.3 = bf16[2048,512]{1,0:T(8,128)(2,1)S(1)} copy-done((bf16[2048,512]{1,0:T(8,128)(2,1)S(1)}, bf16[2048,512]{1,0:T(8,128)(2,1)}, u32[]{:S(2)}) %copy-start.3) | copy-done | bytes 2097176
  88.8 1.4 %copy-done.5 = bf16[512,1536]{1,0:T(8,128)(2,1)S(1)} copy-done((bf16[512,1536]{1,0:T(8,128)(2,1)S(1)}, bf16[512,1536]{1,0:T(8,128)(2,1)}, u32[]{:S(2)}) %copy-start.5) | copy-done | bytes 1572888
  90.2 0.9 copy-done.11
  91.2 0.8 copy-done.23
  92.0 0.8 copy-done.25
  92.9 5.9 %fine_masked.2 = (bf16[256,512]{1,0:T(8,128)(2,1)S(1)}, bf16[64,1024]{1,0:T(8,128)(2,1)S(1)}) custom-call(s32[1]{0:T(128)} %bitcast.last, bf16[8,8,512]{2,1,0:T(8,128)(2,1)S(1)} %copy-done.23, bf16[32,8,512]{2,1,0:T(8,128)(2,1)S(1)} %copy-done.11, bf16[8,24,512]{2,1,0:T(8,128)(2,1)} %collective-permute-done.1.refs_2_.refs_1_, ...), custom_call_target="tpu_custom_call" | custom-call | flops 1879048192 | bytes 11272192 | tf_op jit(solution)/shard_map/fine_masked/pallas_call | solution.py:156
  98.9 0.8 copy-done.15
  99.8 1.2 fusion.3
  101.9 0.9 collective-permute-start.3
  102.8 9.5 %coarse.1 = bf16[256,1024]{1,0:T(8,128)(2,1)S(1)} custom-call(s32[1]{0:T(128)} %bitcast.last, s32[56]{0:T(128)S(1)} %dynamic-slice_bitcast_fusion.table, bf16[256,1024]{1,0:T(8,128)(2,1)S(1)} %bitcast.25, bf16[1024,384]{1,0:T(8,128)(2,1)} %rest_0_.1, bf16[1024,384]{1,0:T(8,128)(2,1)} %collective-permute-done.8.rest_1_, bf16[1024,128]{1,0:T(8,128)(2,1)} %rest_2_.1, ...), custom_call_target="tpu_custom_call" | custom-call | flops 2147483648 | bytes 8388608 | tf_op jit(solution)/shard_map/coarse/pallas_call | solution.py:258
  112.8 1.5 %collective-permute-start.23 = (bf16[8,8,1024]{2,1,0:T(8,128)(2,1)S(1)}, bf16[8,8,1024]{2,1,0:T(8,128)(2,1)S(1)}, u32[]{:S(2)}, u32[]{:S(2)}) collective-permute-start(bf16[8,8,1024]{2,1,0:T(8,128)(2,1)S(1)} %get-tuple-element.47), channel_id=1, source_target_pairs={{0,8},{1,9},{2,10},{3,11},{4,12},{5,13},{6,14},{7,15},{8,16},{9,17... | collective-permute-start | bytes 393224 | tf_op jit(solution)/shard_map/ppermute | solution.py:293
  114.3 0.9 collective-permute-start.22
  115.2 1.1 fusion.2
  116.3 2.3 %collective-permute-done.24 = bf16[8,8,1024]{2,1,0:T(8,128)(2,1)S(1)} collective-permute-done((bf16[8,8,1024]{2,1,0:T(8,128)(2,1)S(1)}, bf16[8,8,1024]{2,1,0:T(8,128)(2,1)S(1)}, u32[]{:S(2)}, u32[]{:S(2)}) %collective-permute-start.24) | collective-permute-done | bytes 131104 | tf_op jit(solution)/shard_map/ppermute | solution.py:293
  119.2 3.1 %collective-permute-done.22 = bf16[8,8,1024]{2,1,0:T(8,128)(2,1)S(1)} collective-permute-done((bf16[8,8,1024]{2,1,0:T(8,128)(2,1)S(1)}, bf16[8,8,1024]{2,1,0:T(8,128)(2,1)S(1)}, u32[]{:S(2)}, u32[]{:S(2)}) %collective-permute-start.22) | collective-permute-done | bytes 131104 | tf_op jit(solution)/shard_map/ppermute | solution.py:293
  122.3 0.8 maximum_maximum_fusion
  (83 shorter events, 5.3 us)
Async XLA Ops:
  1.8 1.2 copy-start.12
  8.1 16.2 %collective-permute-start.10 = (bf16[512,512]{1,0:T(8,128)(2,1)S(1)}, bf16[512,512]{1,0:T(8,128)(2,1)}, u32[]{:S(2)}, u32[]{:S(2)}) collective-permute-start(bf16[512,512]{1,0:T(8,128)(2,1)S(1)} %get-tuple-element.43), channel_id=1, source_target_pairs={{0,2},{1,3},{2,6},{3,7},{4,0},{5,1},{6,4},{7,5},{8,10},{9,11},{10,... | collective-permute-start | bytes 1572872 | tf_op jit(solution)/shard_map/ppermute | solution.py:293
  11.2 30.4 %collective-permute-start = (bf16[32,8,512]{2,1,0:T(8,128)(2,1)}, bf16[32,8,512]{2,1,0:T(8,128)(2,1)S(1)}, u32[]{:S(2)}, u32[]{:S(2)}) collective-permute-start(bf16[32,8,512]{2,1,0:T(8,128)(2,1)} %get-tuple-element.24), channel_id=1, source_target_pairs={{0,7},{1,0},{2,1},{3,2},{4,3},{5,4},{6,5},{7,6},{8,15},{9,8},{10,9... | collective-permute-start | bytes 786440 | tf_op jit(solution)/shard_map/ppermute | solution.py:293
  12.8 55.6 %collective-permute-start.8 = (bf16[1024,384]{1,0:T(8,128)(2,1)}, bf16[1024,384]{1,0:T(8,128)(2,1)}, u32[]{:S(2)}, u32[]{:S(2)}) collective-permute-start(bf16[1024,384]{1,0:T(8,128)(2,1)} %rest_0_.1), channel_id=1, source_target_pairs={{0,1},{1,0},{2,3},{3,2},{4,5},{5,4},{6,7},{7,6},{8,9},{9,8},{10,11... | collective-permute-start | bytes 2359304 | tf_op jit(solution)/shard_map/ppermute | solution.py:293
  12.8 51.8 %collective-permute-start.9 = (bf16[1024,128]{1,0:T(8,128)(2,1)}, bf16[1024,128]{1,0:T(8,128)(2,1)}, u32[]{:S(2)}, u32[]{:S(2)}) collective-permute-start(bf16[1024,128]{1,0:T(8,128)(2,1)} %rest_2_.1), channel_id=1, source_target_pairs={{0,1},{1,0},{2,3},{3,2},{4,5},{5,4},{6,7},{7,6},{8,9},{9,8},{10,11... | collective-permute-start | bytes 786440 | tf_op jit(solution)/shard_map/ppermute | solution.py:293
  13.3 39.6 %collective-permute-start.1 = (bf16[8,24,512]{2,1,0:T(8,128)(2,1)}, bf16[8,24,512]{2,1,0:T(8,128)(2,1)}, u32[]{:S(2)}, u32[]{:S(2)}) collective-permute-start(bf16[8,24,512]{2,1,0:T(8,128)(2,1)} %get-tuple-element.25), channel_id=1, source_target_pairs={{0,24},{1,25},{2,26},{3,27},{4,28},{5,29},{6,30},{7,31},{8,0},{9,1... | collective-permute-start | bytes 589832 | tf_op jit(solution)/shard_map/ppermute | solution.py:293
  24.3 22.3 %collective-permute-start.14 = (bf16[512,512]{1,0:T(8,128)(2,1)}, bf16[512,512]{1,0:T(8,128)(2,1)}, u32[]{:S(2)}, u32[]{:S(2)}) collective-permute-start(bf16[512,512]{1,0:T(8,128)(2,1)} %collective-permute-done.10.rest_4_), channel_id=1, source_target_pairs={{0,2},{1,3},{2,6},{3,7},{4,0},{5,1},{6,4},{7,5},{8,10},{9,11},{10,... | collective-permute-start | bytes 1572872 | tf_op jit(solution)/shard_map/ppermute | solution.py:293
  27.7 2.2 %copy-start.6 = (bf16[2048,1024]{1,0:T(8,128)(2,1)S(1)}, bf16[2048,1024]{1,0:T(8,128)(2,1)}, u32[]{:S(2)}) copy-start(bf16[2048,1024]{1,0:T(8,128)(2,1)} %refs_5_.1) | copy-start | bytes 12582916
  29.9 1.6 %copy-start.7 = (bf16[512,2048]{1,0:T(8,128)(2,1)S(1)}, bf16[512,2048]{1,0:T(8,128)(2,1)}, u32[]{:S(2)}) copy-start(bf16[512,2048]{1,0:T(8,128)(2,1)} %refs_3_.1) | copy-start | bytes 6291460
  31.5 1.6 %copy-start.8 = (bf16[2048,512]{1,0:T(8,128)(2,1)S(1)}, bf16[2048,512]{1,0:T(8,128)(2,1)}, u32[]{:S(2)}) copy-start(bf16[2048,512]{1,0:T(8,128)(2,1)} %refs_4_.1) | copy-start | bytes 6291460
  33.1 1.4 %copy-start.9 = (bf16[512,1536]{1,0:T(8,128)(2,1)S(1)}, bf16[512,1536]{1,0:T(8,128)(2,1)}, u32[]{:S(2)}) copy-start(bf16[512,1536]{1,0:T(8,128)(2,1)} %refs_1_.3) | copy-start | bytes 4718596
  34.5 1.0 copy-start.13
  35.6 6.0 %copy-start.21 = (bf16[16,8,512]{2,1,0:T(8,128)(2,1)S(1)}, bf16[16,8,512]{2,1,0:T(8,128)(2,1)}, u32[]{:S(2)}) copy-start(bf16[16,8,512]{2,1,0:T(8,128)(2,1)} %copy-done.20) | copy-start | bytes 393220
  41.5 11.4 %copy-start = (bf16[2048,1024]{1,0:T(8,128)(2,1)}, bf16[2048,1024]{1,0:T(8,128)(2,1)S(1)}, u32[]{:S(2)}) copy-start(bf16[2048,1024]{1,0:T(8,128)(2,1)S(1)} %get-tuple-element.32.refs_8_.refs_6_) | copy-start | bytes 12582916
  41.5 11.4 %copy-start.2 = (bf16[2048,512]{1,0:T(8,128)(2,1)}, bf16[2048,512]{1,0:T(8,128)(2,1)S(1)}, u32[]{:S(2)}) copy-start(bf16[2048,512]{1,0:T(8,128)(2,1)S(1)} %get-tuple-element.31.refs_7_.refs_5_) | copy-start | bytes 6291460
  41.5 11.4 %copy-start.4 = (bf16[512,1536]{1,0:T(8,128)(2,1)}, bf16[512,1536]{1,0:T(8,128)(2,1)S(1)}, u32[]{:S(2)}) copy-start(bf16[512,1536]{1,0:T(8,128)(2,1)S(1)} %get-tuple-element.28.refs_4_.refs_2_) | copy-start | bytes 4718596
  41.6 5.0 %copy-start.10 = (bf16[32,8,512]{2,1,0:T(8,128)(2,1)}, bf16[32,8,512]{2,1,0:T(8,128)(2,1)S(1)}, u32[]{:S(2)}) copy-start(bf16[32,8,512]{2,1,0:T(8,128)(2,1)S(1)} %collective-permute-done.refs_1_) | copy-start | bytes 786436
  41.6 11.3 %copy-start.19 = (bf16[8,16,512]{2,1,0:T(8,128)(2,1)S(1)}, bf16[8,16,512]{2,1,0:T(8,128)(2,1)}, u32[]{:S(2)}) copy-start(bf16[8,16,512]{2,1,0:T(8,128)(2,1)} %copy-done.18) | copy-start | bytes 393220
  46.6 6.3 %copy-start.16 = (bf16[64,1024]{1,0:T(8,128)(2,1)}, bf16[64,1024]{1,0:T(8,128)(2,1)S(1)}, u32[]{:S(2)}) copy-start(bf16[64,1024]{1,0:T(8,128)(2,1)S(1)} %get-tuple-element.40) | copy-start | bytes 393220
  46.6 20.6 %collective-permute-start.18 = (bf16[512,512]{1,0:T(8,128)(2,1)}, bf16[512,512]{1,0:T(8,128)(2,1)}, u32[]{:S(2)}, u32[]{:S(2)}) collective-permute-start(bf16[512,512]{1,0:T(8,128)(2,1)} %collective-permute-done.14.rest_8_), channel_id=1, source_target_pairs={{0,2},{1,3},{2,6},{3,7},{4,0},{5,1},{6,4},{7,5},{8,10},{9,11},{10,... | collective-permute-start | bytes 1572872 | tf_op jit(solution)/shard_map/ppermute | solution.py:293
  50.2 9.3 %collective-permute-start.6 = (bf16[4,16,1024]{2,1,0:T(8,128)(2,1)S(1)}, bf16[4,16,1024]{2,1,0:T(8,128)(2,1)S(1)}, u32[]{:S(2)}, u32[]{:S(2)}) collective-permute-start(bf16[4,16,1024]{2,1,0:T(8,128)(2,1)S(1)} %pad_maximum_fusion.7), channel_id=1, source_target_pairs={{0,24},{8,0},{16,8},{24,16},{1,25},{9,1},{17,9},{25,17},{2,26},{10... | collective-permute-start | bytes 393224 | tf_op jit(solution)/shard_map/ppermute | solution.py:341
  52.9 6.8 %copy-start.27 = (bf16[8,8,512]{2,1,0:T(8,128)(2,1)S(1)}, bf16[8,8,512]{2,1,0:T(8,128)(2,1)}, u32[]{:S(2)}) copy-start(bf16[8,8,512]{2,1,0:T(8,128)(2,1)} %copy-done.26) | copy-start | bytes 196612
  59.6 4.0 %copy-start.28 = (bf16[4,16,1024]{2,1,0:T(8,128)(2,1)}, bf16[4,16,1024]{2,1,0:T(8,128)(2,1)S(1)}, u32[]{:S(2)}) copy-start(bf16[4,16,1024]{2,1,0:T(8,128)(2,1)S(1)} %collective-permute-done.6) | copy-start | bytes 393220
  59.7 6.0 %collective-permute-start.7 = (bf16[16,4,1024]{2,1,0:T(4,128)(2,1)S(1)}, bf16[16,4,1024]{2,1,0:T(4,128)(2,1)}, u32[]{:S(2)}, u32[]{:S(2)}) collective-permute-start(bf16[16,4,1024]{2,1,0:T(4,128)(2,1)S(1)} %fusion.5), channel_id=1, source_target_pairs={{0,7},{1,0},{2,1},{3,2},{4,3},{5,4},{6,5},{7,6},{8,15},{9,8},{10,9... | collective-permute-start | bytes 393224 | tf_op jit(solution)/shard_map/ppermute | solution.py:341
  59.8 3.7 %collective-permute-start.2 = (bf16[8,8,512]{2,1,0:T(8,128)(2,1)S(1)}, bf16[8,8,512]{2,1,0:T(8,128)(2,1)S(1)}, u32[]{:S(2)}, u32[]{:S(2)}) collective-permute-start(bf16[8,8,512]{2,1,0:T(8,128)(2,1)S(1)} %copy-done.27), channel_id=1, source_target_pairs={{0,31},{1,24},{2,25},{3,26},{4,27},{5,28},{6,29},{7,30},{8,7},{9,0... | collective-permute-start | bytes 196616 | tf_op jit(solution)/shard_map/ppermute | solution.py:293
  64.1 9.5 %collective-permute-start.12 = (bf16[512,512]{1,0:T(8,128)(2,1)}, bf16[512,512]{1,0:T(8,128)(2,1)}, u32[]{:S(2)}, u32[]{:S(2)}) collective-permute-start(bf16[512,512]{1,0:T(8,128)(2,1)} %collective-permute-done.10.rest_4_), channel_id=1, source_target_pairs={{0,8},{1,17},{2,10},{3,19},{4,12},{5,21},{6,14},{7,23},{8,24},{9,1... | collective-permute-start | bytes 1572872 | tf_op jit(solution)/shard_map/ppermute | solution.py:293
  64.6 9.5 %collective-permute-start.11 = (bf16[512,512]{1,0:T(8,128)(2,1)}, bf16[512,512]{1,0:T(8,128)(2,1)}, u32[]{:S(2)}, u32[]{:S(2)}) collective-permute-start(bf16[512,512]{1,0:T(8,128)(2,1)} %collective-permute-done.10.rest_4_), channel_id=1, source_target_pairs={{0,1},{1,0},{2,3},{3,2},{4,5},{5,4},{6,7},{7,6},{8,9},{9,8},{10,11... | collective-permute-start | bytes 1572872 | tf_op jit(solution)/shard_map/ppermute | solution.py:293
  65.7 13.5 %collective-permute-start.16 = (bf16[512,512]{1,0:T(8,128)(2,1)}, bf16[512,512]{1,0:T(8,128)(2,1)}, u32[]{:S(2)}, u32[]{:S(2)}) collective-permute-start(bf16[512,512]{1,0:T(8,128)(2,1)} %collective-permute-done.14.rest_8_), channel_id=1, source_target_pairs={{0,8},{1,17},{2,10},{3,19},{4,12},{5,21},{6,14},{7,23},{8,24},{9,1... | collective-permute-start | bytes 1572872 | tf_op jit(solution)/shard_map/ppermute | solution.py:293
  67.2 17.6 %collective-permute-start.20 = (bf16[512,512]{1,0:T(8,128)(2,1)}, bf16[512,512]{1,0:T(8,128)(2,1)}, u32[]{:S(2)}, u32[]{:S(2)}) collective-permute-start(bf16[512,512]{1,0:T(8,128)(2,1)} %collective-permute-done.18.rest_12_), channel_id=1, source_target_pairs={{0,8},{1,17},{2,10},{3,19},{4,12},{5,21},{6,14},{7,23},{8,24},{9,1... | collective-permute-start | bytes 1572872 | tf_op jit(solution)/shard_map/ppermute | solution.py:293
  68.4 33.0 %collective-permute-start.15 = (bf16[512,512]{1,0:T(8,128)(2,1)}, bf16[512,512]{1,0:T(8,128)(2,1)S(1)}, u32[]{:S(2)}, u32[]{:S(2)}) collective-permute-start(bf16[512,512]{1,0:T(8,128)(2,1)} %collective-permute-done.14.rest_8_), channel_id=1, source_target_pairs={{0,1},{1,0},{2,3},{3,2},{4,5},{5,4},{6,7},{7,6},{8,9},{9,8},{10,11... | collective-permute-start | bytes 1572872 | tf_op jit(solution)/shard_map/ppermute | solution.py:293
  73.6 27.4 %collective-permute-start.13 = (bf16[512,512]{1,0:T(8,128)(2,1)}, bf16[512,512]{1,0:T(8,128)(2,1)S(1)}, u32[]{:S(2)}, u32[]{:S(2)}) collective-permute-start(bf16[512,512]{1,0:T(8,128)(2,1)} %collective-permute-done.12.rest_6_), channel_id=1, source_target_pairs={{0,1},{1,0},{2,3},{3,2},{4,5},{5,4},{6,7},{7,6},{8,9},{9,8},{10,11... | collective-permute-start | bytes 1572872 | tf_op jit(solution)/shard_map/ppermute | solution.py:293
  74.1 28.6 %collective-permute-start.19 = (bf16[512,512]{1,0:T(8,128)(2,1)}, bf16[512,512]{1,0:T(8,128)(2,1)S(1)}, u32[]{:S(2)}, u32[]{:S(2)}) collective-permute-start(bf16[512,512]{1,0:T(8,128)(2,1)} %collective-permute-done.18.rest_12_), channel_id=1, source_target_pairs={{0,1},{1,0},{2,3},{3,2},{4,5},{5,4},{6,7},{7,6},{8,9},{9,8},{10,11... | collective-permute-start | bytes 1572872 | tf_op jit(solution)/shard_map/ppermute | solution.py:293
  79.3 22.6 %collective-permute-start.17 = (bf16[512,512]{1,0:T(8,128)(2,1)}, bf16[512,512]{1,0:T(8,128)(2,1)S(1)}, u32[]{:S(2)}, u32[]{:S(2)}) collective-permute-start(bf16[512,512]{1,0:T(8,128)(2,1)} %collective-permute-done.16.rest_10_), channel_id=1, source_target_pairs={{0,1},{1,0},{2,3},{3,2},{4,5},{5,4},{6,7},{7,6},{8,9},{9,8},{10,11... | collective-permute-start | bytes 1572872 | tf_op jit(solution)/shard_map/ppermute | solution.py:293
  84.9 17.9 %collective-permute-start.21 = (bf16[512,512]{1,0:T(8,128)(2,1)}, bf16[512,512]{1,0:T(8,128)(2,1)S(1)}, u32[]{:S(2)}, u32[]{:S(2)}) collective-permute-start(bf16[512,512]{1,0:T(8,128)(2,1)} %collective-permute-done.20.rest_14_), channel_id=1, source_target_pairs={{0,1},{1,0},{2,3},{3,2},{4,5},{5,4},{6,7},{7,6},{8,9},{9,8},{10,11... | collective-permute-start | bytes 1572872 | tf_op jit(solution)/shard_map/ppermute | solution.py:293
  85.1 2.2 %copy-start.1 = (bf16[2048,1024]{1,0:T(8,128)(2,1)S(1)}, bf16[2048,1024]{1,0:T(8,128)(2,1)}, u32[]{:S(2)}) copy-start(bf16[2048,1024]{1,0:T(8,128)(2,1)} %copy-done) | copy-start | bytes 12582916
  87.2 1.6 %copy-start.3 = (bf16[2048,512]{1,0:T(8,128)(2,1)S(1)}, bf16[2048,512]{1,0:T(8,128)(2,1)}, u32[]{:S(2)}) copy-start(bf16[2048,512]{1,0:T(8,128)(2,1)} %copy-done.2) | copy-start | bytes 6291460
  88.8 1.4 %copy-start.5 = (bf16[512,1536]{1,0:T(8,128)(2,1)S(1)}, bf16[512,1536]{1,0:T(8,128)(2,1)}, u32[]{:S(2)}) copy-start(bf16[512,1536]{1,0:T(8,128)(2,1)} %copy-done.4) | copy-start | bytes 4718596
  90.2 0.9 copy-start.11
  91.2 0.8 copy-start.23
  98.8 0.9 copy-start.15
  98.8 1.0 copy-start.17
  98.8 1.0 copy-start.29
  101.0 14.2 %collective-permute-start.5 = (bf16[24,8,512]{2,1,0:T(8,128)(2,1)S(1)}, bf16[24,8,512]{2,1,0:T(8,128)(2,1)S(1)}, u32[]{:S(2)}, u32[]{:S(2)}) collective-permute-start(bf16[24,8,512]{2,1,0:T(8,128)(2,1)S(1)} %maximum_maximum_fusion.1), channel_id=1, source_target_pairs={{0,1},{1,2},{2,3},{3,4},{4,5},{5,6},{6,7},{7,0},{8,9},{9,10},{10,1... | collective-permute-start | bytes 589832 | tf_op jit(solution)/shard_map/ppermute | solution.py:293
  101.4 13.8 %collective-permute-start.4 = (bf16[8,24,512]{2,1,0:T(8,128)(2,1)S(1)}, bf16[8,24,512]{2,1,0:T(8,128)(2,1)S(1)}, u32[]{:S(2)}, u32[]{:S(2)}) collective-permute-start(bf16[8,24,512]{2,1,0:T(8,128)(2,1)S(1)} %pad_maximum_fusion.5), channel_id=1, source_target_pairs={{0,8},{1,9},{2,10},{3,11},{4,12},{5,13},{6,14},{7,15},{8,16},{9,17... | collective-permute-start | bytes 589832 | tf_op jit(solution)/shard_map/ppermute | solution.py:293
  101.9 12.4 %collective-permute-start.3 = (bf16[8,8,512]{2,1,0:T(8,128)(2,1)S(1)}, bf16[8,8,512]{2,1,0:T(8,128)(2,1)S(1)}, u32[]{:S(2)}, u32[]{:S(2)}) collective-permute-start(bf16[8,8,512]{2,1,0:T(8,128)(2,1)S(1)} %slice.72), channel_id=1, source_target_pairs={{0,9},{1,10},{2,11},{3,12},{4,13},{5,14},{6,15},{7,8},{8,17},{9,18... | collective-permute-start | bytes 196616 | tf_op jit(solution)/shard_map/ppermute | solution.py:293
  112.3 6.3 %collective-permute-start.24 = (bf16[8,8,1024]{2,1,0:T(8,128)(2,1)S(1)}, bf16[8,8,1024]{2,1,0:T(8,128)(2,1)S(1)}, u32[]{:S(2)}, u32[]{:S(2)}) collective-permute-start(bf16[8,8,1024]{2,1,0:T(8,128)(2,1)S(1)} %get-tuple-element.46), channel_id=1, source_target_pairs={{0,1},{1,2},{2,3},{3,4},{4,5},{5,6},{6,7},{7,0},{8,9},{9,10},{10,1... | collective-permute-start | bytes 393224 | tf_op jit(solution)/shard_map/ppermute | solution.py:293
  112.8 6.4 %collective-permute-start.23 = (bf16[8,8,1024]{2,1,0:T(8,128)(2,1)S(1)}, bf16[8,8,1024]{2,1,0:T(8,128)(2,1)S(1)}, u32[]{:S(2)}, u32[]{:S(2)}) collective-permute-start(bf16[8,8,1024]{2,1,0:T(8,128)(2,1)S(1)} %get-tuple-element.47), channel_id=1, source_target_pairs={{0,8},{1,9},{2,10},{3,11},{4,12},{5,13},{6,14},{7,15},{8,16},{9,17... | collective-permute-start | bytes 393224 | tf_op jit(solution)/shard_map/ppermute | solution.py:293
  114.3 8.0 %collective-permute-start.22 = (bf16[8,8,1024]{2,1,0:T(8,128)(2,1)S(1)}, bf16[8,8,1024]{2,1,0:T(8,128)(2,1)S(1)}, u32[]{:S(2)}, u32[]{:S(2)}) collective-permute-start(bf16[8,8,1024]{2,1,0:T(8,128)(2,1)S(1)} %get-tuple-element.44), channel_id=1, source_target_pairs={{0,9},{1,10},{2,11},{3,12},{4,13},{5,14},{6,15},{7,8},{8,17},{9,18... | collective-permute-start | bytes 393224 | tf_op jit(solution)/shard_map/ppermute | solution.py:293
  (7 other events, 4.6 us)

commit v3 on v2

--- a/solution.py
+++ b/solution.py
@@ -152,7 +152,9 @@
     size = sum(w.size * 2 for w in weights)
     hbm = pl.BlockSpec(memory_space=pltpu.HBM)
     vmem = pl.BlockSpec(memory_space=pltpu.VMEM)
-    held = [jax.ShapeDtypeStruct(w.shape, BF) for w in weights] if first else []
+    held = [pltpu.VMEM(w.shape, BF) for w in weights] if first else []
+    if first:
+        weights = [pltpu.with_memory_space_constraint(w, pltpu.HBM) for w in weights]
     return pl.pallas_call(
         functools.partial(fine_kernel, masked, first, names, blocks),
         out_shape=[
@@ -202,7 +204,7 @@
     vmem = pl.BlockSpec(memory_space=pltpu.VMEM)
     return pl.pallas_call(
         functools.partial(cut_kernel, tuple(parts)),
-        out_shape=[jax.ShapeDtypeStruct(shape, BF) for shape in shapes],
+        out_shape=[pltpu.VMEM(shape, BF) for shape in shapes],
         in_specs=[pl.BlockSpec(memory_space=pltpu.SMEM)] + [hbm] * len(arrays),
         out_specs=[vmem] * len(shapes),
         scratch_shapes=[pltpu.SemaphoreType.DMA((len(parts),))],
@@ -211,37 +213,64 @@
             flops=0, bytes_accessed=sum(2 * int(np.prod(shape)) for shape in shapes), transcendentals=0
         ),
         name="cut",
-    )(offsets, *arrays)
-
-
-def coarse_kernel(plan, last, table, x_ref, *rest):
-    count = max(entry[0] for entry in plan) + 1
-    pieces = rest[:count]
-    out_ref, xn, qkv, mixed, proj, sem = rest[count:]
-    width = x_ref.shape[1]
-
-    def place(slot, rows, columns):
-        row = pl.multiple_of(table[2 * slot], rows)
-        column = pl.multiple_of(table[2 * slot + 1] * columns, 128)
-        return pl.ds(row, rows), pl.ds(column, columns)
-
-    copies, shards = [], {}
-    for slot, (piece, r, rows, c, columns, shard, which) in enumerate(plan):
-        part = pieces[piece].at[pl.ds(r, rows), pl.ds(c, columns)]
+    )(offsets, *[pltpu.with_memory_space_constraint(array, pltpu.HBM) for array in arrays])
+
+
+def place(table, slot, rows, columns):
+    row = pl.multiple_of(table[2 * slot], rows)
+    column = pl.multiple_of(table[2 * slot + 1] * columns, 128)
+    return pl.ds(row, rows), pl.ds(column, columns)
+
+
+def output_copies(plan, table, pieces, proj, sems):
+    copies = []
+    for slot, piece, r, rows, c, columns, _, which in plan:
         if which == 1:
-            copies.append(pltpu.make_async_copy(part, proj.at[place(slot, rows, columns)], sem.at[len(copies)]))
-        else:
+            part = pieces[piece].at[pl.ds(r, rows), pl.ds(c, columns)]
+            at = place(table, slot, rows, columns)
+            copies.append(pltpu.make_async_copy(part, proj.at[at], sems.at[len(copies)]))
+    return copies
+
+
+def project_shards(plan, table, pieces, xn, qkv):
+    shards = {}
+    for slot, piece, r, rows, c, columns, shard, which in plan:
+        if which == 0:
+            part = pieces[piece].at[pl.ds(r, rows), pl.ds(c, columns)]
             shards.setdefault(shard, []).append((slot, part, rows, columns))
-    for copy in copies:
-        copy.start()
-    xn[...] = norm(x_ref[...].astype(F32))
     for parts in shards.values():
         total = 0.0
         for slot, part, rows, columns in parts:
-            row, column = place(slot, rows, columns)
-            lhs = xn[...] if rows == width else xn[:, row]
+            row, column = place(table, slot, rows, columns)
+            lhs = xn[...] if rows == xn.shape[1] else xn[:, row]
             total = total + dot(lhs, part[...])
         qkv[:, column] = total.astype(BF)
+
+
+def coarse_early_kernel(plan, count, table, x_ref, *rest):
+    pieces = rest[:count]
+    xn, qkv, proj, sems = rest[count:]
+    copies = output_copies(plan, table, pieces, proj, sems)
+    for copy in copies:
+        copy.start()
+    xn[...] = norm(x_ref[...].astype(F32))
+    project_shards(plan, table, pieces, xn, qkv)
+    for copy in copies:
+        copy.wait()
+
+
+def coarse_late_kernel(plan, count, last, table, x_ref, xn, qkv_in, proj_in, *rest):
+    pieces = rest[:count]
+    out_ref, qkv, mixed, proj, sems = rest[count:]
+    base = pltpu.make_async_copy(proj_in, proj, sems.at[0])
+    base.start()
+    qkv[...] = qkv_in[...]
+    project_shards(plan, table, pieces, xn, qkv)
+    base.wait()
+    copies = output_copies(plan, table, pieces, proj, sems)
+    for copy in copies:
+        copy.start()
+    width = x_ref.shape[1]
     attention(qkv, mixed, width, mask_bias(last))
     for copy in copies:
         copy.wait()
@@ -251,28 +280,54 @@
         out_ref[:, cols] = (x_ref[:, cols].astype(F32) + dot(mixed[...], proj[:, cols])).astype(BF)
 
 
-def coarse_window(x, last, table, pieces, plan):
+def split_plan(plan, late):
+    chosen = [(slot, entry) for slot, entry in enumerate(plan) if (entry[5][1] in late[1]) == late[0]]
+    used = sorted({entry[0] for _, entry in chosen})
+    return tuple((slot, used.index(entry[0]), *entry[1:]) for slot, entry in chosen), used
+
+
+def coarse_window(x, last, table, pieces, plan, late):
     width = x.shape[-1]
     vmem = pl.BlockSpec(memory_space=pltpu.VMEM)
     smem = pl.BlockSpec(memory_space=pltpu.SMEM)
+    params = pltpu.CompilerParams(vmem_limit_bytes=24 << 20)
+
+    def cost(share, extra):
+        return pl.CostEstimate(
+            flops=int(6 * TOK * width * width * share + extra * TOK * width * (2 * width + 4 * TOK)),
+            bytes_accessed=int(6 * width * width * share), transcendentals=extra * TOK * TOK * 16)
+
+    early_plan, used = split_plan(plan, (False, late))
+    sent = [pieces[k] for k in used]
+    xn, qkv, proj = pl.pallas_call(
+        functools.partial(coarse_early_kernel, early_plan, len(sent)),
+        out_shape=[
+            pltpu.VMEM((TOK, width), BF), pltpu.VMEM((TOK, 3 * width), BF), pltpu.VMEM((width, width), BF)
+        ],
+        in_specs=[smem, vmem] + [vmem] * len(sent),
+        out_specs=[vmem] * 3,
+        scratch_shapes=[pltpu.SemaphoreType.DMA((len(early_plan),))],
+        compiler_params=params,
+        cost_estimate=cost(0.75, 0),
+        name="coarse_early",
+    )(table, x, *sent)
+    late_plan, used = split_plan(plan, (True, late))
+    sent = [pieces[k] for k in used]
     return pl.pallas_call(
-        functools.partial(coarse_kernel, plan),
+        functools.partial(coarse_late_kernel, late_plan, len(sent)),
         out_shape=jax.ShapeDtypeStruct((TOK, width), BF),
-        in_specs=[smem, smem, vmem] + [vmem] * len(pieces),
+        in_specs=[smem, smem] + [vmem] * (4 + len(sent)),
         out_specs=vmem,
         scratch_shapes=[
-            pltpu.VMEM((TOK, width), BF),
             pltpu.VMEM((TOK, 3 * width), BF),
             pltpu.VMEM((TOK, width), BF),
             pltpu.VMEM((width, width), BF),
-            pltpu.SemaphoreType.DMA((sum(entry[6] for entry in plan),)),
+            pltpu.SemaphoreType.DMA((len(late_plan) + 1,)),
         ],
-        compiler_params=pltpu.CompilerParams(vmem_limit_bytes=24 << 20),
-        cost_estimate=pl.CostEstimate(
-            flops=8 * TOK * width * width, bytes_accessed=8 * width * width, transcendentals=TOK * TOK * 16
-        ),
-        name="coarse",
-    )(last, table, x, *pieces)
+        compiler_params=params,
+        cost_estimate=cost(0.25, 1),
+        name="coarse_late",
+    )(last, table, x, xn, qkv, proj, *sent)
 
 
 def line_ring(count):
@@ -386,7 +441,7 @@
         pieces, plan, table = gather_weights(qkv_coarse, proj_coarse, got[-1], m, n)
     else:
         pieces = [lax.all_gather(w, "lon", axis=1, tiled=True) for w in (qkv_coarse, proj_coarse)]
-        plan = ((0, 0, deep, 0, a * n, 0, 0), (1, 0, deep, 0, b * n, 0, 1))
+        plan = ((0, 0, deep, 0, a * n, (0, 0), 0), (1, 0, deep, 0, b * n, (0, 0), 1))
         table = jnp.zeros((4,), jnp.int32)
 
     fine, merged = {}, {}
@@ -428,7 +483,7 @@
         for j in range(cc):
             block = coarse[i * WIN:(i + 1) * WIN, j * WIN:(j + 1) * WIN].reshape(TOK, wide)
             seam = last if i == cr - 1 else jnp.zeros_like(last)
-            out = coarse_window(block, seam, table, pieces, plan)
+            out = coarse_window(block, seam, table, pieces, plan, (n // 2 - 1,) if direct else ())
             outs[i, j] = out.reshape(WIN, WIN, wide)
     coarse_out = jnp.concatenate(
         [jnp.concatenate([outs[i, j] for j in range(cc)], axis=1) for i in range(cr)], axis=0

time: 124 us -> 119 us (0.960)
  local copies, waits for them, and re-layouts: 23.6 us -> 16.1 us
  Pallas kernels: 34.8 us -> 38 us
    unnamed x60 -> x62, local copies, waits for them, and re-layouts: 21.6 us -> 14 us
    pallas_call x4, Pallas kernels: 22.7 us -> 24.7 us  [fine_window(): pl.pallas_call(functools.partial(fine_kernel, masked, first, names, block...]
    pallas_call x2 -> x3, Pallas kernels: 12.1 us -> 13.4 us  [the longest x1 5.6 us: coarse_window(): pl.pallas_call(functools.partial(coarse_late_kernel, late_plan, len(sent)...]
  transfers between devices with their start and end apart: 25 -> 25, of which waited for: 8 -> 8; matrix products, arithmetic and copies ran while one was open for 3% -> 3% of each run, Pallas kernels for 26% -> 30%
where the time goes in v3:
time: 119 us
  Pallas kernels  38 us (32%)
  waiting for transfers between devices  33.8 us (28%)
  starting transfers between devices  26.7 us (22%)
  local copies, waits for them, and re-layouts  16.1 us (14%)
  other arithmetic  3.2 us (3%)
    ppermute x23, waiting for transfers between devices, send(): return lax.ppermute(value, ('lat', 'lon'), pairs)  33.8 us
    pallas_call x4, Pallas kernels, fine_window(): pl.pallas_call(functools.partial(fine_kernel, masked, first, names, block...  24.7 us
    ppermute x23, starting transfers between devices, send(): return lax.ppermute(value, ('lat', 'lon'), pairs)  24 us
    unnamed x62, local copies, waits for them, and re-layouts  14 us
    pallas_call x1, Pallas kernels, coarse_window(): pl.pallas_call(functools.partial(coarse_late_kernel, late_plan, len(sent)...  5.6 us
    pallas_call x1, Pallas kernels, coarse_window(): pl.pallas_call(functools.partial(coarse_early_kernel, early_plan, len(sen...  4.86 us
    pallas_call x1, Pallas kernels, cut(): pl.pallas_call(functools.partial(cut_kernel, tuple(parts)), out_shape=[pl...  2.89 us
    ppermute x2, starting transfers between devices, shifted(): lax.ppermute(value, axis, [(s, (s + steps) % count) for s in range(count)])  2.75 us
  transfers between devices with their start and end apart: 25, of which 8 were waited for; matrix products, arithmetic and copies ran while one was open for 3% of the time, Pallas kernels for 30%

profile of v3, /device:TPU:0, one launch (start us, length us, event | category | flops | bytes accessed | tf_op | source)
XLA Modules:
  0.0 118.9 jit_solution(1264409720868876008)
XLA Ops:
  0.6 1.3 %constant_dynamic-slice_fusion = s32[1,1]{1,0:T(1,128)} fusion(s32[4,1]{1,0:T(4,128)} %constant.22.clone, s32[]{:T(128)S(6)} %select_n.6), kind=kLoop, calls=%fused_computation.19 | loop fusion | bytes 12 | tf_op jit(solution)/shard_map/dynamic_slice | solution.py:425
  1.9 2.9 %cut.1 = (bf16[32,8,512]{2,1,0:T(8,128)(2,1)}, bf16[8,24,512]{2,1,0:T(8,128)(2,1)}, bf16[8,8,512]{2,1,0:T(8,128)(2,1)S(1)}, bf16[16,16,512]{2,1,0:T(8,128)(2,1)S...) custom-call(s32[1]{0:T(128)} %bitcast.1.offsets, ...), custom_call_target="tpu_custom_call" | custom-call | bytes 1638400 | tf_op jit(solution)/shard_map/cut/pallas_call | solution.py:205
  4.8 0.7 copy-done.17
  5.5 0.6 copy-done.19
  6.2 0.6 copy-done.21
  6.8 0.6 copy-done.23
  7.4 0.6 copy-done.27
  8.1 3.1 %collective-permute-start.10 = (bf16[512,512]{1,0:T(8,128)(2,1)S(1)}, bf16[512,512]{1,0:T(8,128)(2,1)}, u32[]{:S(2)}, u32[]{:S(2)}) collective-permute-start(bf16[512,512]{1,0:T(8,128)(2,1)S(1)} %get-tuple-element.46), channel_id=1, source_target_pairs={{0,2},{1,3},{2,6},{3,7},{4,0},{5,1},{6,4},{7,5},{8,10},{9,11},{10,... | collective-permute-start | bytes 1572872 | tf_op jit(solution)/shard_map/ppermute | solution.py:348
  11.1 1.6 %collective-permute-start = (bf16[32,8,512]{2,1,0:T(8,128)(2,1)}, bf16[32,8,512]{2,1,0:T(8,128)(2,1)}, u32[]{:S(2)}, u32[]{:S(2)}) collective-permute-start(bf16[32,8,512]{2,1,0:T(8,128)(2,1)} %get-tuple-element.27), channel_id=1, source_target_pairs={{0,7},{1,0},{2,1},{3,2},{4,3},{5,4},{6,5},{7,6},{8,15},{9,8},{10,9... | collective-permute-start | bytes 786440 | tf_op jit(solution)/shard_map/ppermute | solution.py:348
  12.8 0.5 collective-permute-start.9
  13.3 2.4 %collective-permute-start.1 = (bf16[8,24,512]{2,1,0:T(8,128)(2,1)}, bf16[8,24,512]{2,1,0:T(8,128)(2,1)}, u32[]{:S(2)}, u32[]{:S(2)}) collective-permute-start(bf16[8,24,512]{2,1,0:T(8,128)(2,1)} %get-tuple-element.28), channel_id=1, source_target_pairs={{0,24},{1,25},{2,26},{3,27},{4,28},{5,29},{6,30},{7,31},{8,0},{9,1... | collective-permute-start | bytes 589832 | tf_op jit(solution)/shard_map/ppermute | solution.py:348
  15.7 8.5 %collective-permute-done.10.rest_4_ = bf16[512,512]{1,0:T(8,128)(2,1)} collective-permute-done((bf16[512,512]{1,0:T(8,128)(2,1)S(1)}, bf16[512,512]{1,0:T(8,128)(2,1)}, u32[]{:S(2)}, u32[]{:S(2)}) %collective-permute-start.10) | collective-permute-done | bytes 524320 | tf_op jit(solution)/shard_map/ppermute | solution.py:348
  24.2 3.4 %collective-permute-start.14 = (bf16[512,512]{1,0:T(8,128)(2,1)}, bf16[512,512]{1,0:T(8,128)(2,1)}, u32[]{:S(2)}, u32[]{:S(2)}) collective-permute-start(bf16[512,512]{1,0:T(8,128)(2,1)} %collective-permute-done.10.rest_4_), channel_id=1, source_target_pairs={{0,2},{1,3},{2,6},{3,7},{4,0},{5,1},{6,4},{7,5},{8,10},{9,11},{10,... | collective-permute-start | bytes 1572872 | tf_op jit(solution)/shard_map/ppermute | solution.py:348
  27.7 0.9 copy-done.18
  28.6 6.4 %fine_first.1 = (bf16[256,512]{1,0:T(8,128)(2,1)S(1)}, bf16[64,1024]{1,0:T(8,128)(2,1)S(1)}, bf16[512,1536]{1,0:T(8,128)(2,1)S(1)}, bf16[512,512]{1,0:T(8,128)(2...) custom-call(s32[1]{0:T(128)} %bitcast.last, ...), custom_call_target="tpu_custom_call" | custom-call | flops 1879048192 | bytes 11272192 | tf_op jit(solution)/shard_map/fine_first/pallas_call | solution.py:158
  35.2 6.2 %fine_plain.1 = (bf16[256,512]{1,0:T(8,128)(2,1)S(1)}, bf16[64,1024]{1,0:T(8,128)(2,1)S(1)}) custom-call(s32[1]{0:T(128)} %bitcast.last, bf16[16,8,512]{2,1,0:T(8,128)(2,1)S(1)} %copy-done.22, bf16[32,8,512]{2,1,0:T(8,128)(2,1)} %collective-permute-done.refs_1_, bf16[512,1536]{1,0:T(8,128)(2,1)S(1)} %get-tuple-element.31.refs_4_.refs_2_, ...), custom_call_target="tpu_custom_call" | custom-call | flops 1879048192 | bytes 11272192 | tf_op jit(solution)/shard_map/fine_plain/pallas_call | solution.py:158
  41.5 3.6 %collective-permute-start.18 = (bf16[512,512]{1,0:T(8,128)(2,1)}, bf16[512,512]{1,0:T(8,128)(2,1)}, u32[]{:S(2)}, u32[]{:S(2)}) collective-permute-start(bf16[512,512]{1,0:T(8,128)(2,1)} %collective-permute-done.14.rest_8_), channel_id=1, source_target_pairs={{0,2},{1,3},{2,6},{3,7},{4,0},{5,1},{6,4},{7,5},{8,10},{9,11},{10,... | collective-permute-start | bytes 1572872 | tf_op jit(solution)/shard_map/ppermute | solution.py:348
  45.1 2.7 %collective-permute-start.6 = (bf16[4,16,1024]{2,1,0:T(8,128)(2,1)S(1)}, bf16[4,16,1024]{2,1,0:T(8,128)(2,1)S(1)}, u32[]{:S(2)}, u32[]{:S(2)}) collective-permute-start(bf16[4,16,1024]{2,1,0:T(8,128)(2,1)S(1)} %pad_maximum_fusion.7), channel_id=1, source_target_pairs={{0,24},{8,0},{16,8},{24,16},{1,25},{9,1},{17,9},{25,17},{2,26},{10... | collective-permute-start | bytes 393224 | tf_op jit(solution)/shard_map/ppermute | solution.py:396
  47.8 5.9 %fine_masked.3 = (bf16[256,512]{1,0:T(8,128)(2,1)S(1)}, bf16[64,1024]{1,0:T(8,128)(2,1)S(1)}) custom-call(s32[1]{0:T(128)} %bitcast.last, bf16[8,16,512]{2,1,0:T(8,128)(2,1)S(1)} %copy-done.20, bf16[8,24,512]{2,1,0:T(8,128)(2,1)} %collective-permute-done.1.refs_2_.refs_1_, bf16[512,1536]{1,0:T(8,128)(2,1)S(1)} %get-tuple-element.31.refs_4_.refs_2_, ...), custom_call_target="tpu_custom_call" | custom-call | flops 1879048192 | bytes 11272192 | tf_op jit(solution)/shard_map/fine_masked/pallas_call | solution.py:158
  53.8 0.7 copy-done.7
  54.5 0.7 copy-done.13
  55.4 3.7 %collective-permute-done.2.refs_3_ = bf16[8,8,512]{2,1,0:T(8,128)(2,1)S(1)} collective-permute-done((bf16[8,8,512]{2,1,0:T(8,128)(2,1)S(1)}, bf16[8,8,512]{2,1,0:T(8,128)(2,1)S(1)}, u32[]{:S(2)}, u32[]{:S(2)}) %collective-permute-start.2) | collective-permute-done | bytes 65568 | tf_op jit(solution)/shard_map/ppermute | solution.py:348
  59.1 0.6 copy-done.25
  60.2 1.1 collective-permute-start.11
  61.3 1.5 %collective-permute-start.16 = (bf16[512,512]{1,0:T(8,128)(2,1)}, bf16[512,512]{1,0:T(8,128)(2,1)}, u32[]{:S(2)}, u32[]{:S(2)}) collective-permute-start(bf16[512,512]{1,0:T(8,128)(2,1)} %collective-permute-done.14.rest_8_), channel_id=1, source_target_pairs={{0,8},{1,17},{2,10},{3,19},{4,12},{5,21},{6,14},{7,23},{8,24},{9,1... | collective-permute-start | bytes 1572872 | tf_op jit(solution)/shard_map/ppermute | solution.py:348
  63.3 0.7 dynamic-slice_bitcast_fusion.table
  64.0 5.2 %collective-permute-done.12.rest_6_ = bf16[512,512]{1,0:T(8,128)(2,1)} collective-permute-done((bf16[512,512]{1,0:T(8,128)(2,1)}, bf16[512,512]{1,0:T(8,128)(2,1)}, u32[]{:S(2)}, u32[]{:S(2)}) %collective-permute-start.12) | collective-permute-done | bytes 524320 | tf_op jit(solution)/shard_map/ppermute | solution.py:348
  69.2 0.5 collective-permute-start.13
  69.7 5.1 %collective-permute-done.16.rest_10_ = bf16[512,512]{1,0:T(8,128)(2,1)} collective-permute-done((bf16[512,512]{1,0:T(8,128)(2,1)}, bf16[512,512]{1,0:T(8,128)(2,1)}, u32[]{:S(2)}, u32[]{:S(2)}) %collective-permute-start.16) | collective-permute-done | bytes 524320 | tf_op jit(solution)/shard_map/ppermute | solution.py:348
  75.3 5.1 %collective-permute-done.20.rest_2_ = bf16[512,512]{1,0:T(8,128)(2,1)} collective-permute-done((bf16[512,512]{1,0:T(8,128)(2,1)}, bf16[512,512]{1,0:T(8,128)(2,1)}, u32[]{:S(2)}, u32[]{:S(2)}) %collective-permute-start.20) | collective-permute-done | bytes 524320 | tf_op jit(solution)/shard_map/ppermute | solution.py:348
  80.7 2.2 %copy-done.1 = bf16[2048,1024]{1,0:T(8,128)(2,1)S(1)} copy-done((bf16[2048,1024]{1,0:T(8,128)(2,1)S(1)}, bf16[2048,1024]{1,0:T(8,128)(2,1)}, u32[]{:S(2)}) %copy-start.1) | copy-done | bytes 4194328
  82.8 1.6 %copy-done.3 = bf16[2048,512]{1,0:T(8,128)(2,1)S(1)} copy-done((bf16[2048,512]{1,0:T(8,128)(2,1)S(1)}, bf16[2048,512]{1,0:T(8,128)(2,1)}, u32[]{:S(2)}) %copy-start.3) | copy-done | bytes 2097176
  84.4 1.4 %copy-done.5 = bf16[512,1536]{1,0:T(8,128)(2,1)S(1)} copy-done((bf16[512,1536]{1,0:T(8,128)(2,1)S(1)}, bf16[512,1536]{1,0:T(8,128)(2,1)}, u32[]{:S(2)}) %copy-start.5) | copy-done | bytes 1572888
  85.8 0.8 copy-done.24
  86.7 0.8 copy-done.26
  87.5 6.1 %fine_masked.2 = (bf16[256,512]{1,0:T(8,128)(2,1)S(1)}, bf16[64,1024]{1,0:T(8,128)(2,1)S(1)}) custom-call(s32[1]{0:T(128)} %bitcast.last, bf16[8,8,512]{2,1,0:T(8,128)(2,1)S(1)} %copy-done.24, bf16[32,8,512]{2,1,0:T(8,128)(2,1)} %collective-permute-done.refs_1_, bf16[8,24,512]{2,1,0:T(8,128)(2,1)} %collective-permute-done.1.refs_2_.refs_1_, ...), custom_call_target="tpu_custom_call" | custom-call | flops 1879048192 | bytes 11272192 | tf_op jit(solution)/shard_map/fine_masked/pallas_call | solution.py:158
  93.7 0.8 copy-done.14
  94.6 1.2 fusion.3
  96.6 0.9 collective-permute-start.3
  97.6 4.9 %coarse_early.1 = (bf16[256,1024]{1,0:T(8,128)(2,1)S(1)}, bf16[256,3072]{1,0:T(8,128)(2,1)S(1)}, bf16[1024,1024]{1,0:T(8,128)(2,1)S(1)}) custom-call(s32[56]{0:T(128)S(1)} %dynamic-slice_bitcast_fusion.table, bf16[256,1024]{1,0:T(8,128)(2,1)S(1)} %bitcast.18, bf16[1024,384]{1,0:T(8,128)(2,1)S(1)} %copy-done.6, ...), custom_call_target="tpu_custom_call" | custom-call | flops 1207959552 | bytes 4718592 | tf_op jit(solution)/shard_map/coarse_early/pallas_call | solution.py:302
  102.4 5.6 %coarse_late.1 = bf16[256,1024]{1,0:T(8,128)(2,1)S(1)} custom-call(s32[1]{0:T(128)} %bitcast.last, s32[56]{0:T(128)S(1)} %dynamic-slice_bitcast_fusion.table, bf16[256,1024]{1,0:T(8,128)(2,1)S(1)} %bitcast.19, bf16[256,1024]{1,0:T(8,128)(2,1)S(1)} %get-tuple-element.47.xn, bf16[256,3072]{1,0:T(8,128)(2,1)S(1)} %get-tuple-element.48.qkv_in, ...), custom_call_target="tpu_custom_call" | custom-call | flops 1207959552 | bytes 1572864 | tf_op jit(solution)/shard_map/coarse_late/pallas_call | solution.py:316
  108.5 1.5 %collective-permute-start.23 = (bf16[8,8,1024]{2,1,0:T(8,128)(2,1)S(1)}, bf16[8,8,1024]{2,1,0:T(8,128)(2,1)S(1)}, u32[]{:S(2)}, u32[]{:S(2)}) collective-permute-start(bf16[8,8,1024]{2,1,0:T(8,128)(2,1)S(1)} %get-tuple-element.53), channel_id=1, source_target_pairs={{0,8},{1,9},{2,10},{3,11},{4,12},{5,13},{6,14},{7,15},{8,16},{9,17... | collective-permute-start | bytes 393224 | tf_op jit(solution)/shard_map/ppermute | solution.py:348
  110.1 0.9 collective-permute-start.22
  110.9 1.1 fusion.2
  112.0 2.4 %collective-permute-done.24 = bf16[8,8,1024]{2,1,0:T(8,128)(2,1)S(1)} collective-permute-done((bf16[8,8,1024]{2,1,0:T(8,128)(2,1)S(1)}, bf16[8,8,1024]{2,1,0:T(8,128)(2,1)S(1)}, u32[]{:S(2)}, u32[]{:S(2)}) %collective-permute-start.24) | collective-permute-done | bytes 131104 | tf_op jit(solution)/shard_map/ppermute | solution.py:348
  114.4 0.6 collective-permute-done.23
  114.9 3.1 %collective-permute-done.22 = bf16[8,8,1024]{2,1,0:T(8,128)(2,1)S(1)} collective-permute-done((bf16[8,8,1024]{2,1,0:T(8,128)(2,1)S(1)}, bf16[8,8,1024]{2,1,0:T(8,128)(2,1)S(1)}, u32[]{:S(2)}, u32[]{:S(2)}) %collective-permute-start.22) | collective-permute-done | bytes 131104 | tf_op jit(solution)/shard_map/ppermute | solution.py:348
  118.0 0.8 maximum_maximum_fusion
  (86 shorter events, 3.5 us)
Async XLA Ops:
  0.6 12.1 %copy-start.6 = (bf16[1024,384]{1,0:T(8,128)(2,1)S(1)}, bf16[1024,384]{1,0:T(8,128)(2,1)}, u32[]{:S(2)}) copy-start(bf16[1024,384]{1,0:T(8,128)(2,1)} %rest_0_.1) | copy-start | bytes 2359300
  8.1 16.2 %collective-permute-start.10 = (bf16[512,512]{1,0:T(8,128)(2,1)S(1)}, bf16[512,512]{1,0:T(8,128)(2,1)}, u32[]{:S(2)}, u32[]{:S(2)}) collective-permute-start(bf16[512,512]{1,0:T(8,128)(2,1)S(1)} %get-tuple-element.46), channel_id=1, source_target_pairs={{0,2},{1,3},{2,6},{3,7},{4,0},{5,1},{6,4},{7,5},{8,10},{9,11},{10,... | collective-permute-start | bytes 1572872 | tf_op jit(solution)/shard_map/ppermute | solution.py:348
  11.1 24.0 %collective-permute-start = (bf16[32,8,512]{2,1,0:T(8,128)(2,1)}, bf16[32,8,512]{2,1,0:T(8,128)(2,1)}, u32[]{:S(2)}, u32[]{:S(2)}) collective-permute-start(bf16[32,8,512]{2,1,0:T(8,128)(2,1)} %get-tuple-element.27), channel_id=1, source_target_pairs={{0,7},{1,0},{2,1},{3,2},{4,3},{5,4},{6,5},{7,6},{8,15},{9,8},{10,9... | collective-permute-start | bytes 786440 | tf_op jit(solution)/shard_map/ppermute | solution.py:348
  12.8 51.2 %collective-permute-start.8 = (bf16[1024,384]{1,0:T(8,128)(2,1)S(1)}, bf16[1024,384]{1,0:T(8,128)(2,1)}, u32[]{:S(2)}, u32[]{:S(2)}) collective-permute-start(bf16[1024,384]{1,0:T(8,128)(2,1)S(1)} %copy-done.6), channel_id=1, source_target_pairs={{0,1},{1,0},{2,3},{3,2},{4,5},{5,4},{6,7},{7,6},{8,9},{9,8},{10,11... | collective-permute-start | bytes 2359304 | tf_op jit(solution)/shard_map/ppermute | solution.py:348
  12.8 47.4 %collective-permute-start.9 = (bf16[1024,128]{1,0:T(8,128)(2,1)}, bf16[1024,128]{1,0:T(8,128)(2,1)}, u32[]{:S(2)}, u32[]{:S(2)}) collective-permute-start(bf16[1024,128]{1,0:T(8,128)(2,1)} %rest_2_.1), channel_id=1, source_target_pairs={{0,1},{1,0},{2,3},{3,2},{4,5},{5,4},{6,7},{7,6},{8,9},{9,8},{10,11... | collective-permute-start | bytes 786440 | tf_op jit(solution)/shard_map/ppermute | solution.py:348
  13.3 34.5 %collective-permute-start.1 = (bf16[8,24,512]{2,1,0:T(8,128)(2,1)}, bf16[8,24,512]{2,1,0:T(8,128)(2,1)}, u32[]{:S(2)}, u32[]{:S(2)}) collective-permute-start(bf16[8,24,512]{2,1,0:T(8,128)(2,1)} %get-tuple-element.28), channel_id=1, source_target_pairs={{0,24},{1,25},{2,26},{3,27},{4,28},{5,29},{6,30},{7,31},{8,0},{9,1... | collective-permute-start | bytes 589832 | tf_op jit(solution)/shard_map/ppermute | solution.py:348
  24.2 17.2 %collective-permute-start.14 = (bf16[512,512]{1,0:T(8,128)(2,1)}, bf16[512,512]{1,0:T(8,128)(2,1)}, u32[]{:S(2)}, u32[]{:S(2)}) collective-permute-start(bf16[512,512]{1,0:T(8,128)(2,1)} %collective-permute-done.10.rest_4_), channel_id=1, source_target_pairs={{0,2},{1,3},{2,6},{3,7},{4,0},{5,1},{6,4},{7,5},{8,10},{9,11},{10,... | collective-permute-start | bytes 1572872 | tf_op jit(solution)/shard_map/ppermute | solution.py:348
  27.7 0.9 copy-start.18
  28.6 6.5 %copy-start.22 = (bf16[16,8,512]{2,1,0:T(8,128)(2,1)S(1)}, bf16[16,8,512]{2,1,0:T(8,128)(2,1)}, u32[]{:S(2)}) copy-start(bf16[16,8,512]{2,1,0:T(8,128)(2,1)} %copy-done.21) | copy-start | bytes 393220
  35.1 6.3 %copy-start.9 = (bf16[256,512]{1,0:T(8,128)(2,1)}, bf16[256,512]{1,0:T(8,128)(2,1)S(1)}, u32[]{:S(2)}) copy-start(bf16[256,512]{1,0:T(8,128)(2,1)S(1)} %get-tuple-element.39) | copy-start | bytes 786436
  35.1 12.7 %copy-start = (bf16[2048,1024]{1,0:T(8,128)(2,1)}, bf16[2048,1024]{1,0:T(8,128)(2,1)S(1)}, u32[]{:S(2)}) copy-start(bf16[2048,1024]{1,0:T(8,128)(2,1)S(1)} %get-tuple-element.35.refs_8_.refs_6_) | copy-start | bytes 12582916
  35.1 12.7 %copy-start.2 = (bf16[2048,512]{1,0:T(8,128)(2,1)}, bf16[2048,512]{1,0:T(8,128)(2,1)S(1)}, u32[]{:S(2)}) copy-start(bf16[2048,512]{1,0:T(8,128)(2,1)S(1)} %get-tuple-element.34.refs_7_.refs_5_) | copy-start | bytes 6291460
  35.1 12.7 %copy-start.4 = (bf16[512,1536]{1,0:T(8,128)(2,1)}, bf16[512,1536]{1,0:T(8,128)(2,1)S(1)}, u32[]{:S(2)}) copy-start(bf16[512,1536]{1,0:T(8,128)(2,1)S(1)} %get-tuple-element.31.refs_4_.refs_2_) | copy-start | bytes 4718596
  35.1 12.6 %copy-start.20 = (bf16[8,16,512]{2,1,0:T(8,128)(2,1)S(1)}, bf16[8,16,512]{2,1,0:T(8,128)(2,1)}, u32[]{:S(2)}) copy-start(bf16[8,16,512]{2,1,0:T(8,128)(2,1)} %copy-done.19) | copy-start | bytes 393220
  41.4 6.3 %copy-start.11 = (bf16[256,512]{1,0:T(8,128)(2,1)}, bf16[256,512]{1,0:T(8,128)(2,1)S(1)}, u32[]{:S(2)}) copy-start(bf16[256,512]{1,0:T(8,128)(2,1)S(1)} %get-tuple-element.41) | copy-start | bytes 786436
  41.4 12.3 %copy-start.15 = (bf16[64,1024]{1,0:T(8,128)(2,1)}, bf16[64,1024]{1,0:T(8,128)(2,1)S(1)}, u32[]{:S(2)}) copy-start(bf16[64,1024]{1,0:T(8,128)(2,1)S(1)} %get-tuple-element.43) | copy-start | bytes 393220
  41.5 21.4 %collective-permute-start.18 = (bf16[512,512]{1,0:T(8,128)(2,1)}, bf16[512,512]{1,0:T(8,128)(2,1)}, u32[]{:S(2)}, u32[]{:S(2)}) collective-permute-start(bf16[512,512]{1,0:T(8,128)(2,1)} %collective-permute-done.14.rest_8_), channel_id=1, source_target_pairs={{0,2},{1,3},{2,6},{3,7},{4,0},{5,1},{6,4},{7,5},{8,10},{9,11},{10,... | collective-permute-start | bytes 1572872 | tf_op jit(solution)/shard_map/ppermute | solution.py:348
  45.1 10.1 %collective-permute-start.6 = (bf16[4,16,1024]{2,1,0:T(8,128)(2,1)S(1)}, bf16[4,16,1024]{2,1,0:T(8,128)(2,1)S(1)}, u32[]{:S(2)}, u32[]{:S(2)}) collective-permute-start(bf16[4,16,1024]{2,1,0:T(8,128)(2,1)S(1)} %pad_maximum_fusion.7), channel_id=1, source_target_pairs={{0,24},{8,0},{16,8},{24,16},{1,25},{9,1},{17,9},{25,17},{2,26},{10... | collective-permute-start | bytes 393224 | tf_op jit(solution)/shard_map/ppermute | solution.py:396
  47.8 7.6 %copy-start.28 = (bf16[8,8,512]{2,1,0:T(8,128)(2,1)S(1)}, bf16[8,8,512]{2,1,0:T(8,128)(2,1)}, u32[]{:S(2)}) copy-start(bf16[8,8,512]{2,1,0:T(8,128)(2,1)} %copy-done.27) | copy-start | bytes 196612
  55.2 4.0 %copy-start.29 = (bf16[4,16,1024]{2,1,0:T(8,128)(2,1)}, bf16[4,16,1024]{2,1,0:T(8,128)(2,1)S(1)}, u32[]{:S(2)}) copy-start(bf16[4,16,1024]{2,1,0:T(8,128)(2,1)S(1)} %collective-permute-done.6) | copy-start | bytes 393220
  55.3 6.0 %collective-permute-start.7 = (bf16[16,4,1024]{2,1,0:T(4,128)(2,1)S(1)}, bf16[16,4,1024]{2,1,0:T(4,128)(2,1)}, u32[]{:S(2)}, u32[]{:S(2)}) collective-permute-start(bf16[16,4,1024]{2,1,0:T(4,128)(2,1)S(1)} %fusion.5), channel_id=1, source_target_pairs={{0,7},{1,0},{2,1},{3,2},{4,3},{5,4},{6,5},{7,6},{8,15},{9,8},{10,9... | collective-permute-start | bytes 393224 | tf_op jit(solution)/shard_map/ppermute | solution.py:396
  55.4 3.7 %collective-permute-start.2 = (bf16[8,8,512]{2,1,0:T(8,128)(2,1)S(1)}, bf16[8,8,512]{2,1,0:T(8,128)(2,1)S(1)}, u32[]{:S(2)}, u32[]{:S(2)}) collective-permute-start(bf16[8,8,512]{2,1,0:T(8,128)(2,1)S(1)} %copy-done.28), channel_id=1, source_target_pairs={{0,31},{1,24},{2,25},{3,26},{4,27},{5,28},{6,29},{7,30},{8,7},{9,0... | collective-permute-start | bytes 196616 | tf_op jit(solution)/shard_map/ppermute | solution.py:348
  59.7 9.5 %collective-permute-start.12 = (bf16[512,512]{1,0:T(8,128)(2,1)}, bf16[512,512]{1,0:T(8,128)(2,1)}, u32[]{:S(2)}, u32[]{:S(2)}) collective-permute-start(bf16[512,512]{1,0:T(8,128)(2,1)} %collective-permute-done.10.rest_4_), channel_id=1, source_target_pairs={{0,8},{1,17},{2,10},{3,19},{4,12},{5,21},{6,14},{7,23},{8,24},{9,1... | collective-permute-start | bytes 1572872 | tf_op jit(solution)/shard_map/ppermute | solution.py:348
  60.2 9.5 %collective-permute-start.11 = (bf16[512,512]{1,0:T(8,128)(2,1)}, bf16[512,512]{1,0:T(8,128)(2,1)}, u32[]{:S(2)}, u32[]{:S(2)}) collective-permute-start(bf16[512,512]{1,0:T(8,128)(2,1)} %collective-permute-done.10.rest_4_), channel_id=1, source_target_pairs={{0,1},{1,0},{2,3},{3,2},{4,5},{5,4},{6,7},{7,6},{8,9},{9,8},{10,11... | collective-permute-start | bytes 1572872 | tf_op jit(solution)/shard_map/ppermute | solution.py:348
  61.3 13.5 %collective-permute-start.16 = (bf16[512,512]{1,0:T(8,128)(2,1)}, bf16[512,512]{1,0:T(8,128)(2,1)}, u32[]{:S(2)}, u32[]{:S(2)}) collective-permute-start(bf16[512,512]{1,0:T(8,128)(2,1)} %collective-permute-done.14.rest_8_), channel_id=1, source_target_pairs={{0,8},{1,17},{2,10},{3,19},{4,12},{5,21},{6,14},{7,23},{8,24},{9,1... | collective-permute-start | bytes 1572872 | tf_op jit(solution)/shard_map/ppermute | solution.py:348
  62.8 17.6 %collective-permute-start.20 = (bf16[512,512]{1,0:T(8,128)(2,1)}, bf16[512,512]{1,0:T(8,128)(2,1)}, u32[]{:S(2)}, u32[]{:S(2)}) collective-permute-start(bf16[512,512]{1,0:T(8,128)(2,1)} %collective-permute-done.18.rest_0_), channel_id=1, source_target_pairs={{0,8},{1,17},{2,10},{3,19},{4,12},{5,21},{6,14},{7,23},{8,24},{9,1... | collective-permute-start | bytes 1572872 | tf_op jit(solution)/shard_map/ppermute | solution.py:348
  64.0 32.2 %collective-permute-start.15 = (bf16[512,512]{1,0:T(8,128)(2,1)}, bf16[512,512]{1,0:T(8,128)(2,1)S(1)}, u32[]{:S(2)}, u32[]{:S(2)}) collective-permute-start(bf16[512,512]{1,0:T(8,128)(2,1)} %collective-permute-done.14.rest_8_), channel_id=1, source_target_pairs={{0,1},{1,0},{2,3},{3,2},{4,5},{5,4},{6,7},{7,6},{8,9},{9,8},{10,11... | collective-permute-start | bytes 1572872 | tf_op jit(solution)/shard_map/ppermute | solution.py:348
  69.2 26.6 %collective-permute-start.13 = (bf16[512,512]{1,0:T(8,128)(2,1)}, bf16[512,512]{1,0:T(8,128)(2,1)S(1)}, u32[]{:S(2)}, u32[]{:S(2)}) collective-permute-start(bf16[512,512]{1,0:T(8,128)(2,1)} %collective-permute-done.12.rest_6_), channel_id=1, source_target_pairs={{0,1},{1,0},{2,3},{3,2},{4,5},{5,4},{6,7},{7,6},{8,9},{9,8},{10,11... | collective-permute-start | bytes 1572872 | tf_op jit(solution)/shard_map/ppermute | solution.py:348
  69.7 32.7 %collective-permute-start.19 = (bf16[512,512]{1,0:T(8,128)(2,1)}, bf16[512,512]{1,0:T(8,128)(2,1)S(1)}, u32[]{:S(2)}, u32[]{:S(2)}) collective-permute-start(bf16[512,512]{1,0:T(8,128)(2,1)} %collective-permute-done.18.rest_0_), channel_id=1, source_target_pairs={{0,1},{1,0},{2,3},{3,2},{4,5},{5,4},{6,7},{7,6},{8,9},{9,8},{10,11... | collective-permute-start | bytes 1572872 | tf_op jit(solution)/shard_map/ppermute | solution.py:348
  74.8 21.8 %collective-permute-start.17 = (bf16[512,512]{1,0:T(8,128)(2,1)}, bf16[512,512]{1,0:T(8,128)(2,1)S(1)}, u32[]{:S(2)}, u32[]{:S(2)}) collective-permute-start(bf16[512,512]{1,0:T(8,128)(2,1)} %collective-permute-done.16.rest_10_), channel_id=1, source_target_pairs={{0,1},{1,0},{2,3},{3,2},{4,5},{5,4},{6,7},{7,6},{8,9},{9,8},{10,11... | collective-permute-start | bytes 1572872 | tf_op jit(solution)/shard_map/ppermute | solution.py:348
  80.5 22.0 %collective-permute-start.21 = (bf16[512,512]{1,0:T(8,128)(2,1)}, bf16[512,512]{1,0:T(8,128)(2,1)S(1)}, u32[]{:S(2)}, u32[]{:S(2)}) collective-permute-start(bf16[512,512]{1,0:T(8,128)(2,1)} %collective-permute-done.20.rest_2_), channel_id=1, source_target_pairs={{0,1},{1,0},{2,3},{3,2},{4,5},{5,4},{6,7},{7,6},{8,9},{9,8},{10,11... | collective-permute-start | bytes 1572872 | tf_op jit(solution)/shard_map/ppermute | solution.py:348
  80.7 2.2 %copy-start.1 = (bf16[2048,1024]{1,0:T(8,128)(2,1)S(1)}, bf16[2048,1024]{1,0:T(8,128)(2,1)}, u32[]{:S(2)}) copy-start(bf16[2048,1024]{1,0:T(8,128)(2,1)} %copy-done) | copy-start | bytes 12582916
  82.8 1.6 %copy-start.3 = (bf16[2048,512]{1,0:T(8,128)(2,1)S(1)}, bf16[2048,512]{1,0:T(8,128)(2,1)}, u32[]{:S(2)}) copy-start(bf16[2048,512]{1,0:T(8,128)(2,1)} %copy-done.2) | copy-start | bytes 6291460
  84.4 1.4 %copy-start.5 = (bf16[512,1536]{1,0:T(8,128)(2,1)S(1)}, bf16[512,1536]{1,0:T(8,128)(2,1)}, u32[]{:S(2)}) copy-start(bf16[512,1536]{1,0:T(8,128)(2,1)} %copy-done.4) | copy-start | bytes 4718596
  85.8 0.8 copy-start.24
  86.7 0.8 copy-start.26
  87.5 6.1 %copy-start.8 = (bf16[256,512]{1,0:T(8,128)(2,1)S(1)}, bf16[256,512]{1,0:T(8,128)(2,1)}, u32[]{:S(2)}) copy-start(bf16[256,512]{1,0:T(8,128)(2,1)} %copy-done.7) | copy-start | bytes 786436
  87.5 6.1 %copy-start.10 = (bf16[256,512]{1,0:T(8,128)(2,1)S(1)}, bf16[256,512]{1,0:T(8,128)(2,1)}, u32[]{:S(2)}) copy-start(bf16[256,512]{1,0:T(8,128)(2,1)} %copy-done.9) | copy-start | bytes 786436
  87.5 6.2 %copy-start.12 = (bf16[256,512]{1,0:T(8,128)(2,1)S(1)}, bf16[256,512]{1,0:T(8,128)(2,1)}, u32[]{:S(2)}) copy-start(bf16[256,512]{1,0:T(8,128)(2,1)} %copy-done.11) | copy-start | bytes 786436
  93.6 0.9 copy-start.14
  93.6 1.0 copy-start.16
  93.6 1.0 copy-start.30
  95.8 15.1 %collective-permute-start.5 = (bf16[24,8,512]{2,1,0:T(8,128)(2,1)S(1)}, bf16[24,8,512]{2,1,0:T(8,128)(2,1)S(1)}, u32[]{:S(2)}, u32[]{:S(2)}) collective-permute-start(bf16[24,8,512]{2,1,0:T(8,128)(2,1)S(1)} %maximum_maximum_fusion.1), channel_id=1, source_target_pairs={{0,1},{1,2},{2,3},{3,4},{4,5},{5,6},{6,7},{7,0},{8,9},{9,10},{10,1... | collective-permute-start | bytes 589832 | tf_op jit(solution)/shard_map/ppermute | solution.py:348
  96.2 14.7 %collective-permute-start.4 = (bf16[8,24,512]{2,1,0:T(8,128)(2,1)S(1)}, bf16[8,24,512]{2,1,0:T(8,128)(2,1)S(1)}, u32[]{:S(2)}, u32[]{:S(2)}) collective-permute-start(bf16[8,24,512]{2,1,0:T(8,128)(2,1)S(1)} %pad_maximum_fusion.5), channel_id=1, source_target_pairs={{0,8},{1,9},{2,10},{3,11},{4,12},{5,13},{6,14},{7,15},{8,16},{9,17... | collective-permute-start | bytes 589832 | tf_op jit(solution)/shard_map/ppermute | solution.py:348
  96.6 13.4 %collective-permute-start.3 = (bf16[8,8,512]{2,1,0:T(8,128)(2,1)S(1)}, bf16[8,8,512]{2,1,0:T(8,128)(2,1)S(1)}, u32[]{:S(2)}, u32[]{:S(2)}) collective-permute-start(bf16[8,8,512]{2,1,0:T(8,128)(2,1)S(1)} %slice.72), channel_id=1, source_target_pairs={{0,9},{1,10},{2,11},{3,12},{4,13},{5,14},{6,15},{7,8},{8,17},{9,18... | collective-permute-start | bytes 196616 | tf_op jit(solution)/shard_map/ppermute | solution.py:348
  108.1 6.3 %collective-permute-start.24 = (bf16[8,8,1024]{2,1,0:T(8,128)(2,1)S(1)}, bf16[8,8,1024]{2,1,0:T(8,128)(2,1)S(1)}, u32[]{:S(2)}, u32[]{:S(2)}) collective-permute-start(bf16[8,8,1024]{2,1,0:T(8,128)(2,1)S(1)} %get-tuple-element.52), channel_id=1, source_target_pairs={{0,1},{1,2},{2,3},{3,4},{4,5},{5,6},{6,7},{7,0},{8,9},{9,10},{10,1... | collective-permute-start | bytes 393224 | tf_op jit(solution)/shard_map/ppermute | solution.py:348
  108.5 6.4 %collective-permute-start.23 = (bf16[8,8,1024]{2,1,0:T(8,128)(2,1)S(1)}, bf16[8,8,1024]{2,1,0:T(8,128)(2,1)S(1)}, u32[]{:S(2)}, u32[]{:S(2)}) collective-permute-start(bf16[8,8,1024]{2,1,0:T(8,128)(2,1)S(1)} %get-tuple-element.53), channel_id=1, source_target_pairs={{0,8},{1,9},{2,10},{3,11},{4,12},{5,13},{6,14},{7,15},{8,16},{9,17... | collective-permute-start | bytes 393224 | tf_op jit(solution)/shard_map/ppermute | solution.py:348
  110.1 8.0 %collective-permute-start.22 = (bf16[8,8,1024]{2,1,0:T(8,128)(2,1)S(1)}, bf16[8,8,1024]{2,1,0:T(8,128)(2,1)S(1)}, u32[]{:S(2)}, u32[]{:S(2)}) collective-permute-start(bf16[8,8,1024]{2,1,0:T(8,128)(2,1)S(1)} %get-tuple-element.50), channel_id=1, source_target_pairs={{0,9},{1,10},{2,11},{3,12},{4,13},{5,14},{6,15},{7,8},{8,17},{9,18... | collective-permute-start | bytes 393224 | tf_op jit(solution)/shard_map/ppermute | solution.py:348
  (8 other events, 5.2 us)

commit v4 on v3

--- a/solution.py
+++ b/solution.py
@@ -55,10 +55,10 @@
         slab_attention(qkv, mixed, at, width, bias)
 
 
-def mask_bias(last_ref):
+def mask_bias(here, seam):
     lead = lax.broadcasted_iota(jnp.int32, (TOK, TOK), 0) < TOK // 2
     other = lax.broadcasted_iota(jnp.int32, (TOK, TOK), 1) < TOK // 2
-    return jnp.where(lead == other, 0.0, jnp.where(last_ref[0] > 0, NEG, 0.0))
+    return jnp.where(lead == other, 0.0, jnp.where(here[0] == seam, NEG, 0.0))
 
 
 def window_blocks(i, j, rows, cols):
@@ -78,10 +78,11 @@
     return out
 
 
-def fine_kernel(masked, first, names, blocks, last, *refs):
+def fine_kernel(masked, first, names, blocks, wr, wc, ends, last, *refs):
     count = len(names)
     sources = dict(zip(names, refs[:count]))
     weights, refs = refs[count:count + 5], refs[count + 5:]
+    edges, refs = refs[:ends], refs[ends:]
     out_ref, merged_ref = refs[:2]
     qkv, mixed, wide, window, sems = refs[-5:]
     loads = []
@@ -106,7 +107,7 @@
     for part in range(3):
         cols = slice(part * width, (part + 1) * width)
         qkv[:, cols] = dot(normed, vq[:, cols]).astype(BF)
-    attention(qkv, mixed, width, mask_bias(last) if masked else None)
+    attention(qkv, mixed, width, mask_bias(last, masked) if masked is not None else None)
     ready(1)
     attended = (x + dot(mixed[...], vp[...])).astype(BF).astype(F32)
     normed = norm(attended)
@@ -119,6 +120,16 @@
         total = total + dot(hidden, vd[at:at + step, :])
     fine = total.astype(BF)
     out_ref[...] = fine
+    if ends:
+        own = fine.reshape(WIN, WIN, width)
+        to_e, to_s, to_d = refs[2:5]
+        for at in range(wr - 1):
+            to_e[at * WIN:(at + 1) * WIN] = edges[at][:, HALF:]
+        to_e[(wr - 1) * WIN:] = own[:HALF, HALF:]
+        for at in range(wc - 1):
+            to_s[:, at * WIN:(at + 1) * WIN] = edges[wr - 1 + at][HALF:]
+        to_s[:, (wc - 1) * WIN:] = own[HALF:, :HALF]
+        to_d[...] = own[HALF:, HALF:]
     for c in range(width // 128):
         wide[c] = fine[:, c * 128:(c + 1) * 128].astype(F32)
     groups = []
@@ -140,7 +151,7 @@
     merged_ref[...] = merged.astype(BF)
 
 
-def fine_window(i, j, arrays, last, weights, masked, first):
+def fine_window(i, j, arrays, last, weights, masked, first, edges=None):
     rows, cols, width = arrays["shape"]
     wide = weights[-1].shape[1]
     blocks = window_blocks(i, j, rows, cols)
@@ -150,20 +161,26 @@
     names = tuple(dict.fromkeys(block[0] for block in blocks))
     flops = 2 * TOK * width * (3 * width + width + 4 * width * 2) + TOK * 2 * width * wide
     size = sum(w.size * 2 for w in weights)
+    wr, wc = rows // WIN, cols // WIN
+    edges = edges or []
+    sends = []
+    if edges:
+        sends = [(rows - HALF, HALF, width), (HALF, cols - HALF, width), (HALF, HALF, width)]
     hbm = pl.BlockSpec(memory_space=pltpu.HBM)
     vmem = pl.BlockSpec(memory_space=pltpu.VMEM)
     held = [pltpu.VMEM(w.shape, BF) for w in weights] if first else []
     if first:
         weights = [pltpu.with_memory_space_constraint(w, pltpu.HBM) for w in weights]
     return pl.pallas_call(
-        functools.partial(fine_kernel, masked, first, names, blocks),
+        functools.partial(fine_kernel, masked, first, names, blocks, wr, wc, len(edges)),
         out_shape=[
             jax.ShapeDtypeStruct((TOK, width), BF),
             jax.ShapeDtypeStruct((TOK // 4, wide), BF),
         ]
-        + held,
-        in_specs=[pl.BlockSpec(memory_space=pltpu.SMEM)] + [vmem] * len(names) + [hbm if first else vmem] * 5,
-        out_specs=[vmem] * (2 + len(held)),
+        + held
+        + [pltpu.VMEM(shape, BF) for shape in sends],
+        in_specs=[pl.BlockSpec(memory_space=pltpu.SMEM)] + [vmem] * len(names) + [hbm if first else vmem] * 5 + [vmem] * len(edges),
+        out_specs=[vmem] * (2 + len(held) + len(sends)),
         scratch_shapes=[
             pltpu.VMEM((TOK, 3 * width), BF),
             pltpu.VMEM((TOK, width), BF),
@@ -171,15 +188,15 @@
             pltpu.VMEM((WIN, WIN, width), BF),
             pltpu.SemaphoreType.DMA((5,)),
         ],
-        compiler_params=pltpu.CompilerParams(vmem_limit_bytes=24 << 20),
+        compiler_params=pltpu.CompilerParams(vmem_limit_bytes=14 << 20),
         cost_estimate=pl.CostEstimate(
             flops=flops, bytes_accessed=size + 3 * TOK * width * 2, transcendentals=TOK * 4 * width * 2
         ),
-        name="fine_first" if first else "fine_masked" if masked else "fine_plain",
-    )(last, *[arrays[name] for name in names], *weights)
-
-
-def cut_kernel(parts, offsets, *refs):
+        name="fine_first" if first else "fine_masked" if masked is not None else "fine_plain",
+    )(last, *[arrays[name] for name in names], *weights, *edges)
+
+
+def cut_kernel(parts, starts, here, *refs):
     arrays = max(part[0] for part in parts) + 1
     sems = refs[-1]
     copies = []
@@ -187,7 +204,7 @@
         where = []
         for start, size in region:
             if start is None:
-                start = pl.multiple_of(offsets[0], size)
+                start = pl.multiple_of(pick(here[0], starts), size)
             where.append(pl.ds(start, size))
         src, dst = refs[source].at[tuple(where)], refs[arrays + out]
         if column is not None:
@@ -199,11 +216,11 @@
         copy.wait()
 
 
-def cut(offsets, arrays, parts, shapes):
+def cut(here, starts, arrays, parts, shapes):
     hbm = pl.BlockSpec(memory_space=pltpu.HBM)
     vmem = pl.BlockSpec(memory_space=pltpu.VMEM)
     return pl.pallas_call(
-        functools.partial(cut_kernel, tuple(parts)),
+        functools.partial(cut_kernel, tuple(parts), starts),
         out_shape=[pltpu.VMEM(shape, BF) for shape in shapes],
         in_specs=[pl.BlockSpec(memory_space=pltpu.SMEM)] + [hbm] * len(arrays),
         out_specs=[vmem] * len(shapes),
@@ -213,65 +230,76 @@
             flops=0, bytes_accessed=sum(2 * int(np.prod(shape)) for shape in shapes), transcendentals=0
         ),
         name="cut",
-    )(offsets, *[pltpu.with_memory_space_constraint(array, pltpu.HBM) for array in arrays])
-
-
-def place(table, slot, rows, columns):
-    row = pl.multiple_of(table[2 * slot], rows)
-    column = pl.multiple_of(table[2 * slot + 1] * columns, 128)
+    )(here, *[pltpu.with_memory_space_constraint(array, pltpu.HBM) for array in arrays])
+
+
+def pick(index, values):
+    out = jnp.int32(values[0])
+    for at in range(1, len(values)):
+        out = jnp.where(index == at, jnp.int32(values[at]), out)
+    return out
+
+
+def place(here, spot, rows, columns):
+    row = pl.multiple_of(pick(here[0], spot[0]), rows)
+    column = pl.multiple_of(pick(here[1], spot[1]) * columns, 128)
     return pl.ds(row, rows), pl.ds(column, columns)
 
 
-def output_copies(plan, table, pieces, proj, sems):
+def output_copies(plan, here, pieces, proj, sems):
     copies = []
-    for slot, piece, r, rows, c, columns, _, which in plan:
+    for piece, r, rows, c, columns, _, which, spot in plan:
         if which == 1:
             part = pieces[piece].at[pl.ds(r, rows), pl.ds(c, columns)]
-            at = place(table, slot, rows, columns)
+            at = place(here, spot, rows, columns)
             copies.append(pltpu.make_async_copy(part, proj.at[at], sems.at[len(copies)]))
     return copies
 
 
-def project_shards(plan, table, pieces, xn, qkv):
+def project_shards(plan, here, pieces, xn, qkv):
     shards = {}
-    for slot, piece, r, rows, c, columns, shard, which in plan:
+    for piece, r, rows, c, columns, shard, which, spot in plan:
         if which == 0:
             part = pieces[piece].at[pl.ds(r, rows), pl.ds(c, columns)]
-            shards.setdefault(shard, []).append((slot, part, rows, columns))
+            shards.setdefault(shard, []).append((spot, part, rows, columns))
     for parts in shards.values():
         total = 0.0
-        for slot, part, rows, columns in parts:
-            row, column = place(table, slot, rows, columns)
+        for spot, part, rows, columns in parts:
+            row, column = place(here, spot, rows, columns)
             lhs = xn[...] if rows == xn.shape[1] else xn[:, row]
             total = total + dot(lhs, part[...])
         qkv[:, column] = total.astype(BF)
 
 
-def coarse_early_kernel(plan, count, table, x_ref, *rest):
-    pieces = rest[:count]
-    xn, qkv, proj, sems = rest[count:]
-    copies = output_copies(plan, table, pieces, proj, sems)
+def coarse_early_kernel(plan, count, blocks, here, *rest):
+    pieces, rest = rest[:count], rest[count:]
+    x, xn, qkv, proj, window, sems = rest[-6:]
+    copies = output_copies(plan, here, pieces, proj, sems)
     for copy in copies:
         copy.start()
-    xn[...] = norm(x_ref[...].astype(F32))
-    project_shards(plan, table, pieces, xn, qkv)
+    for source, r, c, to_r, to_c, nr, nc in blocks:
+        window[to_r:to_r + nr, to_c:to_c + nc] = rest[source][r:r + nr, c:c + nc]
+    value = window[...].reshape(x.shape)
+    x[...] = value
+    xn[...] = norm(value.astype(F32))
+    project_shards(plan, here, pieces, xn, qkv)
     for copy in copies:
         copy.wait()
 
 
-def coarse_late_kernel(plan, count, last, table, x_ref, xn, qkv_in, proj_in, *rest):
+def coarse_late_kernel(plan, count, seam, here, x_ref, xn, qkv_in, proj_in, *rest):
     pieces = rest[:count]
     out_ref, qkv, mixed, proj, sems = rest[count:]
     base = pltpu.make_async_copy(proj_in, proj, sems.at[0])
     base.start()
     qkv[...] = qkv_in[...]
-    project_shards(plan, table, pieces, xn, qkv)
+    project_shards(plan, here, pieces, xn, qkv)
     base.wait()
-    copies = output_copies(plan, table, pieces, proj, sems)
+    copies = output_copies(plan, here, pieces, proj, sems)
     for copy in copies:
         copy.start()
     width = x_ref.shape[1]
-    attention(qkv, mixed, width, mask_bias(last))
+    attention(qkv, mixed, width, mask_bias(here, seam) if seam is not None else None)
     for copy in copies:
         copy.wait()
     step = width // 2
@@ -281,16 +309,16 @@
 
 
 def split_plan(plan, late):
-    chosen = [(slot, entry) for slot, entry in enumerate(plan) if (entry[5][1] in late[1]) == late[0]]
-    used = sorted({entry[0] for _, entry in chosen})
-    return tuple((slot, used.index(entry[0]), *entry[1:]) for slot, entry in chosen), used
-
-
-def coarse_window(x, last, table, pieces, plan, late):
-    width = x.shape[-1]
+    chosen = [entry for entry in plan if (entry[5][1] in late[1]) == late[0]]
+    used = sorted({entry[0] for entry in chosen})
+    return tuple((used.index(entry[0]), *entry[1:]) for entry in chosen), used
+
+
+def coarse_window(arrays, blocks, seam, here, pieces, plan, late):
+    width = arrays[0].shape[-1]
     vmem = pl.BlockSpec(memory_space=pltpu.VMEM)
     smem = pl.BlockSpec(memory_space=pltpu.SMEM)
-    params = pltpu.CompilerParams(vmem_limit_bytes=24 << 20)
+    params = pltpu.CompilerParams(vmem_limit_bytes=14 << 20)
 
     def cost(share, extra):
         return pl.CostEstimate(
@@ -299,24 +327,24 @@
 
     early_plan, used = split_plan(plan, (False, late))
     sent = [pieces[k] for k in used]
-    xn, qkv, proj = pl.pallas_call(
-        functools.partial(coarse_early_kernel, early_plan, len(sent)),
+    x, xn, qkv, proj = pl.pallas_call(
+        functools.partial(coarse_early_kernel, early_plan, len(sent), blocks),
         out_shape=[
-            pltpu.VMEM((TOK, width), BF), pltpu.VMEM((TOK, 3 * width), BF), pltpu.VMEM((width, width), BF)
+            pltpu.VMEM((TOK, width), BF), pltpu.VMEM((TOK, width), BF), pltpu.VMEM((TOK, 3 * width), BF), pltpu.VMEM((width, width), BF)
         ],
-        in_specs=[smem, vmem] + [vmem] * len(sent),
-        out_specs=[vmem] * 3,
-        scratch_shapes=[pltpu.SemaphoreType.DMA((len(early_plan),))],
+        in_specs=[smem] + [vmem] * (len(sent) + len(arrays)),
+        out_specs=[vmem] * 4,
+        scratch_shapes=[pltpu.VMEM((WIN, WIN, width), BF), pltpu.SemaphoreType.DMA((len(early_plan),))],
         compiler_params=params,
         cost_estimate=cost(0.75, 0),
         name="coarse_early",
-    )(table, x, *sent)
+    )(here, *sent, *arrays)
     late_plan, used = split_plan(plan, (True, late))
     sent = [pieces[k] for k in used]
     return pl.pallas_call(
-        functools.partial(coarse_late_kernel, late_plan, len(sent)),
+        functools.partial(coarse_late_kernel, late_plan, len(sent), seam),
         out_shape=jax.ShapeDtypeStruct((TOK, width), BF),
-        in_specs=[smem, smem] + [vmem] * (4 + len(sent)),
+        in_specs=[smem] + [vmem] * (4 + len(sent)),
         out_specs=vmem,
         scratch_shapes=[
             pltpu.VMEM((TOK, 3 * width), BF),
@@ -327,7 +355,28 @@
         compiler_params=params,
         cost_estimate=cost(0.25, 1),
         name="coarse_late",
-    )(last, table, x, xn, qkv, proj, *sent)
+    )(here, x, xn, qkv, proj, *sent)
+
+
+def coarse_blocks(i, j, wr, wc):
+    def segments(start):
+        out, at = [], start
+        while at < start + WIN:
+            size = min(HALF - at % HALF, start + WIN - at)
+            out.append((at // HALF, at % HALF, at - start, size))
+            at += size
+        return out
+
+    blocks = []
+    for p, r, to_r, nr in segments(QUART + i * WIN):
+        for q, c, to_c, nc in segments(QUART + j * WIN):
+            if q == wc:
+                blocks.append((wr * wc + 1, i * WIN + to_r, 0, to_r, to_c, nr, nc))
+            elif p == wr:
+                blocks.append((wr * wc, 0, q * HALF + c, to_r, to_c, nr, nc))
+            else:
+                blocks.append((p * wc + q, r, c, to_r, to_c, nr, nc))
+    return tuple(blocks)
 
 
 def line_ring(count):
@@ -366,29 +415,24 @@
     def swap(value):
         return send(value, m, n, lambda la, lo: (la, lo ^ 1))
 
-    pieces, plan, spots = [], [], []
-
-    def add(value, spot, rows, key, columns):
+    pieces, plan = [], []
+
+    def add(value, by_lat, rows, key, columns):
         for twin in range(2):
             for c, count, which in columns:
-                plan.append((len(pieces), 0, rows, c, count, (twin, key), which))
-                spots.append((twin, spot, key))
+                spot = (by_lat, tuple(origin(lo ^ twin, -key) for lo in range(n)))
+                plan.append((len(pieces), 0, rows, c, count, (twin, key), which, spot))
             pieces.append(swap(value) if twin else value)
 
-    add(qkv_shard, lambda la, lo, key: (0, lo), deep, 0, [(0, a, 0)])
-    add(proj_shard, lambda la, lo, key: (0, lo), deep, 0, [(0, b, 1)])
+    add(qkv_shard, (0,) * m, deep, 0, [(0, a, 0)])
+    add(proj_shard, (0,) * m, deep, 0, [(0, b, 1)])
     for s in range(1, places):
         part = send(part, m, n, lambda la, lo: (la, origin(lo, 1)))
         other = send(part, m, n, lambda la, lo: (across(la, turn(lo)), lo))
         for value, flip in ((part, 0), (other, 1)):
-            spot = lambda la, lo, key, flip=flip: ((half_of(ring, la) ^ flip) * half, origin(lo, -key))
-            add(value, spot, half, s, [(0, a, 0), (a, b, 1)])
-    tables = np.zeros((m, n, len(spots), 2), np.int32)
-    for la in range(m):
-        for lo in range(n):
-            tables[la, lo] = [spot(la, lo ^ twin, key) for twin, spot, key in spots]
-    table = jnp.asarray(tables.reshape(m * n, -1))[lax.axis_index("lat") * n + lax.axis_index("lon")]
-    return pieces, tuple(plan), table
+            by_lat = tuple((half_of(ring, la) ^ flip) * half for la in range(m))
+            add(value, by_lat, half, s, [(0, a, 0), (a, b, 1)])
+    return pieces, tuple(plan)
 
 
 def shifted(value, axis, steps):
@@ -402,7 +446,7 @@
     m = lax.axis_size("lat")
     n = lax.axis_size("lon")
     wr, wc = rows // WIN, cols // WIN
-    last = (lax.axis_index("lat") == m - 1).astype(jnp.int32).reshape(1)
+    here = jnp.stack([lax.axis_index("lat"), lax.axis_index("lon")]).astype(jnp.int32)
     fine_weights = (qkv_fine, proj_fine, up_fine, down_fine, merge_weight)
 
     deep, a = qkv_coarse.shape
@@ -420,15 +464,14 @@
         parts.append((0, 3 + at, region, None))
     shapes = [tuple(size for _, size in part[2]) for part in parts]
     sources = [field]
-    lat = lax.axis_index("lat")
     ring = line_ring(m)
-    offsets = jnp.asarray(np.array([[half_of(ring, la) * (deep // 2)] for la in range(m)], np.int32))[lat]
+    starts = tuple(half_of(ring, la) * (deep // 2) for la in range(m))
     if direct:
         parts.append((1, len(shapes), ((None, deep // 2), (0, a)), 0))
         parts.append((2, len(shapes), ((None, deep // 2), (0, b)), a))
         shapes.append((deep // 2, a + b))
         sources += [qkv_coarse, proj_coarse]
-    got = cut(offsets, sources, parts, shapes)
+    got = cut(here, starts, sources, parts, shapes)
     up = lambda la: (la - 1) % m
     left = lambda lo: (lo - 1) % n
     arrays = {"shape": field.shape}
@@ -438,19 +481,23 @@
     arrays["south"] = send(got[1], m, n, lambda la, lo: (up(la), lo))
     arrays["corner"] = send(got[2], m, n, lambda la, lo: (up(la), left(lo)))
     if direct:
-        pieces, plan, table = gather_weights(qkv_coarse, proj_coarse, got[-1], m, n)
+        pieces, plan = gather_weights(qkv_coarse, proj_coarse, got[-1], m, n)
     else:
         pieces = [lax.all_gather(w, "lon", axis=1, tiled=True) for w in (qkv_coarse, proj_coarse)]
-        plan = ((0, 0, deep, 0, a * n, (0, 0), 0), (1, 0, deep, 0, b * n, (0, 0), 1))
-        table = jnp.zeros((4,), jnp.int32)
+        plan = ((0, 0, deep, 0, a * n, (0, 0), 0, ((0,), (0,))), (1, 0, deep, 0, b * n, (0, 0), 1, ((0,), (0,))))
 
     fine, merged = {}, {}
     held = fine_weights
     for i in range(wr):
         for j in range(wc):
             first = i == 0 and j == 0
-            out, mer, *kept = fine_window(i, j, arrays, last, held, i == wr - 1, first)
-            held = kept if first else held
+            edges = None
+            if wr * wc > 1 and (i, j) == (wr - 1, wc - 1):
+                edges = [fine[p, wc - 1] for p in range(wr - 1)] + [fine[wr - 1, q] for q in range(wc - 1)]
+            out, mer, *more = fine_window(
+                i, j, arrays, here, held, m - 1 if i == wr - 1 else None, first, edges)
+            held = more[:5] if first else held
+            sends = more if edges else None
             fine[i, j] = out.reshape(WIN, WIN, width)
             merged[i, j] = mer.reshape(HALF, HALF, wide)
 
@@ -464,26 +511,26 @@
     side = jnp.concatenate([merged[i, 0][:, :QUART] for i in range(wr)], axis=0)
     side = jnp.concatenate([side[QUART:], below[:, :QUART]], axis=0)
     beside = shifted(side, "lon", -1)
-    tall = jnp.concatenate([lay(merged)[QUART:], below], axis=0)
-    coarse = jnp.concatenate([tall[:, QUART:], beside], axis=1)
-
-    def back(values):
+
+    def back(values, sends=None):
         down = lambda la: (la + 1) % m
         right = lambda lo: (lo + 1) % n
-        side = send(values[:-HALF, -HALF:], m, n, lambda la, lo: (la, right(lo)))
-        prev = send(values[-HALF:, :-HALF], m, n, lambda la, lo: (down(la), lo))
-        corner = send(values[-HALF:, -HALF:], m, n, lambda la, lo: (down(la), right(lo)))
+        sends = sends or (values[:-HALF, -HALF:], values[-HALF:, :-HALF], values[-HALF:, -HALF:])
+        side = send(sends[0], m, n, lambda la, lo: (la, right(lo)))
+        prev = send(sends[1], m, n, lambda la, lo: (down(la), lo))
+        corner = send(sends[2], m, n, lambda la, lo: (down(la), right(lo)))
         top = jnp.concatenate([corner, prev], axis=1)
         return jnp.concatenate([top, jnp.concatenate([side, values[:-HALF, :-HALF]], axis=1)], axis=0)
 
-    fine_out = back(lay(fine))
+    fine_out = back(lay(fine), sends)
     cr, cc = rows // 2 // WIN, cols // 2 // WIN
     outs = {}
     for i in range(cr):
         for j in range(cc):
-            block = coarse[i * WIN:(i + 1) * WIN, j * WIN:(j + 1) * WIN].reshape(TOK, wide)
-            seam = last if i == cr - 1 else jnp.zeros_like(last)
-            out = coarse_window(block, seam, table, pieces, plan, (n // 2 - 1,) if direct else ())
+            tiles = [merged[p, q] for p in range(wr) for q in range(wc)] + [below, beside]
+            out = coarse_window(
+                tiles, coarse_blocks(i, j, wr, wc), m - 1 if i == cr - 1 else None, here, pieces, plan,
+                (n // 2 - 1,) if direct else ())
             outs[i, j] = out.reshape(WIN, WIN, wide)
     coarse_out = jnp.concatenate(
         [jnp.concatenate([outs[i, j] for j in range(cc)], axis=1) for i in range(cr)], axis=0

time: 119 us -> 93.3 us (0.78)
  local copies, waits for them, and re-layouts: 16.1 us -> 0.12 us
  waiting for transfers between devices: 33.8 us -> 21.9 us
  starting transfers between devices: 26.7 us -> 34.3 us
  Pallas kernels: 38 us -> 33.9 us
    unnamed x62 -> x4, local copies, waits for them, and re-layouts: 14 us -> 0.01 us
    ppermute x23, waiting for transfers between devices: 33.8 us -> 19.8 us  [send(): return lax.ppermute(value, ('lat', 'lon'), pairs)]
    ppermute x23, starting transfers between devices: 24 us -> 30.5 us  [send(): return lax.ppermute(value, ('lat', 'lon'), pairs)]
    ppermute x2, waiting for transfers between devices: 0.01 us -> 2.11 us  [shifted(): lax.ppermute(value, axis, [(s, (s + steps) % count) for s in range(count)])]
    pallas_call x1, Pallas kernels: 4.86 us -> 3.4 us  [coarse_window(): pl.pallas_call(functools.partial(coarse_early_kernel, early_plan, len(sen...]
    dynamic_slice x1 -> x0, local copies, waits for them, and re-layouts: 1.27 us -> none  [whole_body(): jnp.asarray(np.array([[half_of(ring, la) * (deep // 2)] for la in range(m...]
  transfers between devices with their start and end apart: 25 -> 25, of which waited for: 8 -> 9; matrix products, arithmetic and copies ran while one was open for 3% -> 1% of each run, Pallas kernels for 30% -> 34%
where the time goes in v4:
time: 93.3 us; the launch traced here: 93.1 us
  starting transfers between devices  34.3 us (37%)
  Pallas kernels  33.9 us (36%)
  waiting for transfers between devices  21.9 us (23%)
  other arithmetic  2.08 us (2%)
    ppermute x23, starting transfers between devices, send(): return lax.ppermute(value, ('lat', 'lon'), pairs)  30.5 us
    pallas_call x4, Pallas kernels, fine_window(): pl.pallas_call(functools.partial(fine_kernel, masked, first, names, block...  23.5 us
    ppermute x23, waiting for transfers between devices, send(): return lax.ppermute(value, ('lat', 'lon'), pairs)  19.8 us
    pallas_call x1, Pallas kernels, coarse_window(): pl.pallas_call(functools.partial(coarse_late_kernel, late_plan, len(sent)...  4.92 us
    ppermute x2, starting transfers between devices, shifted(): lax.ppermute(value, axis, [(s, (s + steps) % count) for s in range(count)])  3.72 us
    pallas_call x1, Pallas kernels, coarse_window(): pl.pallas_call(functools.partial(coarse_early_kernel, early_plan, len(sen...  3.4 us
    ppermute x2, waiting for transfers between devices, shifted(): lax.ppermute(value, axis, [(s, (s + steps) % count) for s in range(count)])  2.11 us
    pallas_call x1, Pallas kernels, cut(): pl.pallas_call(functools.partial(cut_kernel, tuple(parts), starts), out_s...  2.03 us
  transfers between devices with their start and end apart: 25, of which 9 were waited for; matrix products, arithmetic and copies ran while one was open for 1% of the time, Pallas kernels for 34%

profile of v4, /device:TPU:0, one launch (start us, length us, event | category | flops | bytes accessed | tf_op | source)
XLA Modules:
  0.0 93.1 jit_solution(16835875610073492826)
XLA Ops:
  0.6 0.0 copy-start
  0.6 0.0 copy-start.1
  0.7 0.1 pad_add_fusion.here.last
  0.7 2.0 %cut.1 = (bf16[32,8,512]{2,1,0:T(8,128)(2,1)S(1)}, bf16[8,24,512]{2,1,0:T(8,128)(2,1)S(1)}, bf16[8,8,512]{2,1,0:T(8,128)(2,1)S(1)}, bf16[16,16,512]{2,1,0:T(8,12...) custom-call(s32[2]{0:T(128)S(1)} %pad_add_fusion.here.last, ...), custom_call_target="tpu_custom_call" | custom-call | bytes 1638400 | tf_op jit(solution)/shard_map/cut/pallas_call | solution.py:222
  2.8 3.1 %collective-permute-start.8 = (bf16[512,512]{1,0:T(8,128)(2,1)S(1)}, bf16[512,512]{1,0:T(8,128)(2,1)S(1)}, u32[]{:S(2)}, u32[]{:S(2)}) collective-permute-start(bf16[512,512]{1,0:T(8,128)(2,1)S(1)} %get-tuple-element.49), channel_id=1, source_target_pairs={{0,2},{1,3},{2,6},{3,7},{4,0},{5,1},{6,4},{7,5},{8,10},{9,11},{10,... | collective-permute-start | bytes 1572872 | tf_op jit(solution)/shard_map/ppermute | solution.py:397
  5.9 0.0 collective-permute-start.6
  5.9 0.5 collective-permute-start.7
  6.4 2.1 %collective-permute-start = (bf16[32,8,512]{2,1,0:T(8,128)(2,1)S(1)}, bf16[32,8,512]{2,1,0:T(8,128)(2,1)S(1)}, u32[]{:S(2)}, u32[]{:S(2)}) collective-permute-start(bf16[32,8,512]{2,1,0:T(8,128)(2,1)S(1)} %get-tuple-element.31), channel_id=1, source_target_pairs={{0,7},{1,0},{2,1},{3,2},{4,3},{5,4},{6,5},{7,6},{8,15},{9,8},{10,9... | collective-permute-start | bytes 786440 | tf_op jit(solution)/shard_map/ppermute | solution.py:397
  8.5 2.4 %collective-permute-start.1 = (bf16[8,24,512]{2,1,0:T(8,128)(2,1)S(1)}, bf16[8,24,512]{2,1,0:T(8,128)(2,1)S(1)}, u32[]{:S(2)}, u32[]{:S(2)}) collective-permute-start(bf16[8,24,512]{2,1,0:T(8,128)(2,1)S(1)} %get-tuple-element.32), channel_id=1, source_target_pairs={{0,24},{1,25},{2,26},{3,27},{4,28},{5,29},{6,30},{7,31},{8,0},{9,1... | collective-permute-start | bytes 589832 | tf_op jit(solution)/shard_map/ppermute | solution.py:397
  11.0 7.0 %fine_first.1 = (bf16[256,512]{1,0:T(8,128)(2,1)S(1)}, bf16[64,1024]{1,0:T(8,128)(2,1)S(1)}, bf16[512,1536]{1,0:T(8,128)(2,1)S(1)}, bf16[512,512]{1,0:T(8,128)(2...) custom-call(s32[2]{0:T(128)S(1)} %pad_add_fusion.here.last, ...), custom_call_target="tpu_custom_call" | custom-call | flops 1879048192 | bytes 11272192 | tf_op jit(solution)/shard_map/fine_first/pallas_call | solution.py:174
  18.0 0.9 collective-permute-done.8.rest_4_
  18.9 3.4 %collective-permute-start.12 = (bf16[512,512]{1,0:T(8,128)(2,1)S(1)}, bf16[512,512]{1,0:T(8,128)(2,1)S(1)}, u32[]{:S(2)}, u32[]{:S(2)}) collective-permute-start(bf16[512,512]{1,0:T(8,128)(2,1)S(1)} %collective-permute-done.8.rest_4_), channel_id=1, source_target_pairs={{0,2},{1,3},{2,6},{3,7},{4,0},{5,1},{6,4},{7,5},{8,10},{9,11},{10,... | collective-permute-start | bytes 1572872 | tf_op jit(solution)/shard_map/ppermute | solution.py:397
  22.3 4.4 %collective-permute-start.2 = (bf16[8,8,512]{2,1,0:T(8,128)(2,1)S(1)}, bf16[8,8,512]{2,1,0:T(8,128)(2,1)S(1)}, u32[]{:S(2)}, u32[]{:S(2)}) collective-permute-start(bf16[8,8,512]{2,1,0:T(8,128)(2,1)S(1)} %get-tuple-element.33), channel_id=1, source_target_pairs={{0,31},{1,24},{2,25},{3,26},{4,27},{5,28},{6,29},{7,30},{8,7},{9,0... | collective-permute-start | bytes 196616 | tf_op jit(solution)/shard_map/ppermute | solution.py:397
  26.7 5.5 %fine_plain.1 = (bf16[256,512]{1,0:T(8,128)(2,1)S(1)}, bf16[64,1024]{1,0:T(8,128)(2,1)S(1)}) custom-call(s32[2]{0:T(128)S(1)} %pad_add_fusion.here.last, bf16[16,8,512]{2,1,0:T(8,128)(2,1)S(1)} %get-tuple-element.40.refs_0_, bf16[32,8,512]{2,1,0:T(8,128)(2,1)S(1)} %collective-permute-done.refs_1_, bf16[512,1536]{1,0:T(8,128)(2,1)S(1)} %get-tuple-element.35.refs_2_.refs_4_, ...), custom_call_target="tpu_custom_call" | custom-call | flops 1879048192 | bytes 11272192 | tf_op jit(solution)/shard_map/fine_plain/pallas_call | solution.py:174
  32.2 0.8 collective-permute-done.12.rest_8_
  33.0 1.4 %collective-permute-start.18 = (bf16[512,512]{1,0:T(8,128)(2,1)S(1)}, bf16[512,512]{1,0:T(8,128)(2,1)S(1)}, u32[]{:S(2)}, u32[]{:S(2)}) collective-permute-start(bf16[512,512]{1,0:T(8,128)(2,1)S(1)} %collective-permute-done.12.rest_8_), channel_id=1, source_target_pairs={{0,2},{1,3},{2,6},{3,7},{4,0},{5,1},{6,4},{7,5},{8,10},{9,11},{10,... | collective-permute-start | bytes 1572872 | tf_op jit(solution)/shard_map/ppermute | solution.py:397
  34.4 0.0 collective-permute-done.1.refs_1_.refs_2_
  34.4 3.7 %collective-permute-start.16 = (bf16[4,16,1024]{2,1,0:T(8,128)(2,1)S(1)}, bf16[4,16,1024]{2,1,0:T(8,128)(2,1)S(1)}, u32[]{:S(2)}, u32[]{:S(2)}) collective-permute-start(bf16[4,16,1024]{2,1,0:T(8,128)(2,1)S(1)} %pad_maximum_fusion.3), channel_id=1, source_target_pairs={{0,24},{8,0},{16,8},{24,16},{1,25},{9,1},{17,9},{25,17},{2,26},{10... | collective-permute-start | bytes 393224 | tf_op jit(solution)/shard_map/ppermute | solution.py:440
  38.1 5.5 %fine_masked.2 = (bf16[256,512]{1,0:T(8,128)(2,1)S(1)}, bf16[64,1024]{1,0:T(8,128)(2,1)S(1)}) custom-call(s32[2]{0:T(128)S(1)} %pad_add_fusion.here.last, bf16[8,16,512]{2,1,0:T(8,128)(2,1)S(1)} %get-tuple-element.42.refs_0_, bf16[8,24,512]{2,1,0:T(8,128)(2,1)S(1)} %collective-permute-done.1.refs_1_.refs_2_, ...), custom_call_target="tpu_custom_call" | custom-call | flops 1879048192 | bytes 11272192 | tf_op jit(solution)/shard_map/fine_masked/pallas_call | solution.py:174
  43.7 0.1 fusion.3
  43.8 0.1 collective-permute-start.17
  43.8 0.0 collective-permute-done.2.refs_3_
  43.9 0.1 collective-permute-start.10
  43.9 0.0 collective-permute-done.7.rest_3_
  43.9 0.9 collective-permute-start.14
  44.8 2.1 %collective-permute-done.17.rest_17_ = bf16[16,4,1024]{2,1,0:T(4,128)(2,1)S(1)} collective-permute-done((bf16[16,4,1024]{2,1,0:T(4,128)(2,1)S(1)}, bf16[16,4,1024]{2,1,0:T(4,128)(2,1)S(1)}, u32[]{:S(2)}, u32[]{:S(2)}) %collective-permute-start.17) | collective-permute-done | bytes 131104 | tf_op jit(solution)/shard_map/ppermute | solution.py:440
  46.9 3.3 %collective-permute-start.9 = (bf16[512,512]{1,0:T(8,128)(2,1)S(1)}, bf16[512,512]{1,0:T(8,128)(2,1)S(1)}, u32[]{:S(2)}, u32[]{:S(2)}) collective-permute-start(bf16[512,512]{1,0:T(8,128)(2,1)S(1)} %collective-permute-done.8.rest_4_), channel_id=1, source_target_pairs={{0,1},{1,0},{2,3},{3,2},{4,5},{5,4},{6,7},{7,6},{8,9},{9,8},{10,11... | collective-permute-start | bytes 1572872 | tf_op jit(solution)/shard_map/ppermute | solution.py:397
  50.3 0.0 collective-permute-done.18.rest_0_
  50.3 0.0 collective-permute-start.20
  50.3 2.8 %collective-permute-done.10.rest_6_ = bf16[512,512]{1,0:T(8,128)(2,1)S(1)} collective-permute-done((bf16[512,512]{1,0:T(8,128)(2,1)S(1)}, bf16[512,512]{1,0:T(8,128)(2,1)S(1)}, u32[]{:S(2)}, u32[]{:S(2)}) %collective-permute-start.10) | collective-permute-done | bytes 524320 | tf_op jit(solution)/shard_map/ppermute | solution.py:397
  53.1 0.5 collective-permute-start.13
  53.6 5.1 %collective-permute-done.14.rest_10_ = bf16[512,512]{1,0:T(8,128)(2,1)S(1)} collective-permute-done((bf16[512,512]{1,0:T(8,128)(2,1)S(1)}, bf16[512,512]{1,0:T(8,128)(2,1)S(1)}, u32[]{:S(2)}, u32[]{:S(2)}) %collective-permute-start.14) | collective-permute-done | bytes 524320 | tf_op jit(solution)/shard_map/ppermute | solution.py:397
  58.7 0.5 collective-permute-start.19
  59.2 5.1 %collective-permute-done.20.rest_2_ = bf16[512,512]{1,0:T(8,128)(2,1)S(1)} collective-permute-done((bf16[512,512]{1,0:T(8,128)(2,1)S(1)}, bf16[512,512]{1,0:T(8,128)(2,1)S(1)}, u32[]{:S(2)}, u32[]{:S(2)}) %collective-permute-start.20) | collective-permute-done | bytes 524320 | tf_op jit(solution)/shard_map/ppermute | solution.py:397
  64.3 5.5 %fine_masked.3 = (bf16[256,512]{1,0:T(8,128)(2,1)S(1)}, bf16[64,1024]{1,0:T(8,128)(2,1)S(1)}, bf16[24,8,512]{2,1,0:T(8,128)(2,1)S(1)}, bf16[8,24,512]{2,1,0:T(8,128)(2,1)S(1)}, bf16[8,8,512]{2,1,0:T(8,128)(2,1)S(1)}) custom-call(s32[2]{0:T(128)S(1)} %pad_add_fusion.here.last, bf16[8,8,512]{2,1,0:T(8,128)(2,1)S(1)} %get-tuple-element.30.refs_0_, ...), custom_call_target="tpu_custom_call" | custom-call | flops 1879048192 | bytes 11272192 | tf_op jit(solution)/shard_map/fine_masked/pallas_call | solution.py:174
  69.9 0.6 collective-permute-start.5
  70.5 0.0 collective-permute-start.4
  70.5 4.3 %collective-permute-start.3 = (bf16[8,8,512]{2,1,0:T(8,128)(2,1)S(1)}, bf16[8,8,512]{2,1,0:T(8,128)(2,1)S(1)}, u32[]{:S(2)}, u32[]{:S(2)}) collective-permute-start(bf16[8,8,512]{2,1,0:T(8,128)(2,1)S(1)} %get-tuple-element.44), channel_id=1, source_target_pairs={{0,9},{1,10},{2,11},{3,12},{4,13},{5,14},{6,15},{7,8},{8,17},{9,18... | collective-permute-start | bytes 196616 | tf_op jit(solution)/shard_map/ppermute | solution.py:397
  74.7 3.4 %coarse_early.1 = (bf16[256,1024]{1,0:T(8,128)(2,1)S(1)}, bf16[256,1024]{1,0:T(8,128)(2,1)S(1)}, bf16[256,3072]{1,0:T(8,128)(2,1)S(1)}, bf16[1024,1024]{1,0:T(8,128)(2,1)S(1)}) custom-call(s32[2]{0:T(128)S(1)} %pad_add_fusion.here.last, bf16[1024,384]{1,0:T(8,128)(2,1)S(1)} %copy-done, bf16[1024,384]{1,0:T(8,128)(2,1)S(1)} %collective-permute-done.6.rest_1_, ...), custom_call_target="tpu_custom_call" | custom-call | flops 1207959552 | bytes 4718592 | tf_op jit(solution)/shard_map/coarse_early/pallas_call | solution.py:330
  78.2 4.9 %coarse_late.1 = bf16[256,1024]{1,0:T(8,128)(2,1)S(1)} custom-call(s32[2]{0:T(128)S(1)} %pad_add_fusion.here.last, bf16[256,1024]{1,0:T(8,128)(2,1)S(1)} %get-tuple-element.54.x_ref, bf16[256,1024]{1,0:T(8,128)(2,1)S(1)} %get-tuple-element.55.xn, bf16[256,3072]{1,0:T(8,128)(2,1)S(1)} %get-tuple-element.56.qkv_in, ...), custom_call_target="tpu_custom_call" | custom-call | flops 1207959552 | bytes 1572864 | tf_op jit(solution)/shard_map/coarse_late/pallas_call | solution.py:344
  83.1 0.7 collective-permute-start.24
  83.8 0.4 collective-permute-start.23
  84.2 1.9 %collective-permute-start.22 = (bf16[8,8,1024]{2,1,0:T(8,128)(2,1)S(1)}, bf16[8,8,1024]{2,1,0:T(8,128)(2,1)S(1)}, u32[]{:S(2)}, u32[]{:S(2)}) collective-permute-start(bf16[8,8,1024]{2,1,0:T(8,128)(2,1)S(1)} %get-tuple-element.58), channel_id=1, source_target_pairs={{0,9},{1,10},{2,11},{3,12},{4,13},{5,14},{6,15},{7,8},{8,17},{9,18... | collective-permute-start | bytes 393224 | tf_op jit(solution)/shard_map/ppermute | solution.py:397
  86.2 1.1 %fusion.2 = bf16[32,32,512]{2,1,0:T(8,128)(2,1)} fusion(bf16[16,16,512]{2,1,0:T(8,128)(2,1)S(1)} %bitcast.26, bf16[16,16,512]{2,1,0:T(8,128)(2,1)S(1)} %bitcast.19, bf16[16,16,512]{2,1,0:T(8,128)(2,1)S(1)} %bitcast.17, bf16[16,16,512]{2,1,0:T(8,128)(2,1)S(1)} %bitcast.25, bf16[24,8,512]{2,1,0:T(8,128)(2,1)S(1)} %collective-permute-done.5, ...), kind=kLoop, calls=%fused_computation.3 | loop fusion | flops 7340032 | bytes 2555904 | tf_op jit(solution)/shard_map/concatenate | solution.py:523
  87.3 2.1 %collective-permute-done.24 = bf16[8,8,1024]{2,1,0:T(8,128)(2,1)S(1)} collective-permute-done((bf16[8,8,1024]{2,1,0:T(8,128)(2,1)S(1)}, bf16[8,8,1024]{2,1,0:T(8,128)(2,1)S(1)}, u32[]{:S(2)}, u32[]{:S(2)}) %collective-permute-start.24) | collective-permute-done | bytes 131104 | tf_op jit(solution)/shard_map/ppermute | solution.py:397
  89.4 0.8 collective-permute-done.23
  90.2 2.1 %collective-permute-done.22 = bf16[8,8,1024]{2,1,0:T(8,128)(2,1)S(1)} collective-permute-done((bf16[8,8,1024]{2,1,0:T(8,128)(2,1)S(1)}, bf16[8,8,1024]{2,1,0:T(8,128)(2,1)S(1)}, u32[]{:S(2)}, u32[]{:S(2)}) %collective-permute-start.22) | collective-permute-done | bytes 131104 | tf_op jit(solution)/shard_map/ppermute | solution.py:397
  92.3 0.8 maximum_maximum_fusion
  (24 shorter events, 0.2 us)
Async XLA Ops:
  0.6 5.2 %copy-start = (bf16[1024,384]{1,0:T(8,128)(2,1)S(1)}, bf16[1024,384]{1,0:T(8,128)(2,1)}, u32[]{:S(2)}) copy-start(bf16[1024,384]{1,0:T(8,128)(2,1)} %rest_0_.1) | copy-start | bytes 2359300
  0.6 5.2 %copy-start.1 = (bf16[1024,128]{1,0:T(8,128)(2,1)S(1)}, bf16[1024,128]{1,0:T(8,128)(2,1)}, u32[]{:S(2)}) copy-start(bf16[1024,128]{1,0:T(8,128)(2,1)} %rest_2_.1) | copy-start | bytes 786436
  2.8 16.1 %collective-permute-start.8 = (bf16[512,512]{1,0:T(8,128)(2,1)S(1)}, bf16[512,512]{1,0:T(8,128)(2,1)S(1)}, u32[]{:S(2)}, u32[]{:S(2)}) collective-permute-start(bf16[512,512]{1,0:T(8,128)(2,1)S(1)} %get-tuple-element.49), channel_id=1, source_target_pairs={{0,2},{1,3},{2,6},{3,7},{4,0},{5,1},{6,4},{7,5},{8,10},{9,11},{10,... | collective-permute-start | bytes 1572872 | tf_op jit(solution)/shard_map/ppermute | solution.py:397
  5.9 47.2 %collective-permute-start.6 = (bf16[1024,384]{1,0:T(8,128)(2,1)S(1)}, bf16[1024,384]{1,0:T(8,128)(2,1)S(1)}, u32[]{:S(2)}, u32[]{:S(2)}) collective-permute-start(bf16[1024,384]{1,0:T(8,128)(2,1)S(1)} %copy-done), channel_id=1, source_target_pairs={{0,1},{1,0},{2,3},{3,2},{4,5},{5,4},{6,7},{7,6},{8,9},{9,8},{10,11... | collective-permute-start | bytes 2359304 | tf_op jit(solution)/shard_map/ppermute | solution.py:397
  5.9 38.0 %collective-permute-start.7 = (bf16[1024,128]{1,0:T(8,128)(2,1)S(1)}, bf16[1024,128]{1,0:T(8,128)(2,1)S(1)}, u32[]{:S(2)}, u32[]{:S(2)}) collective-permute-start(bf16[1024,128]{1,0:T(8,128)(2,1)S(1)} %copy-done.1), channel_id=1, source_target_pairs={{0,1},{1,0},{2,3},{3,2},{4,5},{5,4},{6,7},{7,6},{8,9},{9,8},{10,11... | collective-permute-start | bytes 786440 | tf_op jit(solution)/shard_map/ppermute | solution.py:397
  6.4 15.9 %collective-permute-start = (bf16[32,8,512]{2,1,0:T(8,128)(2,1)S(1)}, bf16[32,8,512]{2,1,0:T(8,128)(2,1)S(1)}, u32[]{:S(2)}, u32[]{:S(2)}) collective-permute-start(bf16[32,8,512]{2,1,0:T(8,128)(2,1)S(1)} %get-tuple-element.31), channel_id=1, source_target_pairs={{0,7},{1,0},{2,1},{3,2},{4,3},{5,4},{6,5},{7,6},{8,15},{9,8},{10,9... | collective-permute-start | bytes 786440 | tf_op jit(solution)/shard_map/ppermute | solution.py:397
  8.5 25.9 %collective-permute-start.1 = (bf16[8,24,512]{2,1,0:T(8,128)(2,1)S(1)}, bf16[8,24,512]{2,1,0:T(8,128)(2,1)S(1)}, u32[]{:S(2)}, u32[]{:S(2)}) collective-permute-start(bf16[8,24,512]{2,1,0:T(8,128)(2,1)S(1)} %get-tuple-element.32), channel_id=1, source_target_pairs={{0,24},{1,25},{2,26},{3,27},{4,28},{5,29},{6,30},{7,31},{8,0},{9,1... | collective-permute-start | bytes 589832 | tf_op jit(solution)/shard_map/ppermute | solution.py:397
  18.9 14.1 %collective-permute-start.12 = (bf16[512,512]{1,0:T(8,128)(2,1)S(1)}, bf16[512,512]{1,0:T(8,128)(2,1)S(1)}, u32[]{:S(2)}, u32[]{:S(2)}) collective-permute-start(bf16[512,512]{1,0:T(8,128)(2,1)S(1)} %collective-permute-done.8.rest_4_), channel_id=1, source_target_pairs={{0,2},{1,3},{2,6},{3,7},{4,0},{5,1},{6,4},{7,5},{8,10},{9,11},{10,... | collective-permute-start | bytes 1572872 | tf_op jit(solution)/shard_map/ppermute | solution.py:397
  22.3 21.5 %collective-permute-start.2 = (bf16[8,8,512]{2,1,0:T(8,128)(2,1)S(1)}, bf16[8,8,512]{2,1,0:T(8,128)(2,1)S(1)}, u32[]{:S(2)}, u32[]{:S(2)}) collective-permute-start(bf16[8,8,512]{2,1,0:T(8,128)(2,1)S(1)} %get-tuple-element.33), channel_id=1, source_target_pairs={{0,31},{1,24},{2,25},{3,26},{4,27},{5,28},{6,29},{7,30},{8,7},{9,0... | collective-permute-start | bytes 196616 | tf_op jit(solution)/shard_map/ppermute | solution.py:397
  33.0 17.3 %collective-permute-start.18 = (bf16[512,512]{1,0:T(8,128)(2,1)S(1)}, bf16[512,512]{1,0:T(8,128)(2,1)S(1)}, u32[]{:S(2)}, u32[]{:S(2)}) collective-permute-start(bf16[512,512]{1,0:T(8,128)(2,1)S(1)} %collective-permute-done.12.rest_8_), channel_id=1, source_target_pairs={{0,2},{1,3},{2,6},{3,7},{4,0},{5,1},{6,4},{7,5},{8,10},{9,11},{10,... | collective-permute-start | bytes 1572872 | tf_op jit(solution)/shard_map/ppermute | solution.py:397
  34.4 9.2 %collective-permute-start.16 = (bf16[4,16,1024]{2,1,0:T(8,128)(2,1)S(1)}, bf16[4,16,1024]{2,1,0:T(8,128)(2,1)S(1)}, u32[]{:S(2)}, u32[]{:S(2)}) collective-permute-start(bf16[4,16,1024]{2,1,0:T(8,128)(2,1)S(1)} %pad_maximum_fusion.3), channel_id=1, source_target_pairs={{0,24},{8,0},{16,8},{24,16},{1,25},{9,1},{17,9},{25,17},{2,26},{10... | collective-permute-start | bytes 393224 | tf_op jit(solution)/shard_map/ppermute | solution.py:440
  43.8 3.2 %collective-permute-start.17 = (bf16[16,4,1024]{2,1,0:T(4,128)(2,1)S(1)}, bf16[16,4,1024]{2,1,0:T(4,128)(2,1)S(1)}, u32[]{:S(2)}, u32[]{:S(2)}) collective-permute-start(bf16[16,4,1024]{2,1,0:T(4,128)(2,1)S(1)} %fusion.3), channel_id=1, source_target_pairs={{0,7},{1,0},{2,1},{3,2},{4,3},{5,4},{6,5},{7,6},{8,15},{9,8},{10,9... | collective-permute-start | bytes 393224 | tf_op jit(solution)/shard_map/ppermute | solution.py:440
  43.9 9.2 %collective-permute-start.10 = (bf16[512,512]{1,0:T(8,128)(2,1)S(1)}, bf16[512,512]{1,0:T(8,128)(2,1)S(1)}, u32[]{:S(2)}, u32[]{:S(2)}) collective-permute-start(bf16[512,512]{1,0:T(8,128)(2,1)S(1)} %collective-permute-done.8.rest_4_), channel_id=1, source_target_pairs={{0,8},{1,17},{2,10},{3,19},{4,12},{5,21},{6,14},{7,23},{8,24},{9,1... | collective-permute-start | bytes 1572872 | tf_op jit(solution)/shard_map/ppermute | solution.py:397
  43.9 14.8 %collective-permute-start.14 = (bf16[512,512]{1,0:T(8,128)(2,1)S(1)}, bf16[512,512]{1,0:T(8,128)(2,1)S(1)}, u32[]{:S(2)}, u32[]{:S(2)}) collective-permute-start(bf16[512,512]{1,0:T(8,128)(2,1)S(1)} %collective-permute-done.12.rest_8_), channel_id=1, source_target_pairs={{0,8},{1,17},{2,10},{3,19},{4,12},{5,21},{6,14},{7,23},{8,24},{9,1... | collective-permute-start | bytes 1572872 | tf_op jit(solution)/shard_map/ppermute | solution.py:397
  46.9 11.8 %collective-permute-start.9 = (bf16[512,512]{1,0:T(8,128)(2,1)S(1)}, bf16[512,512]{1,0:T(8,128)(2,1)S(1)}, u32[]{:S(2)}, u32[]{:S(2)}) collective-permute-start(bf16[512,512]{1,0:T(8,128)(2,1)S(1)} %collective-permute-done.8.rest_4_), channel_id=1, source_target_pairs={{0,1},{1,0},{2,3},{3,2},{4,5},{5,4},{6,7},{7,6},{8,9},{9,8},{10,11... | collective-permute-start | bytes 1572872 | tf_op jit(solution)/shard_map/ppermute | solution.py:397
  50.3 14.0 %collective-permute-start.20 = (bf16[512,512]{1,0:T(8,128)(2,1)S(1)}, bf16[512,512]{1,0:T(8,128)(2,1)S(1)}, u32[]{:S(2)}, u32[]{:S(2)}) collective-permute-start(bf16[512,512]{1,0:T(8,128)(2,1)S(1)} %collective-permute-done.18.rest_0_), channel_id=1, source_target_pairs={{0,8},{1,17},{2,10},{3,19},{4,12},{5,21},{6,14},{7,23},{8,24},{9,1... | collective-permute-start | bytes 1572872 | tf_op jit(solution)/shard_map/ppermute | solution.py:397
  53.1 16.8 %collective-permute-start.11 = (bf16[512,512]{1,0:T(8,128)(2,1)S(1)}, bf16[512,512]{1,0:T(8,128)(2,1)S(1)}, u32[]{:S(2)}, u32[]{:S(2)}) collective-permute-start(bf16[512,512]{1,0:T(8,128)(2,1)S(1)} %collective-permute-done.10.rest_6_), channel_id=1, source_target_pairs={{0,1},{1,0},{2,3},{3,2},{4,5},{5,4},{6,7},{7,6},{8,9},{9,8},{10,11... | collective-permute-start | bytes 1572872 | tf_op jit(solution)/shard_map/ppermute | solution.py:397
  53.1 17.4 %collective-permute-start.13 = (bf16[512,512]{1,0:T(8,128)(2,1)S(1)}, bf16[512,512]{1,0:T(8,128)(2,1)S(1)}, u32[]{:S(2)}, u32[]{:S(2)}) collective-permute-start(bf16[512,512]{1,0:T(8,128)(2,1)S(1)} %collective-permute-done.12.rest_8_), channel_id=1, source_target_pairs={{0,1},{1,0},{2,3},{3,2},{4,5},{5,4},{6,7},{7,6},{8,9},{9,8},{10,11... | collective-permute-start | bytes 1572872 | tf_op jit(solution)/shard_map/ppermute | solution.py:397
  58.7 11.8 %collective-permute-start.15 = (bf16[512,512]{1,0:T(8,128)(2,1)S(1)}, bf16[512,512]{1,0:T(8,128)(2,1)S(1)}, u32[]{:S(2)}, u32[]{:S(2)}) collective-permute-start(bf16[512,512]{1,0:T(8,128)(2,1)S(1)} %collective-permute-done.14.rest_10_), channel_id=1, source_target_pairs={{0,1},{1,0},{2,3},{3,2},{4,5},{5,4},{6,7},{7,6},{8,9},{9,8},{10,11... | collective-permute-start | bytes 1572872 | tf_op jit(solution)/shard_map/ppermute | solution.py:397
  58.7 19.4 %collective-permute-start.19 = (bf16[512,512]{1,0:T(8,128)(2,1)S(1)}, bf16[512,512]{1,0:T(8,128)(2,1)S(1)}, u32[]{:S(2)}, u32[]{:S(2)}) collective-permute-start(bf16[512,512]{1,0:T(8,128)(2,1)S(1)} %collective-permute-done.18.rest_0_), channel_id=1, source_target_pairs={{0,1},{1,0},{2,3},{3,2},{4,5},{5,4},{6,7},{7,6},{8,9},{9,8},{10,11... | collective-permute-start | bytes 1572872 | tf_op jit(solution)/shard_map/ppermute | solution.py:397
  64.3 13.8 %collective-permute-start.21 = (bf16[512,512]{1,0:T(8,128)(2,1)S(1)}, bf16[512,512]{1,0:T(8,128)(2,1)S(1)}, u32[]{:S(2)}, u32[]{:S(2)}) collective-permute-start(bf16[512,512]{1,0:T(8,128)(2,1)S(1)} %collective-permute-done.20.rest_2_), channel_id=1, source_target_pairs={{0,1},{1,0},{2,3},{3,2},{4,5},{5,4},{6,7},{7,6},{8,9},{9,8},{10,11... | collective-permute-start | bytes 1572872 | tf_op jit(solution)/shard_map/ppermute | solution.py:397
  69.9 16.3 %collective-permute-start.5 = (bf16[24,8,512]{2,1,0:T(8,128)(2,1)S(1)}, bf16[24,8,512]{2,1,0:T(8,128)(2,1)S(1)}, u32[]{:S(2)}, u32[]{:S(2)}) collective-permute-start(bf16[24,8,512]{2,1,0:T(8,128)(2,1)S(1)} %get-tuple-element.46), channel_id=1, source_target_pairs={{0,1},{1,2},{2,3},{3,4},{4,5},{5,6},{6,7},{7,0},{8,9},{9,10},{10,1... | collective-permute-start | bytes 589832 | tf_op jit(solution)/shard_map/ppermute | solution.py:397
  70.5 15.7 %collective-permute-start.4 = (bf16[8,24,512]{2,1,0:T(8,128)(2,1)S(1)}, bf16[8,24,512]{2,1,0:T(8,128)(2,1)S(1)}, u32[]{:S(2)}, u32[]{:S(2)}) collective-permute-start(bf16[8,24,512]{2,1,0:T(8,128)(2,1)S(1)} %get-tuple-element.45), channel_id=1, source_target_pairs={{0,8},{1,9},{2,10},{3,11},{4,12},{5,13},{6,14},{7,15},{8,16},{9,17... | collective-permute-start | bytes 589832 | tf_op jit(solution)/shard_map/ppermute | solution.py:397
  70.5 13.8 %collective-permute-start.3 = (bf16[8,8,512]{2,1,0:T(8,128)(2,1)S(1)}, bf16[8,8,512]{2,1,0:T(8,128)(2,1)S(1)}, u32[]{:S(2)}, u32[]{:S(2)}) collective-permute-start(bf16[8,8,512]{2,1,0:T(8,128)(2,1)S(1)} %get-tuple-element.44), channel_id=1, source_target_pairs={{0,9},{1,10},{2,11},{3,12},{4,13},{5,14},{6,15},{7,8},{8,17},{9,18... | collective-permute-start | bytes 196616 | tf_op jit(solution)/shard_map/ppermute | solution.py:397
  83.1 6.2 %collective-permute-start.24 = (bf16[8,8,1024]{2,1,0:T(8,128)(2,1)S(1)}, bf16[8,8,1024]{2,1,0:T(8,128)(2,1)S(1)}, u32[]{:S(2)}, u32[]{:S(2)}) collective-permute-start(bf16[8,8,1024]{2,1,0:T(8,128)(2,1)S(1)} %get-tuple-element.60), channel_id=1, source_target_pairs={{0,1},{1,2},{2,3},{3,4},{4,5},{5,6},{6,7},{7,0},{8,9},{9,10},{10,1... | collective-permute-start | bytes 393224 | tf_op jit(solution)/shard_map/ppermute | solution.py:397
  83.8 6.4 %collective-permute-start.23 = (bf16[8,8,1024]{2,1,0:T(8,128)(2,1)S(1)}, bf16[8,8,1024]{2,1,0:T(8,128)(2,1)S(1)}, u32[]{:S(2)}, u32[]{:S(2)}) collective-permute-start(bf16[8,8,1024]{2,1,0:T(8,128)(2,1)S(1)} %get-tuple-element.61), channel_id=1, source_target_pairs={{0,8},{1,9},{2,10},{3,11},{4,12},{5,13},{6,14},{7,15},{8,16},{9,17... | collective-permute-start | bytes 393224 | tf_op jit(solution)/shard_map/ppermute | solution.py:397
  84.2 8.1 %collective-permute-start.22 = (bf16[8,8,1024]{2,1,0:T(8,128)(2,1)S(1)}, bf16[8,8,1024]{2,1,0:T(8,128)(2,1)S(1)}, u32[]{:S(2)}, u32[]{:S(2)}) collective-permute-start(bf16[8,8,1024]{2,1,0:T(8,128)(2,1)S(1)} %get-tuple-element.58), channel_id=1, source_target_pairs={{0,9},{1,10},{2,11},{3,12},{4,13},{5,14},{6,15},{7,8},{8,17},{9,18... | collective-permute-start | bytes 393224 | tf_op jit(solution)/shard_map/ppermute | solution.py:397
